TPU v7x, 256 devices: a whole 4x4x8 slice. The times are simulated.
256 devices in a mesh: seq: 32 (over y, x, core), tp: 8 (over z).
Axes of the slice: x: 4, y: 4, z: 8, core: 2. Of those that a mesh axis runs over, the one named last changes fastest.
Arguments:
- tokens: bfloat16 [8192, 4096], P('seq', 'tp'), may hold values from -11 to 11
- grad_out: bfloat16 [8192, 4096], P('seq', 'tp'), may hold values from -1.5 to 1.5
- in_weight: bfloat16 [4096, 4096], P('seq', 'tp'), may hold values from -0.09880682 to 0.09880682
- in_scale: float32 [4096], P('tp'), may hold values from 0.0008238636 to 0.010511364
- out_weight: bfloat16 [4096, 4096], P('seq', 'tp'), may hold values from -0.053943182 to 0.053943182
- out_scale: float32 [4096], replicated, may hold values from 0.00139204545 to 0.0057386364
- state_in: bfloat16 [8192, 128], P('seq'), may hold values from -0.0625 to 0.0625
- state_out: bfloat16 [8192, 128], P('seq'), may hold values from -6 to 6
- log_decay: float32 [8192, 64], P('seq', 'tp'), may hold values from -1.6 to 0
Outputs:
- grad_tokens: bfloat16 [8192, 4096], P('seq', 'tp')
- grad_in_weight: float32 [4096, 4096], P('seq', 'tp')
- grad_in_scale: float32 [4096], P('tp')
- grad_out_weight: float32 [4096, 4096], P('seq', 'tp')
- grad_out_scale: float32 [4096], P('seq')
All inputs are finite; a program needn't handle non-finite values.
Results may differ from a plain program's by a relative error of at most 0.027.
Values may be sent and summed in bfloat16 or wider, within the bound.
No kernel may reach another device: no remote copies, remote signals or barrier semaphores. Data moves between devices by JAX's collectives and lax.ppermute only.
A program may use at most 128 MiB of HBM per device.

v0:
```python
import functools

import jax
import jax.numpy as jnp
from jax import lax
from jax.experimental import pallas as pl
from jax.experimental.pallas import tpu as pltpu
from jax.sharding import PartitionSpec as P

D = 4096
HEADS = 64
HEAD_DIM = 64
QMAX = 7

NY, NX, NC, NZ = 4, 4, 2, 8
T = 256
W = 512
R = 128
N = 128
HP = 8
PAIRS = 4

f32 = jnp.float32
bf16 = jnp.bfloat16


def seq_at(y, x, c):
    return ((y % NY) * NX + x % NX) * NC + c % NC


def hop(v, d, second=False):
    pairs = []
    for y in range(NY):
        for x in range(NX):
            for c in range(NC):
                along_x = (c == 0) != second
                to = seq_at(y, x + d, c) if along_x else seq_at(y + d, x, c)
                pairs.append((seq_at(y, x, c), to))
    return lax.ppermute(v, "seq", pairs)


def axis_hop(v, dy=0, dx=0):
    pairs = []
    for y in range(NY):
        for x in range(NX):
            for c in range(NC):
                pairs.append((seq_at(y, x, c), seq_at(y + dy, x + dx, c)))
    return lax.ppermute(v, "seq", pairs)


def seq_xor(v, bits):
    return lax.ppermute(v, "seq", [(s, s ^ bits) for s in range(NY * NX * NC)])


def swap(v):
    return seq_xor(v, 1)


def z_hop(v, d):
    return lax.ppermute(v, "tp", [(z, (z + d) % NZ) for z in range(NZ)])


def z_xor(v, b):
    return lax.ppermute(v, "tp", [(z, z ^ b) for z in range(NZ)])


def gather_z(own):
    r1 = z_hop(own, 1)
    l1 = z_hop(own, -1)
    r2 = z_hop(r1, 1)
    l2 = z_hop(l1, -1)
    r3 = z_hop(r2, 1)
    l3 = z_hop(l2, -1)
    top = z_hop(r3[:T], 1)
    bot = z_hop(l3[T:], -1)
    return [own, l1, l2, l3, r3, r2, r1, top, bot]


RELATIVE = (0, 1, 2, 3, 5, 6, 7)
smem = pl.BlockSpec(memory_space=pltpu.SMEM)
vmem = pl.BlockSpec(memory_space=pltpu.VMEM)
anyw = pl.BlockSpec(memory_space=pl.ANY)


def sds(shape, dtype):
    return jax.ShapeDtypeStruct(shape, dtype)


def call(body, name, outs, args, flops=10**6, scratch=(), away=0, out_away=()):
    nbytes = sum(a.size * a.dtype.itemsize for a in args)
    nbytes += sum(o.size * o.dtype.itemsize for o in outs)
    return pl.pallas_call(
        body,
        out_shape=outs,
        in_specs=[smem] + [anyw] * away + [vmem] * (len(args) - 1 - away),
        out_specs=[anyw if i in out_away else vmem for i in range(len(outs))],
        scratch_shapes=scratch,
        compiler_params=pltpu.CompilerParams(vmem_limit_bytes=56 * 2**20),
        cost_estimate=pl.CostEstimate(flops=flops, bytes_accessed=nbytes, transcendentals=0),
        name=name,
    )(*args)


def dot(a, b, ca=1, cb=0):
    return lax.dot_general(a, b, (((ca,), (cb,)), ((), ())), preferred_element_type=f32)


def iota(shape, dim):
    return lax.broadcasted_iota(jnp.int32, shape, dim)


def lane_pair(first, second):
    return jnp.where(iota((1, 128), 1) < HEAD_DIM, first, second)


def split3(v):
    hi = v.astype(bf16)
    rest = v - hi.astype(f32)
    mid = rest.astype(bf16)
    return hi, mid, (rest - mid.astype(f32)).astype(bf16)


def levels_of(weight, step):
    ratios = weight.astype(f32) / step
    return jnp.floor(jnp.clip(ratios, -QMAX, QMAX) + 0.5)


def prep_body(
    pos, tok, go, iw, isc, ow, os_rows, ld_t, b_ref, c_ref,
    merged, o_keep, o_give, i_levels, run, run_t, up, down, up_t, down_t, bt, ct,
):
    c, z = pos[2], pos[3]
    s = (pos[0] * NX + pos[1]) * NC + c
    for i in range(4):
        at = slice(R * i, R * i + R)
        step = os_rows[pl.ds(4 * z + i, 1), :]
        merged[:T, at] = (go[:, at].astype(f32) * step).astype(bf16)
    merged[T:, :] = tok[...]
    square = (R, R)
    eye = iota(square, 0) == iota(square, 1)
    step = jnp.sum(jnp.where(eye, os_rows[pl.ds(s, 1), :], 0.0), axis=1, keepdims=True)
    out_lv = levels_of(ow[...], step).astype(bf16)
    i_levels[...] = levels_of(iw[...], isc[...]).astype(bf16)
    for core in range(2):
        mine, other = slice(256 * core, 256 * core + 256), slice(256 - 256 * core, 512 - 256 * core)

        @pl.when(c == core)
        def _():
            o_keep[0:R, :] = out_lv[:, mine]
            o_give[0:R, :] = out_lv[:, other]

    parts = split3(ld_t[...])
    tri = (iota((T, T), 0) >= iota((T, T), 1)).astype(bf16)
    cum = sum(dot(tri, p, 1, 1) for p in parts)
    cum_t = sum(dot(p, tri, 1, 1) for p in parts)
    total = cum[T - 1 : T, :]
    run[...] = cum
    run_t[...] = cum_t
    up[...] = jnp.exp(cum)
    down[...] = jnp.exp(total - cum)
    up_t[...] = jnp.exp(cum_t)
    down_t[...] = jnp.exp(cum_t[:, T - 1 : T] - cum_t)
    lane = iota((1, 256), 1) // HEAD_DIM
    rows = []
    for half in range(2):
        spread = jnp.zeros((1, 256), f32)
        for h in range(4):
            spread = jnp.where(lane == h, total[:, 4 * half + h : 4 * half + h + 1], spread)
        rows += [p.astype(f32) for p in split3(spread)]
    tile_row = iota((16, 256), 0)
    tile = jnp.zeros((16, 256), f32)
    for i, row in enumerate(rows):
        tile = jnp.where(tile_row == i, row, tile)
    o_keep[R:, :] = tile.astype(bf16)
    o_give[R:, :] = tile.astype(bf16)
    bt[...] = b_ref[...].astype(f32).T
    ct[...] = c_ref[...].astype(f32).T


def place(c, core_of, y, x, first, second):
    ch_y = jnp.where(core_of == 0, second, first)
    ch_x = jnp.where(core_of == 0, first, second)
    return lax.rem(y + ch_y, NY) * NX + lax.rem(x + ch_x, NX)


def assemble_body(pos, *refs):
    mine, theirs = refs[:4], refs[4:8]
    w_out, coef, table = refs[8:]
    y, x, c = pos[0], pos[1], pos[2]

    def copy(side, pieces, half):
        for e in range(4):

            def step(d, _):
                core = lax.rem(c + side, 2)
                chip = place(c, core, y, x, d, e)
                for r in range(2):
                    s = chip * NC + lax.rem(core + r, 2)
                    row = pl.multiple_of(s * R, R)
                    w_out[pl.ds(row, R), 256 * half : 256 * half + 256] = pieces[e][d, r, 0:R, :]
                    if side == 0:
                        tile = pieces[e][d, r, R:, :].astype(f32)
                        low = tile[0:1] + tile[1:2] + tile[2:3]
                        high = tile[3:4] + tile[4:5] + tile[5:6]
                        table[pl.ds(s, 1), :] = jnp.where(c == 0, low, high)
                return 0

            lax.fori_loop(0, 4, step, 0)

    for side, pieces in ((0, mine), (1, theirs)):
        for half in range(2):
            pl.when(lax.rem(c + side, 2) == half)(lambda: copy(side, pieces, half))

    chip0, row0 = (y * NX + x) * NC, y * NX * NC
    number = iota((NY * NX * NC, 1), 0)
    totals = table[...]

    def between(at, first, last, ok=None):
        inside = (number >= first) & (number <= last)
        value = jnp.exp(jnp.sum(jnp.where(inside, totals, 0.0), axis=0, keepdims=True))
        if ok is not None:
            value = jnp.where(ok, value, 0.0)
        coef[at : at + 1, :] = value

    between(0, chip0, chip0)
    between(1, chip0 + 1, chip0 + 1)
    for d in range(4):
        src = lax.rem(x - d + NX, NX)
        between(5 + d, row0 + src * NC + 2, row0 + NX * NC - 1)
        between(15 + d, row0, row0 + src * NC - 1)
        if d:
            between(1 + d, row0 + src * NC + 2, chip0 - 1, src < x)
            between(11 + d, chip0 + 2, row0 + src * NC - 1, src > x)
            src = lax.rem(y - d + NY, NY)
            between(8 + d, (src + 1) * NX * NC, chip0 - 1, src < y)
            between(18 + d, chip0 + 2, src * NX * NC - 1, src > y)
    coef[22:24, :] = jnp.zeros((2, 256), f32)


def fetch(blocks, into, sems, first, rows):
    for k, ref in zip(RELATIVE, blocks[:7]):
        pltpu.make_async_copy(ref.at[first : first + rows], into.at[k], sems.at[k]).start()
    if rows == 2 * T:
        pltpu.make_async_copy(blocks[7], into.at[4, 0:T], sems.at[4]).start()
        pltpu.make_async_copy(blocks[8], into.at[4, T : 2 * T], sems.at[4]).start()
    else:
        far = blocks[7 if first == 0 else 8]
        pltpu.make_async_copy(far, into.at[4], sems.at[4]).start()

    def wait(k):
        pltpu.make_async_copy(blocks[0].at[first : first + rows], into.at[k], sems.at[k]).wait()

    return wait


def fetch_rows(z, src, into, sems):
    def copy(k):
        row = pl.multiple_of(lax.rem(z + k, NZ) * W, W)
        return pltpu.make_async_copy(src.at[pl.ds(row, W), :], into.at[k], sems.at[k])

    for k in range(NZ):
        copy(k).start()
    return lambda k: copy(k).wait()


def each_z(step):
    def two(i, _):
        step(2 * i)
        step(2 * i + 1)
        return 0

    lax.fori_loop(0, NZ // 2, two, 0)


def project_body(pos, *refs):
    blocks = refs[:9]
    w_out, w_in, isc, up_t, down_t, bt, ct = refs[9:16]
    v_ref, g_ref, mine_ref, sib_ref = refs[16:20]
    held, wo, wi, acc_g, acc_v, sems, out_sems, in_sems = refs[20:]
    c, z = pos[2], pos[3]
    waits = (
        fetch_rows(z, w_out, wo, out_sems),
        fetch(blocks, held, sems, 0, 2 * T),
        fetch_rows(z, w_in, wi, in_sems),
    )
    acc_g[...] = jnp.zeros((T, W), f32)
    acc_v[...] = jnp.zeros((T, W), f32)

    def two(i, _):
        for k in (2 * i, 2 * i + 1):
            for wait in waits:
                wait(k)
        k, l = 2 * i, 2 * i + 1
        acc_g[...] += dot(held[k, :T, :], wo[k]) + dot(held[l, :T, :], wo[l])
        acc_v[...] += dot(held[k, T:, :], wi[k]) + dot(held[l, T:, :], wi[l])
        return 0

    lax.fori_loop(0, NZ // 2, two, 0)
    g_ref[...] = acc_g[...].astype(bf16)
    v_ref[...] = (acc_v[...] * isc[...]).astype(bf16)

    for base, vals, xt, ew in ((0, v_ref, bt, down_t), (2, g_ref, ct, up_t)):
        for j in range(PAIRS):
            vj = vals[:, 128 * j : 128 * j + 128]
            first = dot((xt[...] * ew[2 * j : 2 * j + 1, :]).astype(bf16), vj)
            second = dot((xt[...] * ew[2 * j + 1 : 2 * j + 2, :]).astype(bf16), vj)
            state = lane_pair(first, second).astype(bf16)

            @pl.when(c == j // 2)
            def _():
                mine_ref[base + j % 2] = state

            @pl.when(c != j // 2)
            def _():
                sib_ref[base + j % 2] = state


def pair_coef(coef, at, i):
    j = i % 2
    return coef[at : at + 1, 128 * j : 128 * j + 128]


def join_chip_body(pos, mine, other, coef, q):
    c = pos[2]
    for i in range(4):
        own, oth = mine[i].astype(f32), other[i].astype(f32)
        s0 = jnp.where(c == 0, own, oth)
        s1 = jnp.where(c == 0, oth, own)
        if i < 2:
            q[i] = (pair_coef(coef, 1, i) * s0 + s1).astype(bf16)
        else:
            q[i] = (s0 + pair_coef(coef, 0, i) * s1).astype(bf16)


def join_row_body(pos, q, g1, g2, g3, coef, u, enter):
    for i in range(4):
        near, end = (2, 5) if i < 2 else (12, 15)
        row = pair_coef(coef, end, i) * q[i].astype(f32)
        reach = jnp.zeros((N, 128), f32)
        for d, g in ((1, g1), (2, g2), (3, g3)):
            val = g[i].astype(f32)
            row += pair_coef(coef, end + d, i) * val
            reach += pair_coef(coef, near + d - 1, i) * val
        u[i] = row.astype(bf16)
        enter[i] = reach


def join_rows_body(pos, enter, g1, g2, g3, mine, other, coef, own, give):
    c = pos[2]
    for i in range(4):
        near = 9 if i < 2 else 19
        chip = enter[i]
        for d, g in ((1, g1), (2, g2), (3, g3)):
            chip += pair_coef(coef, near + d - 1, i) * g[i].astype(f32)
        o, t = mine[i].astype(f32), other[i].astype(f32)
        if i < 2:
            e0 = chip
            e1 = pair_coef(coef, 0, i) * chip + jnp.where(c == 0, o, t)
        else:
            e0 = pair_coef(coef, 1, i) * chip + jnp.where(c == 0, t, o)
            e1 = chip
        own[i] = jnp.where(c == 0, e0, e1).astype(bf16)
        give[i] = jnp.where(c == 0, e1, e0).astype(bf16)


STATES = sds((4, N, 128), bf16)


def exchange(pos, mine, sib, coef, first, second):
    other = swap(sib)
    (q,) = call(join_chip_body, "join_chip", [STATES], (pos, mine, other, coef))
    got = [axis_hop(q, dx=d) for d in (1, 2, 3)]
    *got, one = lax.optimization_barrier((*got, first()))
    u, enter = call(
        join_row_body, "join_row", [STATES, sds((4, N, 128), f32)], (pos, q, *got, coef)
    )
    got = [axis_hop(u, dy=d) for d in (1, 2, 3)]
    *got, two = lax.optimization_barrier((*got, second()))
    own, give = call(
        join_rows_body, "join_rows", [STATES, STATES], (pos, enter, *got, mine, other, coef)
    )
    return own, swap(give), one, two


def local_body(backward, pos, vals, b_ref, c_ref, a_ref, at_ref, out):
    row, col = iota((T, T), 0), iota((T, T), 1)
    first, second = (b_ref, c_ref) if backward else (c_ref, b_ref)
    meet = dot(first[...], second[...], 1, 1)
    keep = (col >= row) if backward else (row >= col)
    for j in range(PAIRS):
        vj = vals[:, 128 * j : 128 * j + 128]
        parts = []
        for h in (2 * j, 2 * j + 1):
            spread = a_ref[:, h : h + 1] - at_ref[h : h + 1, :]
            if backward:
                spread = -spread
            mix = jnp.exp(jnp.where(keep, spread, -1e30)) * meet
            parts.append(dot(mix.astype(bf16), vj))
        out[:, 128 * j : 128 * j + 128] = lane_pair(*parts)


def finish(c, base, local_ref, x_ref, eo_ref, mine_ref, sib_ref, j):
    at = base + j % 2
    state = jnp.where(c == j // 2, mine_ref[at].astype(f32), sib_ref[at].astype(f32)).astype(bf16)
    eo = lane_pair(eo_ref[:, 2 * j : 2 * j + 1], eo_ref[:, 2 * j + 1 : 2 * j + 2])
    return local_ref[:, 128 * j : 128 * j + 128] + eo * dot(x_ref[...], state)


def tokens_body(
    pos, w_in, local_ref, x_ref, eo_ref, mine_ref, sib_ref, isc,
    out, gb_ref, gs_ref, held, buf, in_sems, out_sems,
):
    c, z = pos[2], pos[3]
    wait = fetch_rows(z, w_in, held, in_sems)
    for j in range(PAIRS):
        vals = finish(c, 2, local_ref, x_ref, eo_ref, mine_ref, sib_ref, j)
        at = slice(128 * j, 128 * j + 128)
        gb_ref[:, at] = vals.astype(bf16)
        gs_ref[:, at] = (vals * isc[:, at]).astype(bf16)

    def back(k):
        return pltpu.make_async_copy(buf.at[k], out.at[lax.rem(z + k, NZ)], out_sems.at[k])

    def step(k):
        wait(k)
        buf[k] = dot(gs_ref[...], held[k], 1, 1).astype(bf16)
        back(k).start()

    each_z(step)
    for k in range(NZ):
        back(k).wait()


def store_total(pos, wait, held, right, keep, send, buf, out_sems):
    y, x, c, z = pos[0], pos[1], pos[2], pos[3]
    kept = pl.multiple_of(256 * c, 256)
    sent = pl.multiple_of(256 - 256 * c, 256)

    def back(k):
        copies = []
        for i in range(2):
            chip = lax.rem(z + k, NZ) * 2 + i
            dy = lax.rem(chip // NX - y + NY, NY)
            dx = lax.rem(lax.rem(chip, NX) - x + NX, NX)
            rows = slice(256 * i, 256 * i + 256)
            mine = keep.at[jnp.where(c == 0, dx, dy), jnp.where(c == 0, dy, dx)]
            other = send.at[jnp.where(c == 0, dy, dx), jnp.where(c == 0, dx, dy)]
            for j, (at, to) in enumerate(((kept, mine), (sent, other))):
                copies.append(
                    pltpu.make_async_copy(
                        buf.at[k, rows, pl.ds(at, 256)], to, out_sems.at[k, 2 * i + j]
                    )
                )
        return copies

    def step(k):
        wait(k)
        buf[k] = dot(held[k], right[...], 0, 0).astype(bf16)
        for copy in back(k):
            copy.start()

    each_z(step)

    def last(k, _):
        for copy in back(k):
            copy.wait()
        return 0

    lax.fori_loop(0, NZ, last, 0)


def in_total_body(pos, *refs):
    gb, keep, send, held, buf, sems, out_sems = refs[9:]
    wait = fetch(refs[:9], held, sems, T, T)
    store_total(pos, wait, held, gb, keep, send, buf, out_sems)


def out_total_body(pos, *refs):
    local_ref, x_ref, eo_ref, mine_ref, sib_ref, keep, send, held, buf, sems, out_sems, mb = refs[9:]
    wait = fetch(refs[:9], held, sems, 0, T)
    for j in range(PAIRS):
        at = slice(128 * j, 128 * j + 128)
        vals = finish(pos[2], 0, local_ref, x_ref, eo_ref, mine_ref, sib_ref, j)
        mb[:, at] = vals.astype(bf16)
    store_total(pos, wait, held, mb, keep, send, buf, out_sems)


TOTALS = [sds((4, 4, 256, 256), bf16)] * 2
MATMUL = 2 * T * D * W


def add(*parts):
    total = parts[0].astype(f32)
    for part in parts[1:]:
        total = total + part.astype(f32)
    return total


def scatter_seq(c, first, second):
    pairs = [(keep, swap(send)) for keep, send in (first, second)]

    def own(d):
        return jnp.stack([add(keep[d], came[d]) for keep, came in pairs], axis=1).astype(bf16)

    far = own(2)
    right = hop(far[:2], 1)
    left = hop(far[2:], -1)
    none = ((0, 0),) * 3
    near = add(own(1), jnp.pad(right, ((0, 2), *none))).astype(bf16)
    back = add(own(3), jnp.pad(left, ((2, 0), *none))).astype(bf16)
    total = add(own(0), hop(near, 1), hop(back, -1))
    got = [hop(total[d].astype(bf16), d, True) for d in (1, 2, 3)]
    total = add(total[0], *got)
    upper, lower = total[:, :R], total[:, R:]
    mine = jnp.where(c == 0, upper, lower)
    theirs = swap(jnp.where(c == 0, lower, upper))
    left, right = jnp.where(c == 0, mine, theirs), jnp.where(c == 0, theirs, mine)
    whole = jnp.concatenate([left, right], axis=2)
    return whole[0], whole[1]


def slopes_of(weight, step):
    ratios = weight.astype(f32) / step
    levels = jnp.floor(jnp.clip(ratios, -QMAX, QMAX) + 0.5)
    inside = jnp.abs(ratios) <= QMAX
    return jnp.where(inside, levels - ratios, levels), inside.astype(f32)


def per_device(
    tokens, grad_out, in_weight, in_scale, out_weight, out_scale, state_in, state_out, log_decay
):
    s = lax.axis_index("seq")
    z = lax.axis_index("tp")
    y, x, c = s // (NX * NC), (s // NC) % NX, s % NC
    pos = jnp.stack([y, x, c, z]).astype(jnp.int32)
    scale = in_scale[None, :]

    outs = [sds((2 * T, W), bf16)]
    outs += [sds((R + 16, 256), bf16)] * 2 + [sds((R, W), bf16)]
    outs += [sds((T, HP), f32), sds((HP, T), f32), sds((T, HP), f32), sds((T, HP), f32)]
    outs += [sds((HP, T), f32)] * 2 + [sds((N, T), f32)] * 2
    args = (
        pos, tokens, grad_out, in_weight, scale, out_weight,
        out_scale.reshape(NY * NX * NC, R), log_decay.T, state_in, state_out,
    )
    merged, o_keep, o_give, i_levels, run, run_t, up, down, up_t, down_t, bt, ct = call(
        prep_body, "prep", outs, args
    )

    w_in = lax.all_gather(i_levels, "seq", axis=0, tiled=True)
    out_own = jnp.stack([o_keep, swap(o_give)])
    out_row = jnp.stack([out_own] + [hop(out_own, -d) for d in (1, 2, 3)])
    out_all = [out_row] + [hop(out_row, -d, True) for d in (1, 2, 3)]
    blocks = gather_z(merged)
    w_out, coef = call(
        assemble_body,
        "assemble",
        [sds((D, W), bf16), sds((24, 256), f32)],
        (pos, *out_all, *[swap(v) for v in out_all]),
        10**6,
        [pltpu.VMEM((32, 256), f32)],
    )
    v, g, mine, sib = call(
        project_body,
        "project",
        [sds((T, W), bf16)] * 2 + [STATES] * 2,
        (pos, *blocks, w_out, w_in, scale, up_t, down_t, bt, ct),
        2 * MATMUL,
        [pltpu.VMEM((NZ, 2 * T, W), bf16)]
        + [pltpu.VMEM((NZ, W, W), bf16)] * 2
        + [pltpu.VMEM((T, W), f32)] * 2
        + [pltpu.SemaphoreType.DMA((NZ,))] * 3,
        away=11,
    )
    def local(backward, vals, name):
        return call(
            functools.partial(local_body, backward),
            name,
            [sds((T, W), f32)],
            (pos, vals, state_in, state_out, run, run_t),
            10**9,
        )[0]

    own, came, grad, mixed = exchange(
        pos, mine, sib, coef,
        lambda: local(True, g, "grad_local"),
        lambda: local(False, v, "mixed_local"),
    )
    wide = [pltpu.VMEM((T, W), bf16)]
    sems = [pltpu.SemaphoreType.DMA((NZ,))] * 2
    parts, gb = call(
        tokens_body,
        "token_parts",
        [sds((NZ, T, W), bf16), sds((T, W), bf16)],
        (pos, w_in, grad, state_in, down, own, came, scale),
        MATMUL,
        wide + [pltpu.VMEM((NZ, W, W), bf16), pltpu.VMEM((NZ, T, W), bf16)] + sems,
        away=1,
        out_away=(0,),
    )
    grad_tokens = lax.psum_scatter(
        parts.reshape(NZ * T, W), "tp", scatter_dimension=0, tiled=True
    )
    held = [
        pltpu.VMEM((NZ, T, W), bf16),
        pltpu.VMEM((NZ, W, W), bf16),
        pltpu.SemaphoreType.DMA((NZ,)),
        pltpu.SemaphoreType.DMA((NZ, 4)),
    ]
    in_parts = call(
        in_total_body, "in_parts", TOTALS, (pos, *blocks, gb), MATMUL, held, 9, (0, 1)
    )
    out_parts = call(
        out_total_body,
        "out_parts",
        TOTALS,
        (pos, *blocks, mixed, state_out, up, own, came),
        MATMUL,
        held + wide,
        9,
        (0, 1),
    )
    in_total, out_total = scatter_seq(c, in_parts, out_parts)
    scale_rows = lax.dynamic_slice_in_dim(out_scale, s * R, R)[:, None]
    out_total = out_total / scale_rows

    in_slopes, in_inside = slopes_of(in_weight, scale)
    out_slopes, out_inside = slopes_of(out_weight, scale_rows)
    in_sum = jnp.sum(in_total * in_slopes, axis=0)[None]
    out_sum = jnp.sum(out_total * out_slopes, axis=1)[None]
    for seq_bits, z_bits in ((2, 1), (4, 2), (8, 4), (16, 0), (1, 0)):
        came_in = seq_xor(in_sum, seq_bits)
        if z_bits:
            came_out = z_xor(out_sum, z_bits)
            came_in, came_out = lax.optimization_barrier((came_in, came_out))
            out_sum = out_sum + came_out
        in_sum = in_sum + came_in
    return (
        grad_tokens,
        in_total * in_inside,
        in_sum[0] / jnp.sqrt(f32(D * QMAX)),
        out_total * out_inside,
        out_sum[0] / jnp.sqrt(f32(HEADS * HEAD_DIM * QMAX)),
    )


def solution(mesh):
    placed = (
        P("seq", "tp"),
        P("seq", "tp"),
        P("seq", "tp"),
        P("tp"),
        P("seq", "tp"),
        P(),
        P("seq", None),
        P("seq", None),
        P("seq", "tp"),
    )
    return jax.shard_map(
        per_device,
        mesh=mesh,
        in_specs=placed,
        out_specs=(P("seq", "tp"), P("seq", "tp"), P("tp"), P("seq", "tp"), P("seq")),
        check_vma=False,
    )
```

profile of v0, /device:TPU:1, one launch (start us, length us, event | category | flops | bytes accessed | tf_op | source)
XLA Modules:
  0.0 233.8 jit_solution(3415516958180455318)
XLA Ops:
  7.8 2.6 %prep.1 = (bf16[512,512]{1,0:T(8,128)(2,1)}, bf16[144,256]{1,0:T(8,128)(2,1)}, bf16[144,256]{1,0:T(8,128)(2,1)}, bf16[128,512]{1,0:T(8,128)(2,1)}, f32[256,8]{1,...) custom-call(s32[4]{0:T(128)} %pad_add_fusion.pos, ...), custom_call_target="tpu_custom_call" | custom-call | flops 1000000 | bytes 2058256 | tf_op jit(solution)/shard_map/prep/pallas_call | solution.py:92
  10.6 2.5 %collective-permute-start.3 = (bf16[512,512]{1,0:T(8,128)(2,1)}, bf16[512,512]{1,0:T(8,128)(2,1)S(1)}, u32[]{:S(2)}, u32[]{:S(2)}) collective-permute-start(bf16[512,512]{1,0:T(8,128)(2,1)} %get-tuple-element.48.refs_0_), channel_id=1, source_target_pairs={{0,1},{1,2},{2,3},{3,4},{4,5},{5,6},{6,7},{7,0},{8,9},{9,10},{10,1... | collective-permute-start | bytes 1572872 | tf_op jit(solution)/shard_map/ppermute | solution.py:60
  13.1 1.0 collective-permute-start.8
  14.1 3.8 %collective-permute-start = (bf16[512,512]{1,0:T(8,128)(2,1)}, bf16[512,512]{1,0:T(8,128)(2,1)S(1)}, u32[]{:S(2)}, u32[]{:S(2)}) collective-permute-start(bf16[512,512]{1,0:T(8,128)(2,1)} %get-tuple-element.48.refs_0_), channel_id=1, source_target_pairs={{0,7},{1,0},{2,1},{3,2},{4,3},{5,4},{6,5},{7,6},{8,15},{9,8},{10,9... | collective-permute-start | bytes 1572872 | tf_op jit(solution)/shard_map/ppermute | solution.py:60
  17.8 0.9 fusion.22
  18.7 2.8 %collective-permute-start.9 = (bf16[2,144,256]{2,1,0:T(8,128)(2,1)S(1)}, bf16[2,144,256]{2,1,0:T(8,128)(2,1)S(1)}, u32[]{:S(2)}, u32[]{:S(2)}) collective-permute-start(bf16[2,144,256]{2,1,0:T(8,128)(2,1)S(1)} %get-tuple-element.111), channel_id=1, source_target_pairs={{0,48},{8,200},{16,0},{24,216},{32,16},{40,232},{48,32},{56,248},{... | collective-permute-start | bytes 442376 | tf_op jit(solution)/shard_map/ppermute | solution.py:39
  22.6 6.3 %collective-permute-done.3.refs_6_ = bf16[512,512]{1,0:T(8,128)(2,1)S(1)} collective-permute-done((bf16[512,512]{1,0:T(8,128)(2,1)}, bf16[512,512]{1,0:T(8,128)(2,1)S(1)}, u32[]{:S(2)}, u32[]{:S(2)}) %collective-permute-start.3) | collective-permute-done | bytes 524320 | tf_op jit(solution)/shard_map/ppermute | solution.py:60
  29.0 2.6 %collective-permute-start.12 = (bf16[4,2,144,256]{3,2,1,0:T(8,128)(2,1)S(1)}, bf16[4,2,144,256]{3,2,1,0:T(8,128)(2,1)S(1)}, u32[]{:S(2)}, u32[]{:S(2)}) collective-permute-start(bf16[4,2,144,256]{3,2,1,0:T(8,128)(2,1)S(1)} %pad_maximum_fusion.refs_0_), channel_id=1, source_target_pairs={{0,192},{8,56},{16,208},{24,8},{32,224},{40,24},{48,240},{56,40},{... | collective-permute-start | bytes 1769480 | tf_op jit(solution)/shard_map/ppermute | solution.py:39
  31.6 2.7 %collective-permute-start.1 = (bf16[512,512]{1,0:T(8,128)(2,1)S(1)}, bf16[512,512]{1,0:T(8,128)(2,1)S(1)}, u32[]{:S(2)}, u32[]{:S(2)}) collective-permute-start(bf16[512,512]{1,0:T(8,128)(2,1)S(1)} %collective-permute-done.refs_1_), channel_id=1, source_target_pairs={{0,7},{1,0},{2,1},{3,2},{4,3},{5,4},{6,5},{7,6},{8,15},{9,8},{10,9... | collective-permute-start | bytes 1572872 | tf_op jit(solution)/shard_map/ppermute | solution.py:60
  34.2 1.2 collective-permute-start.13
  35.8 6.6 %collective-permute-done.4.refs_5_ = bf16[512,512]{1,0:T(8,128)(2,1)S(1)} collective-permute-done((bf16[512,512]{1,0:T(8,128)(2,1)S(1)}, bf16[512,512]{1,0:T(8,128)(2,1)S(1)}, u32[]{:S(2)}, u32[]{:S(2)}) %collective-permute-start.4) | collective-permute-done | bytes 524320 | tf_op jit(solution)/shard_map/ppermute | solution.py:60
  42.4 3.7 %collective-permute-done.12.refs_1_ = bf16[4,2,144,256]{3,2,1,0:T(8,128)(2,1)S(1)} collective-permute-done((bf16[4,2,144,256]{3,2,1,0:T(8,128)(2,1)S(1)}, bf16[4,2,144,256]{3,2,1,0:T(8,128)(2,1)S(1)}, u32[]{:S(2)}, u32[]{:S(2)}) %collective-permute-start.12) | collective-permute-done | bytes 589856 | tf_op jit(solution)/shard_map/ppermute | solution.py:39
  46.1 1.7 collective-permute-start.15
  47.8 3.0 %collective-permute-start.2 = (bf16[512,512]{1,0:T(8,128)(2,1)S(1)}, bf16[512,512]{1,0:T(8,128)(2,1)S(1)}, u32[]{:S(2)}, u32[]{:S(2)}) collective-permute-start(bf16[512,512]{1,0:T(8,128)(2,1)S(1)} %collective-permute-done.1.refs_2_), channel_id=1, source_target_pairs={{0,7},{1,0},{2,1},{3,2},{4,3},{5,4},{6,5},{7,6},{8,15},{9,8},{10,9... | collective-permute-start | bytes 1572872 | tf_op jit(solution)/shard_map/ppermute | solution.py:60
  51.5 2.7 %collective-permute-start.17 = (bf16[4,2,144,256]{3,2,1,0:T(8,128)(2,1)S(1)}, bf16[4,2,144,256]{3,2,1,0:T(8,128)(2,1)S(1)}, u32[]{:S(2)}, u32[]{:S(2)}) collective-permute-start(bf16[4,2,144,256]{3,2,1,0:T(8,128)(2,1)S(1)} %collective-permute-done.13.refs_2_), channel_id=1, source_target_pairs={{0,8},{8,0},{16,24},{24,16},{32,40},{40,32},{48,56},{56,48},{64,72... | collective-permute-start | bytes 1769480 | tf_op jit(solution)/shard_map/ppermute | solution.py:52
  55.0 3.2 %collective-permute-start.18 = (bf16[4,2,144,256]{3,2,1,0:T(8,128)(2,1)S(1)}, bf16[4,2,144,256]{3,2,1,0:T(8,128)(2,1)S(1)}, u32[]{:S(2)}, u32[]{:S(2)}) collective-permute-start(bf16[4,2,144,256]{3,2,1,0:T(8,128)(2,1)S(1)} %collective-permute-done.14.refs_3_), channel_id=1, source_target_pairs={{0,8},{8,0},{16,24},{24,16},{32,40},{40,32},{48,56},{56,48},{64,72... | collective-permute-start | bytes 1769480 | tf_op jit(solution)/shard_map/ppermute | solution.py:52
  58.9 3.2 %collective-permute-done.2.refs_3_ = bf16[512,512]{1,0:T(8,128)(2,1)S(1)} collective-permute-done((bf16[512,512]{1,0:T(8,128)(2,1)S(1)}, bf16[512,512]{1,0:T(8,128)(2,1)S(1)}, u32[]{:S(2)}, u32[]{:S(2)}) %collective-permute-start.2) | collective-permute-done | bytes 524320 | tf_op jit(solution)/shard_map/ppermute | solution.py:60
  63.0 3.4 %collective-permute-start.7 = (bf16[256,512]{1,0:T(8,128)(2,1)}, bf16[256,512]{1,0:T(8,128)(2,1)}, u32[]{:S(2)}, u32[]{:S(2)}) collective-permute-start(bf16[256,512]{1,0:T(8,128)(2,1)} %slice.116), channel_id=1, source_target_pairs={{0,7},{1,0},{2,1},{3,2},{4,3},{5,4},{6,5},{7,6},{8,15},{9,8},{10,9... | collective-permute-start | bytes 786440 | tf_op jit(solution)/shard_map/ppermute | solution.py:60
  67.5 0.8 copy-done.16
  68.3 5.2 %assemble.1 = (bf16[4096,512]{1,0:T(8,128)(2,1)}, f32[24,256]{1,0:T(8,128)}) custom-call(s32[4]{0:T(128)} %pad_add_fusion.pos, bf16[4,2,144,256]{3,2,1,0:T(8,128)(2,1)} %copy-done.6, bf16[4,2,144,256]{3,2,1,0:T(8,128)(2,1)} %copy-done.10, bf16[4,2,144,256]{3,2,1,0:T(8,128)(2,1)} %copy-done.11, bf16[4,2,144,256]{3,2,1,0:T(8,128)(2,1)} %copy-done.12, ...), custom_call_target="tpu_custom_call" | custom-call | flops 1000000 | bytes 8937488 | tf_op jit(solution)/shard_map/assemble/pallas_call | solution.py:92
  74.3 9.4 %project.1 = (bf16[256,512]{1,0:T(8,128)(2,1)}, bf16[256,512]{1,0:T(8,128)(2,1)}, bf16[4,128,128]{2,1,0:T(8,128)(2,1)}, bf16[4,128,128]{2,1,0:T(8,128)(2,1)}) custom-call(s32[4]{0:T(128)} %pad_add_fusion.pos, bf16[512,512]{1,0:T(8,128)(2,1)} %get-tuple-element.48.refs_0_, bf16[512,512]{1,0:T(8,128)(2,1)} %copy-done.3, bf16[512,512]{1,0:T(8,128)(2,1)} %copy-done.5, ...), custom_call_target="tpu_custom_call" | custom-call | flops 2147483648 | bytes 13649936 | tf_op jit(solution)/shard_map/project/pallas_call | solution.py:92
  83.7 1.1 collective-permute-start.19
  84.8 1.2 collective-permute-done.19.other
  86.7 1.7 join_chip.1.q
  88.4 1.0 collective-permute-start.20
  89.4 2.5 %collective-permute-start.21 = (bf16[4,128,128]{2,1,0:T(8,128)(2,1)}, bf16[4,128,128]{2,1,0:T(8,128)(2,1)S(1)}, u32[]{:S(2)}, u32[]{:S(2)}) collective-permute-start(bf16[4,128,128]{2,1,0:T(8,128)(2,1)} %join_chip.1.q), channel_id=1, source_target_pairs={{0,32},{8,40},{16,48},{24,56},{32,0},{40,8},{48,16},{56,24},{64,96... | collective-permute-start | bytes 393224 | tf_op jit(solution)/shard_map/ppermute | solution.py:48
  91.9 1.2 collective-permute-start.22
  93.1 2.6 %grad_local.1.local_ref = f32[256,512]{1,0:T(8,128)} custom-call(s32[4]{0:T(128)} %pad_add_fusion.pos, bf16[256,512]{1,0:T(8,128)(2,1)} %get-tuple-element.59.vals, bf16[256,128]{1,0:T(8,128)(2,1)} %x_ref.1, bf16[256,128]{1,0:T(8,128)(2,1)} %refs_10_.1, f32[256,8]{1,0:T(8,128)} %get-tuple-element.60.a_ref, f32[8,256]{1,0:T(8,128)} %get-tuple-element.61.at_ref), custom_call_target="tpu_custom_call" | custom-call | flops 1000000000 | bytes 933904 | tf_op jit(solution)/shard_map/grad_local/pallas_call | solution.py:92
  95.6 2.6 %collective-permute-done.21.g2 = bf16[4,128,128]{2,1,0:T(8,128)(2,1)S(1)} collective-permute-done((bf16[4,128,128]{2,1,0:T(8,128)(2,1)}, bf16[4,128,128]{2,1,0:T(8,128)(2,1)S(1)}, u32[]{:S(2)}, u32[]{:S(2)}) %collective-permute-start.21) | collective-permute-done | bytes 131104 | tf_op jit(solution)/shard_map/ppermute | solution.py:48
  99.5 2.0 join_row.1
  101.7 4.4 %collective-permute-start.24 = (bf16[4,128,128]{2,1,0:T(8,128)(2,1)}, bf16[4,128,128]{2,1,0:T(8,128)(2,1)S(1)}, u32[]{:S(2)}, u32[]{:S(2)}) collective-permute-start(bf16[4,128,128]{2,1,0:T(8,128)(2,1)} %get-tuple-element.68), channel_id=1, source_target_pairs={{0,128},{8,136},{16,144},{24,152},{32,160},{40,168},{48,176},{56,1... | collective-permute-start | bytes 393224 | tf_op jit(solution)/shard_map/ppermute | solution.py:48
  106.1 2.5 %mixed_local.1.refs_9_ = f32[256,512]{1,0:T(8,128)} custom-call(s32[4]{0:T(128)} %pad_add_fusion.pos, bf16[256,512]{1,0:T(8,128)(2,1)} %get-tuple-element.69.vals, bf16[256,128]{1,0:T(8,128)(2,1)} %x_ref.1, bf16[256,128]{1,0:T(8,128)(2,1)} %refs_10_.1, f32[256,8]{1,0:T(8,128)} %get-tuple-element.60.a_ref, f32[8,256]{1,0:T(8,128)} %get-tuple-element.61.at_ref), custom_call_target="tpu_custom_call" | custom-call | flops 1000000000 | bytes 933904 | tf_op jit(solution)/shard_map/mixed_local/pallas_call | solution.py:92
  108.6 2.5 %collective-permute-done.24.g2 = bf16[4,128,128]{2,1,0:T(8,128)(2,1)S(1)} collective-permute-done((bf16[4,128,128]{2,1,0:T(8,128)(2,1)}, bf16[4,128,128]{2,1,0:T(8,128)(2,1)S(1)}, u32[]{:S(2)}, u32[]{:S(2)}) %collective-permute-start.24) | collective-permute-done | bytes 131104 | tf_op jit(solution)/shard_map/ppermute | solution.py:48
  112.2 2.1 join_rows.1
  114.2 2.1 collective-permute-start.26
  116.4 1.2 collective-permute-done.26.sib_ref.refs_13_
  118.2 6.5 %token_parts.1 = (bf16[8,256,512]{2,1,0:T(8,128)(2,1)}, bf16[256,512]{1,0:T(8,128)(2,1)}) custom-call(s32[4]{0:T(128)} %pad_add_fusion.pos, bf16[4096,512]{1,0:T(8,128)(2,1)} %all-gather.2.cloned.1.call-done.refs_10_.w_in, f32[256,512]{1,0:T(8,128)} %grad_local.1.local_ref, bf16[256,128]{1,0:T(8,128)(2,1)} %x_ref.1, f32[256,8]{1,0:T(8,128)} %get-tuple-element.63.eo_ref, ...), custom_call_target="tpu_custom_call" | custom-call | flops 1073741824 | bytes 7415824 | tf_op jit(solution)/shard_map/token_parts/pallas_call | solution.py:92
  124.7 5.7 %in_parts.1 = (bf16[4,4,256,256]{3,2,1,0:T(8,128)(2,1)}, bf16[4,4,256,256]{3,2,1,0:T(8,128)(2,1)}) custom-call(s32[4]{0:T(128)} %pad_add_fusion.pos, bf16[512,512]{1,0:T(8,128)(2,1)} %get-tuple-element.48.refs_0_, bf16[512,512]{1,0:T(8,128)(2,1)} %copy-done.3, bf16[512,512]{1,0:T(8,128)(2,1)} %copy-done.5, bf16[512,512]{1,0:T(8,128)(2,1)} %copy-done.1, ...), custom_call_target="tpu_custom_call" | custom-call | flops 1073741824 | bytes 8650768 | tf_op jit(solution)/shard_map/in_parts/pallas_call | solution.py:92
  130.4 10.7 %collective-permute-start.27 = (bf16[4,4,256,256]{3,2,1,0:T(8,128)(2,1)}, bf16[4,4,256,256]{3,2,1,0:T(8,128)(2,1)S(1)}, u32[]{:S(2)}, u32[]{:S(2)}) collective-permute-start(bf16[4,4,256,256]{3,2,1,0:T(8,128)(2,1)} %get-tuple-element.78), channel_id=1, source_target_pairs={{0,8},{8,0},{16,24},{24,16},{32,40},{40,32},{48,56},{56,48},{64,72... | collective-permute-start | bytes 6291464 | tf_op jit(solution)/shard_map/ppermute | solution.py:52
  141.1 6.1 %out_parts.1 = (bf16[4,4,256,256]{3,2,1,0:T(8,128)(2,1)}, bf16[4,4,256,256]{3,2,1,0:T(8,128)(2,1)}) custom-call(s32[4]{0:T(128)} %pad_add_fusion.pos, bf16[512,512]{1,0:T(8,128)(2,1)} %get-tuple-element.48.refs_0_, bf16[512,512]{1,0:T(8,128)(2,1)} %copy-done.3, bf16[512,512]{1,0:T(8,128)(2,1)} %copy-done.5, bf16[512,512]{1,0:T(8,128)(2,1)} %copy-done.1, ...), custom_call_target="tpu_custom_call" | custom-call | flops 1073741824 | bytes 9248784 | tf_op jit(solution)/shard_map/out_parts/pallas_call | solution.py:92
  148.1 3.6 %collective-permute-done.28 = bf16[4,4,256,256]{3,2,1,0:T(8,128)(2,1)S(1)} collective-permute-done((bf16[4,4,256,256]{3,2,1,0:T(8,128)(2,1)}, bf16[4,4,256,256]{3,2,1,0:T(8,128)(2,1)S(1)}, u32[]{:S(2)}, u32[]{:S(2)}) %collective-permute-start.28) | collective-permute-done | bytes 2097184 | tf_op jit(solution)/shard_map/ppermute | solution.py:52
  152.3 1.1 fusion.8
  153.4 2.7 %collective-permute-start.31 = (bf16[2,2,256,256]{3,2,0,1:T(8,128)(2,1)}, bf16[2,2,256,256]{3,2,0,1:T(8,128)(2,1)}, u32[]{:S(2)}, u32[]{:S(2)}) collective-permute-start(bf16[2,2,256,256]{3,2,0,1:T(8,128)(2,1)} %get-tuple-element.105), channel_id=1, source_target_pairs={{0,48},{8,200},{16,0},{24,216},{32,16},{40,232},{48,32},{56,248},{... | collective-permute-start | bytes 1572872 | tf_op jit(solution)/shard_map/ppermute | solution.py:39
  156.1 7.2 %collective-permute-done.29 = bf16[2,2,256,256]{3,2,0,1:T(8,128)(2,1)} collective-permute-done((bf16[2,2,256,256]{3,2,0,1:T(8,128)(2,1)}, bf16[2,2,256,256]{3,2,0,1:T(8,128)(2,1)}, u32[]{:S(2)}, u32[]{:S(2)}) %collective-permute-start.29) | collective-permute-done | bytes 524320 | tf_op jit(solution)/shard_map/ppermute | solution.py:39
  163.3 1.2 add_convert_fusion.1
  164.6 1.2 add_convert_fusion
  165.7 2.7 %collective-permute-start.32 = (bf16[4,2,256,256]{3,2,0,1:T(8,128)(2,1)S(1)}, bf16[4,2,256,256]{3,2,0,1:T(8,128)(2,1)S(1)}, u32[]{:S(2)}, u32[]{:S(2)}) collective-permute-start(bf16[4,2,256,256]{3,2,0,1:T(8,128)(2,1)S(1)} %add_convert_fusion), channel_id=1, source_target_pairs={{0,48},{8,200},{16,0},{24,216},{32,16},{40,232},{48,32},{56,248},{... | collective-permute-start | bytes 3145736 | tf_op jit(solution)/shard_map/ppermute | solution.py:39
  168.5 11.3 %collective-permute-done.30 = bf16[4,2,256,256]{3,2,0,1:T(8,128)(2,1)S(1)} collective-permute-done((bf16[4,2,256,256]{3,2,0,1:T(8,128)(2,1)S(1)}, bf16[4,2,256,256]{3,2,0,1:T(8,128)(2,1)S(1)}, u32[]{:S(2)}, u32[]{:S(2)}) %collective-permute-start.30) | collective-permute-done | bytes 1048608 | tf_op jit(solution)/shard_map/ppermute | solution.py:39
  181.6 2.4 %collective-permute-start.34 = (bf16[2,256,256]{2,1,0:T(8,128)(2,1)S(1)}, bf16[2,256,256]{2,1,0:T(8,128)(2,1)S(1)}, u32[]{:S(2)}, u32[]{:S(2)}) collective-permute-start(bf16[2,256,256]{2,1,0:T(8,128)(2,1)S(1)} %get-tuple-element.103), channel_id=1, source_target_pairs={{0,128},{8,40},{16,144},{24,56},{32,160},{40,8},{48,176},{56,24},{... | collective-permute-start | bytes 786440 | tf_op jit(solution)/shard_map/ppermute | solution.py:39
  184.6 3.9 %collective-permute-done.33 = bf16[2,256,256]{2,1,0:T(8,128)(2,1)S(1)} collective-permute-done((bf16[2,256,256]{2,1,0:T(8,128)(2,1)}, bf16[2,256,256]{2,1,0:T(8,128)(2,1)S(1)}, u32[]{:S(2)}, u32[]{:S(2)}) %collective-permute-start.33) | collective-permute-done | bytes 262176 | tf_op jit(solution)/shard_map/ppermute | solution.py:39
  188.5 2.4 %collective-permute-done.34 = bf16[2,256,256]{2,1,0:T(8,128)(2,1)S(1)} collective-permute-done((bf16[2,256,256]{2,1,0:T(8,128)(2,1)S(1)}, bf16[2,256,256]{2,1,0:T(8,128)(2,1)S(1)}, u32[]{:S(2)}, u32[]{:S(2)}) %collective-permute-start.34) | collective-permute-done | bytes 262176 | tf_op jit(solution)/shard_map/ppermute | solution.py:39
  190.9 0.8 collective-permute-done.35
  191.7 1.1 fusion.11
  192.8 3.4 %collective-permute-start.36 = (f32[2,128,256]{2,1,0:T(8,128)S(1)}, f32[2,128,256]{2,1,0:T(8,128)S(1)}, u32[]{:S(2)}, u32[]{:S(2)}) collective-permute-start(f32[2,128,256]{2,1,0:T(8,128)S(1)} %slice_select_fusion), channel_id=1, source_target_pairs={{0,8},{8,0},{16,24},{24,16},{32,40},{40,32},{48,56},{56,48},{64,72... | collective-permute-start | bytes 786440 | tf_op jit(solution)/shard_map/ppermute | solution.py:52
  197.4 1.0 fusion.15
  198.8 2.0 collective-permute-done.38
  200.9 4.6 %collective-permute-start.39 = (f32[1,512]{1,0:T(1,128)S(1)}, f32[1,512]{1,0:T(1,128)S(1)}, u32[]{:S(2)}, u32[]{:S(2)}) collective-permute-start(f32[1,512]{1,0:T(1,128)S(1)} %add.201), channel_id=1, source_target_pairs={{0,32},{8,40},{16,48},{24,56},{32,0},{40,8},{48,16},{56,24},{64,96... | collective-permute-start | bytes 6152 | tf_op jit(solution)/shard_map/ppermute | solution.py:52
  205.5 1.7 collective-permute-start.40
  207.2 1.6 collective-permute-done.40
  208.9 3.8 %collective-permute-start.42 = (f32[1,128]{1,0:T(1,128)S(1)}, f32[1,128]{1,0:T(1,128)S(1)}, u32[]{:S(2)}, u32[]{:S(2)}) collective-permute-start(f32[1,128]{1,0:T(1,128)S(1)} %add.204), channel_id=1, source_target_pairs={{0,4},{1,5},{2,6},{3,7},{4,0},{5,1},{6,2},{7,3},{8,12},{9,13},{10,... | collective-permute-start | bytes 1544 | tf_op jit(solution)/shard_map/ppermute | solution.py:64
  212.7 2.6 %collective-permute-done.42 = f32[1,128]{1,0:T(1,128)S(1)} collective-permute-done((f32[1,128]{1,0:T(1,128)S(1)}, f32[1,128]{1,0:T(1,128)S(1)}, u32[]{:S(2)}, u32[]{:S(2)}) %collective-permute-start.42) | collective-permute-done | bytes 544 | tf_op jit(solution)/shard_map/ppermute | solution.py:64
  215.3 3.5 %collective-permute-start.43 = (f32[1,512]{1,0:T(1,128)S(1)}, f32[1,512]{1,0:T(1,128)S(1)}, u32[]{:S(2)}, u32[]{:S(2)}) collective-permute-start(f32[1,512]{1,0:T(1,128)S(1)} %add.205), channel_id=1, source_target_pairs={{0,128},{8,136},{16,144},{24,152},{32,160},{40,168},{48,176},{56,1... | collective-permute-start | bytes 6152 | tf_op jit(solution)/shard_map/ppermute | solution.py:52
  218.8 1.0 collective-permute-done.43
  219.8 5.5 %collective-permute-start.44 = (f32[1,512]{1,0:T(1,128)S(1)}, f32[1,512]{1,0:T(1,128)S(1)}, u32[]{:S(2)}, u32[]{:S(2)}) collective-permute-start(f32[1,512]{1,0:T(1,128)S(1)} %add.206), channel_id=1, source_target_pairs={{0,8},{8,0},{16,24},{24,16},{32,40},{40,32},{48,56},{56,48},{64,72... | collective-permute-start | bytes 6152 | tf_op jit(solution)/shard_map/ppermute | solution.py:52
  (124 shorter events, 18.0 us)
Async XLA Ops:
  7.2 66.8 %all-gather.2.cloned.1.call-start = ((), (), s32[]{:S(2)}) async-start(), calls=%async_computation.1 | async-start | bytes 4325376 | tf_op jit(solution)/shard_map/all_gather | solution.py:550
  10.5 216.2 %reduce-scatter.2.cloned.1.call-start = ((), (), s32[]{:S(2)}) async-start(), calls=%async_computation.2 | async-start | bytes 2359296 | tf_op jit(solution)/shard_map/reduce_scatter | solution.py:601
  10.6 18.3 %collective-permute-start.3 = (bf16[512,512]{1,0:T(8,128)(2,1)}, bf16[512,512]{1,0:T(8,128)(2,1)S(1)}, u32[]{:S(2)}, u32[]{:S(2)}) collective-permute-start(bf16[512,512]{1,0:T(8,128)(2,1)} %get-tuple-element.48.refs_0_), channel_id=1, source_target_pairs={{0,1},{1,2},{2,3},{3,4},{4,5},{5,6},{6,7},{7,0},{8,9},{9,10},{10,1... | collective-permute-start | bytes 1572872 | tf_op jit(solution)/shard_map/ppermute | solution.py:60
  13.1 4.7 %collective-permute-start.8 = (bf16[144,256]{1,0:T(8,128)(2,1)}, bf16[144,256]{1,0:T(8,128)(2,1)S(1)}, u32[]{:S(2)}, u32[]{:S(2)}) collective-permute-start(bf16[144,256]{1,0:T(8,128)(2,1)} %get-tuple-element.50), channel_id=1, source_target_pairs={{0,8},{8,0},{16,24},{24,16},{32,40},{40,32},{48,56},{56,48},{64,72... | collective-permute-start | bytes 221192 | tf_op jit(solution)/shard_map/ppermute | solution.py:52
  14.1 17.5 %collective-permute-start = (bf16[512,512]{1,0:T(8,128)(2,1)}, bf16[512,512]{1,0:T(8,128)(2,1)S(1)}, u32[]{:S(2)}, u32[]{:S(2)}) collective-permute-start(bf16[512,512]{1,0:T(8,128)(2,1)} %get-tuple-element.48.refs_0_), channel_id=1, source_target_pairs={{0,7},{1,0},{2,1},{3,2},{4,3},{5,4},{6,5},{7,6},{8,15},{9,8},{10,9... | collective-permute-start | bytes 1572872 | tf_op jit(solution)/shard_map/ppermute | solution.py:60
  18.7 10.2 %collective-permute-start.9 = (bf16[2,144,256]{2,1,0:T(8,128)(2,1)S(1)}, bf16[2,144,256]{2,1,0:T(8,128)(2,1)S(1)}, u32[]{:S(2)}, u32[]{:S(2)}) collective-permute-start(bf16[2,144,256]{2,1,0:T(8,128)(2,1)S(1)} %get-tuple-element.111), channel_id=1, source_target_pairs={{0,48},{8,200},{16,0},{24,216},{32,16},{40,232},{48,32},{56,248},{... | collective-permute-start | bytes 442376 | tf_op jit(solution)/shard_map/ppermute | solution.py:39
  21.5 7.4 %collective-permute-start.10 = (bf16[2,144,256]{2,1,0:T(8,128)(2,1)S(1)}, bf16[2,144,256]{2,1,0:T(8,128)(2,1)S(1)}, u32[]{:S(2)}, u32[]{:S(2)}) collective-permute-start(bf16[2,144,256]{2,1,0:T(8,128)(2,1)S(1)} %get-tuple-element.111), channel_id=1, source_target_pairs={{0,32},{8,136},{16,48},{24,152},{32,0},{40,168},{48,16},{56,184},{... | collective-permute-start | bytes 442376 | tf_op jit(solution)/shard_map/ppermute | solution.py:39
  21.9 7.0 %collective-permute-start.11 = (bf16[2,144,256]{2,1,0:T(8,128)(2,1)S(1)}, bf16[2,144,256]{2,1,0:T(8,128)(2,1)S(1)}, u32[]{:S(2)}, u32[]{:S(2)}) collective-permute-start(bf16[2,144,256]{2,1,0:T(8,128)(2,1)S(1)} %get-tuple-element.111), channel_id=1, source_target_pairs={{0,16},{8,72},{16,32},{24,88},{32,48},{40,104},{48,0},{56,120},{64... | collective-permute-start | bytes 442376 | tf_op jit(solution)/shard_map/ppermute | solution.py:39
  28.9 44.6 %copy-start.2 = (bf16[512,512]{1,0:T(8,128)(2,1)}, bf16[512,512]{1,0:T(8,128)(2,1)S(1)}, u32[]{:S(2)}) copy-start(bf16[512,512]{1,0:T(8,128)(2,1)S(1)} %collective-permute-done.3.refs_6_) | copy-start | bytes 1572868
  28.9 13.5 %collective-permute-start.4 = (bf16[512,512]{1,0:T(8,128)(2,1)S(1)}, bf16[512,512]{1,0:T(8,128)(2,1)S(1)}, u32[]{:S(2)}, u32[]{:S(2)}) collective-permute-start(bf16[512,512]{1,0:T(8,128)(2,1)S(1)} %collective-permute-done.3.refs_6_), channel_id=1, source_target_pairs={{0,1},{1,2},{2,3},{3,4},{4,5},{5,6},{6,7},{7,0},{8,9},{9,10},{10,1... | collective-permute-start | bytes 1572872 | tf_op jit(solution)/shard_map/ppermute | solution.py:60
  29.0 37.4 %copy-start.6 = (bf16[4,2,144,256]{3,2,1,0:T(8,128)(2,1)}, bf16[4,2,144,256]{3,2,1,0:T(8,128)(2,1)S(1)}, u32[]{:S(2)}) copy-start(bf16[4,2,144,256]{3,2,1,0:T(8,128)(2,1)S(1)} %pad_maximum_fusion.refs_0_) | copy-start | bytes 1769476
  29.0 17.1 %collective-permute-start.12 = (bf16[4,2,144,256]{3,2,1,0:T(8,128)(2,1)S(1)}, bf16[4,2,144,256]{3,2,1,0:T(8,128)(2,1)S(1)}, u32[]{:S(2)}, u32[]{:S(2)}) collective-permute-start(bf16[4,2,144,256]{3,2,1,0:T(8,128)(2,1)S(1)} %pad_maximum_fusion.refs_0_), channel_id=1, source_target_pairs={{0,192},{8,56},{16,208},{24,8},{32,224},{40,24},{48,240},{56,40},{... | collective-permute-start | bytes 1769480 | tf_op jit(solution)/shard_map/ppermute | solution.py:39
  31.6 41.9 %copy-start.3 = (bf16[512,512]{1,0:T(8,128)(2,1)}, bf16[512,512]{1,0:T(8,128)(2,1)S(1)}, u32[]{:S(2)}) copy-start(bf16[512,512]{1,0:T(8,128)(2,1)S(1)} %collective-permute-done.refs_1_) | copy-start | bytes 1572868
  31.6 16.2 %collective-permute-start.1 = (bf16[512,512]{1,0:T(8,128)(2,1)S(1)}, bf16[512,512]{1,0:T(8,128)(2,1)S(1)}, u32[]{:S(2)}, u32[]{:S(2)}) collective-permute-start(bf16[512,512]{1,0:T(8,128)(2,1)S(1)} %collective-permute-done.refs_1_), channel_id=1, source_target_pairs={{0,7},{1,0},{2,1},{3,2},{4,3},{5,4},{6,5},{7,6},{8,15},{9,8},{10,9... | collective-permute-start | bytes 1572872 | tf_op jit(solution)/shard_map/ppermute | solution.py:60
  34.2 16.6 %collective-permute-start.13 = (bf16[4,2,144,256]{3,2,1,0:T(8,128)(2,1)S(1)}, bf16[4,2,144,256]{3,2,1,0:T(8,128)(2,1)S(1)}, u32[]{:S(2)}, u32[]{:S(2)}) collective-permute-start(bf16[4,2,144,256]{3,2,1,0:T(8,128)(2,1)S(1)} %pad_maximum_fusion.refs_0_), channel_id=1, source_target_pairs={{0,128},{8,40},{16,144},{24,56},{32,160},{40,8},{48,176},{56,24},{... | collective-permute-start | bytes 1769480 | tf_op jit(solution)/shard_map/ppermute | solution.py:39
  35.5 16.1 %collective-permute-start.14 = (bf16[4,2,144,256]{3,2,1,0:T(8,128)(2,1)S(1)}, bf16[4,2,144,256]{3,2,1,0:T(8,128)(2,1)S(1)}, u32[]{:S(2)}, u32[]{:S(2)}) collective-permute-start(bf16[4,2,144,256]{3,2,1,0:T(8,128)(2,1)S(1)} %pad_maximum_fusion.refs_0_), channel_id=1, source_target_pairs={{0,64},{8,24},{16,80},{24,40},{32,96},{40,56},{48,112},{56,8},{64,... | collective-permute-start | bytes 1769480 | tf_op jit(solution)/shard_map/ppermute | solution.py:39
  42.4 31.1 %copy-start.4 = (bf16[512,512]{1,0:T(8,128)(2,1)}, bf16[512,512]{1,0:T(8,128)(2,1)S(1)}, u32[]{:S(2)}) copy-start(bf16[512,512]{1,0:T(8,128)(2,1)S(1)} %collective-permute-done.4.refs_5_) | copy-start | bytes 1572868
  42.4 12.6 %collective-permute-start.5 = (bf16[512,512]{1,0:T(8,128)(2,1)S(1)}, bf16[512,512]{1,0:T(8,128)(2,1)S(1)}, u32[]{:S(2)}, u32[]{:S(2)}) collective-permute-start(bf16[512,512]{1,0:T(8,128)(2,1)S(1)} %collective-permute-done.4.refs_5_), channel_id=1, source_target_pairs={{0,1},{1,2},{2,3},{3,4},{4,5},{5,6},{6,7},{7,0},{8,9},{9,10},{10,1... | collective-permute-start | bytes 1572872 | tf_op jit(solution)/shard_map/ppermute | solution.py:60
  46.1 20.3 %copy-start.10 = (bf16[4,2,144,256]{3,2,1,0:T(8,128)(2,1)}, bf16[4,2,144,256]{3,2,1,0:T(8,128)(2,1)S(1)}, u32[]{:S(2)}) copy-start(bf16[4,2,144,256]{3,2,1,0:T(8,128)(2,1)S(1)} %collective-permute-done.12.refs_1_) | copy-start | bytes 1769476
  46.1 16.9 %collective-permute-start.15 = (bf16[4,2,144,256]{3,2,1,0:T(8,128)(2,1)S(1)}, bf16[4,2,144,256]{3,2,1,0:T(8,128)(2,1)S(1)}, u32[]{:S(2)}, u32[]{:S(2)}) collective-permute-start(bf16[4,2,144,256]{3,2,1,0:T(8,128)(2,1)S(1)} %pad_maximum_fusion.refs_0_), channel_id=1, source_target_pairs={{0,8},{8,0},{16,24},{24,16},{32,40},{40,32},{48,56},{56,48},{64,72... | collective-permute-start | bytes 1769480 | tf_op jit(solution)/shard_map/ppermute | solution.py:52
  47.8 25.7 %copy-start.5 = (bf16[512,512]{1,0:T(8,128)(2,1)}, bf16[512,512]{1,0:T(8,128)(2,1)S(1)}, u32[]{:S(2)}) copy-start(bf16[512,512]{1,0:T(8,128)(2,1)S(1)} %collective-permute-done.1.refs_2_) | copy-start | bytes 1572868
  47.8 14.3 %collective-permute-start.2 = (bf16[512,512]{1,0:T(8,128)(2,1)S(1)}, bf16[512,512]{1,0:T(8,128)(2,1)S(1)}, u32[]{:S(2)}, u32[]{:S(2)}) collective-permute-start(bf16[512,512]{1,0:T(8,128)(2,1)S(1)} %collective-permute-done.1.refs_2_), channel_id=1, source_target_pairs={{0,7},{1,0},{2,1},{3,2},{4,3},{5,4},{6,5},{7,6},{8,15},{9,8},{10,9... | collective-permute-start | bytes 1572872 | tf_op jit(solution)/shard_map/ppermute | solution.py:60
  50.8 15.6 %copy-start.11 = (bf16[4,2,144,256]{3,2,1,0:T(8,128)(2,1)}, bf16[4,2,144,256]{3,2,1,0:T(8,128)(2,1)S(1)}, u32[]{:S(2)}) copy-start(bf16[4,2,144,256]{3,2,1,0:T(8,128)(2,1)S(1)} %collective-permute-done.13.refs_2_) | copy-start | bytes 1769476
  50.8 15.6 %collective-permute-start.16 = (bf16[4,2,144,256]{3,2,1,0:T(8,128)(2,1)S(1)}, bf16[4,2,144,256]{3,2,1,0:T(8,128)(2,1)S(1)}, u32[]{:S(2)}, u32[]{:S(2)}) collective-permute-start(bf16[4,2,144,256]{3,2,1,0:T(8,128)(2,1)S(1)} %collective-permute-done.12.refs_1_), channel_id=1, source_target_pairs={{0,8},{8,0},{16,24},{24,16},{32,40},{40,32},{48,56},{56,48},{64,72... | collective-permute-start | bytes 1769480 | tf_op jit(solution)/shard_map/ppermute | solution.py:52
  51.5 14.9 %copy-start.12 = (bf16[4,2,144,256]{3,2,1,0:T(8,128)(2,1)}, bf16[4,2,144,256]{3,2,1,0:T(8,128)(2,1)S(1)}, u32[]{:S(2)}) copy-start(bf16[4,2,144,256]{3,2,1,0:T(8,128)(2,1)S(1)} %collective-permute-done.14.refs_3_) | copy-start | bytes 1769476
  51.5 14.9 %collective-permute-start.17 = (bf16[4,2,144,256]{3,2,1,0:T(8,128)(2,1)S(1)}, bf16[4,2,144,256]{3,2,1,0:T(8,128)(2,1)S(1)}, u32[]{:S(2)}, u32[]{:S(2)}) collective-permute-start(bf16[4,2,144,256]{3,2,1,0:T(8,128)(2,1)S(1)} %collective-permute-done.13.refs_2_), channel_id=1, source_target_pairs={{0,8},{8,0},{16,24},{24,16},{32,40},{40,32},{48,56},{56,48},{64,72... | collective-permute-start | bytes 1769480 | tf_op jit(solution)/shard_map/ppermute | solution.py:52
  55.0 18.5 %copy-start = (bf16[512,512]{1,0:T(8,128)(2,1)}, bf16[512,512]{1,0:T(8,128)(2,1)S(1)}, u32[]{:S(2)}) copy-start(bf16[512,512]{1,0:T(8,128)(2,1)S(1)} %collective-permute-done.5.refs_4_) | copy-start | bytes 1572868
  55.0 11.4 %collective-permute-start.18 = (bf16[4,2,144,256]{3,2,1,0:T(8,128)(2,1)S(1)}, bf16[4,2,144,256]{3,2,1,0:T(8,128)(2,1)S(1)}, u32[]{:S(2)}, u32[]{:S(2)}) collective-permute-start(bf16[4,2,144,256]{3,2,1,0:T(8,128)(2,1)S(1)} %collective-permute-done.14.refs_3_), channel_id=1, source_target_pairs={{0,8},{8,0},{16,24},{24,16},{32,40},{40,32},{48,56},{56,48},{64,72... | collective-permute-start | bytes 1769480 | tf_op jit(solution)/shard_map/ppermute | solution.py:52
  62.1 11.5 %copy-start.1 = (bf16[512,512]{1,0:T(8,128)(2,1)}, bf16[512,512]{1,0:T(8,128)(2,1)S(1)}, u32[]{:S(2)}) copy-start(bf16[512,512]{1,0:T(8,128)(2,1)S(1)} %collective-permute-done.2.refs_3_) | copy-start | bytes 1572868
  62.1 11.5 %collective-permute-start.6 = (bf16[256,512]{1,0:T(8,128)(2,1)}, bf16[256,512]{1,0:T(8,128)(2,1)S(1)}, u32[]{:S(2)}, u32[]{:S(2)}) collective-permute-start(bf16[256,512]{1,0:T(8,128)(2,1)} %slice.115), channel_id=1, source_target_pairs={{0,1},{1,2},{2,3},{3,4},{4,5},{5,6},{6,7},{7,0},{8,9},{9,10},{10,1... | collective-permute-start | bytes 786440 | tf_op jit(solution)/shard_map/ppermute | solution.py:60
  63.0 3.4 %copy-start.13 = (bf16[4,2,144,256]{3,2,1,0:T(8,128)(2,1)}, bf16[4,2,144,256]{3,2,1,0:T(8,128)(2,1)S(1)}, u32[]{:S(2)}) copy-start(bf16[4,2,144,256]{3,2,1,0:T(8,128)(2,1)S(1)} %collective-permute-done.15.refs_4_) | copy-start | bytes 1769476
  63.0 10.5 %collective-permute-start.7 = (bf16[256,512]{1,0:T(8,128)(2,1)}, bf16[256,512]{1,0:T(8,128)(2,1)}, u32[]{:S(2)}, u32[]{:S(2)}) collective-permute-start(bf16[256,512]{1,0:T(8,128)(2,1)} %slice.116), channel_id=1, source_target_pairs={{0,7},{1,0},{2,1},{3,2},{4,3},{5,4},{6,5},{7,6},{8,15},{9,8},{10,9... | collective-permute-start | bytes 786440 | tf_op jit(solution)/shard_map/ppermute | solution.py:60
  83.7 2.3 %collective-permute-start.19 = (bf16[4,128,128]{2,1,0:T(8,128)(2,1)}, bf16[4,128,128]{2,1,0:T(8,128)(2,1)S(1)}, u32[]{:S(2)}, u32[]{:S(2)}) collective-permute-start(bf16[4,128,128]{2,1,0:T(8,128)(2,1)} %get-tuple-element.57), channel_id=1, source_target_pairs={{0,8},{8,0},{16,24},{24,16},{32,40},{40,32},{48,56},{56,48},{64,72... | collective-permute-start | bytes 393224 | tf_op jit(solution)/shard_map/ppermute | solution.py:52
  88.4 7.2 %collective-permute-start.20 = (bf16[4,128,128]{2,1,0:T(8,128)(2,1)}, bf16[4,128,128]{2,1,0:T(8,128)(2,1)S(1)}, u32[]{:S(2)}, u32[]{:S(2)}) collective-permute-start(bf16[4,128,128]{2,1,0:T(8,128)(2,1)} %join_chip.1.q), channel_id=1, source_target_pairs={{0,16},{8,24},{16,32},{24,40},{32,48},{40,56},{48,0},{56,8},{64,80... | collective-permute-start | bytes 393224 | tf_op jit(solution)/shard_map/ppermute | solution.py:48
  89.4 8.7 %collective-permute-start.21 = (bf16[4,128,128]{2,1,0:T(8,128)(2,1)}, bf16[4,128,128]{2,1,0:T(8,128)(2,1)S(1)}, u32[]{:S(2)}, u32[]{:S(2)}) collective-permute-start(bf16[4,128,128]{2,1,0:T(8,128)(2,1)} %join_chip.1.q), channel_id=1, source_target_pairs={{0,32},{8,40},{16,48},{24,56},{32,0},{40,8},{48,16},{56,24},{64,96... | collective-permute-start | bytes 393224 | tf_op jit(solution)/shard_map/ppermute | solution.py:48
  91.9 6.3 %collective-permute-start.22 = (bf16[4,128,128]{2,1,0:T(8,128)(2,1)}, bf16[4,128,128]{2,1,0:T(8,128)(2,1)S(1)}, u32[]{:S(2)}, u32[]{:S(2)}) collective-permute-start(bf16[4,128,128]{2,1,0:T(8,128)(2,1)} %join_chip.1.q), channel_id=1, source_target_pairs={{0,48},{8,56},{16,0},{24,8},{32,16},{40,24},{48,32},{56,40},{64,11... | collective-permute-start | bytes 393224 | tf_op jit(solution)/shard_map/ppermute | solution.py:48
  101.5 7.1 %collective-permute-start.23 = (bf16[4,128,128]{2,1,0:T(8,128)(2,1)}, bf16[4,128,128]{2,1,0:T(8,128)(2,1)S(1)}, u32[]{:S(2)}, u32[]{:S(2)}) collective-permute-start(bf16[4,128,128]{2,1,0:T(8,128)(2,1)} %get-tuple-element.68), channel_id=1, source_target_pairs={{0,64},{8,72},{16,80},{24,88},{32,96},{40,104},{48,112},{56,120},{... | collective-permute-start | bytes 393224 | tf_op jit(solution)/shard_map/ppermute | solution.py:48
  101.7 9.4 %collective-permute-start.24 = (bf16[4,128,128]{2,1,0:T(8,128)(2,1)}, bf16[4,128,128]{2,1,0:T(8,128)(2,1)S(1)}, u32[]{:S(2)}, u32[]{:S(2)}) collective-permute-start(bf16[4,128,128]{2,1,0:T(8,128)(2,1)} %get-tuple-element.68), channel_id=1, source_target_pairs={{0,128},{8,136},{16,144},{24,152},{32,160},{40,168},{48,176},{56,1... | collective-permute-start | bytes 393224 | tf_op jit(solution)/shard_map/ppermute | solution.py:48
  106.1 5.4 %collective-permute-start.25 = (bf16[4,128,128]{2,1,0:T(8,128)(2,1)}, bf16[4,128,128]{2,1,0:T(8,128)(2,1)S(1)}, u32[]{:S(2)}, u32[]{:S(2)}) collective-permute-start(bf16[4,128,128]{2,1,0:T(8,128)(2,1)} %get-tuple-element.68), channel_id=1, source_target_pairs={{0,192},{8,200},{16,208},{24,216},{32,224},{40,232},{48,240},{56,2... | collective-permute-start | bytes 393224 | tf_op jit(solution)/shard_map/ppermute | solution.py:48
  108.6 2.9 %copy-start.21 = (bf16[4,128,128]{2,1,0:T(8,128)(2,1)}, bf16[4,128,128]{2,1,0:T(8,128)(2,1)S(1)}, u32[]{:S(2)}) copy-start(bf16[4,128,128]{2,1,0:T(8,128)(2,1)S(1)} %collective-permute-done.23.g1) | copy-start | bytes 393220
  114.2 3.3 %collective-permute-start.26 = (bf16[4,128,128]{2,1,0:T(8,128)(2,1)}, bf16[4,128,128]{2,1,0:T(8,128)(2,1)S(1)}, u32[]{:S(2)}, u32[]{:S(2)}) collective-permute-start(bf16[4,128,128]{2,1,0:T(8,128)(2,1)} %get-tuple-element.74), channel_id=1, source_target_pairs={{0,8},{8,0},{16,24},{24,16},{32,40},{40,32},{48,56},{56,48},{64,72... | collective-permute-start | bytes 393224 | tf_op jit(solution)/shard_map/ppermute | solution.py:52
  130.4 17.0 %collective-permute-start.27 = (bf16[4,4,256,256]{3,2,1,0:T(8,128)(2,1)}, bf16[4,4,256,256]{3,2,1,0:T(8,128)(2,1)S(1)}, u32[]{:S(2)}, u32[]{:S(2)}) collective-permute-start(bf16[4,4,256,256]{3,2,1,0:T(8,128)(2,1)} %get-tuple-element.78), channel_id=1, source_target_pairs={{0,8},{8,0},{16,24},{24,16},{32,40},{40,32},{48,56},{56,48},{64,72... | collective-permute-start | bytes 6291464 | tf_op jit(solution)/shard_map/ppermute | solution.py:52
  141.1 6.3 %copy-start.9 = (bf16[4,4,256,256]{3,2,1,0:T(8,128)(2,1)S(1)}, bf16[4,4,256,256]{3,2,1,0:T(8,128)(2,1)}, u32[]{:S(2)}) copy-start(bf16[4,4,256,256]{3,2,1,0:T(8,128)(2,1)} %get-tuple-element.77) | copy-start | bytes 6291460
  147.2 4.5 %collective-permute-start.28 = (bf16[4,4,256,256]{3,2,1,0:T(8,128)(2,1)}, bf16[4,4,256,256]{3,2,1,0:T(8,128)(2,1)S(1)}, u32[]{:S(2)}, u32[]{:S(2)}) collective-permute-start(bf16[4,4,256,256]{3,2,1,0:T(8,128)(2,1)} %get-tuple-element.82), channel_id=1, source_target_pairs={{0,8},{8,0},{16,24},{24,16},{32,40},{40,32},{48,56},{56,48},{64,72... | collective-permute-start | bytes 6291464 | tf_op jit(solution)/shard_map/ppermute | solution.py:52
  147.4 4.3 %copy-start.8 = (bf16[4,4,256,256]{3,2,1,0:T(8,128)(2,1)S(1)}, bf16[4,4,256,256]{3,2,1,0:T(8,128)(2,1)}, u32[]{:S(2)}) copy-start(bf16[4,4,256,256]{3,2,1,0:T(8,128)(2,1)} %get-tuple-element.81) | copy-start | bytes 6291460
  153.4 9.9 %collective-permute-start.29 = (bf16[2,2,256,256]{3,2,0,1:T(8,128)(2,1)}, bf16[2,2,256,256]{3,2,0,1:T(8,128)(2,1)}, u32[]{:S(2)}, u32[]{:S(2)}) collective-permute-start(bf16[2,2,256,256]{3,2,0,1:T(8,128)(2,1)} %get-tuple-element.104), channel_id=1, source_target_pairs={{0,16},{8,72},{16,32},{24,88},{32,48},{40,104},{48,0},{56,120},{64... | collective-permute-start | bytes 1572872 | tf_op jit(solution)/shard_map/ppermute | solution.py:39
  153.4 11.1 %collective-permute-start.31 = (bf16[2,2,256,256]{3,2,0,1:T(8,128)(2,1)}, bf16[2,2,256,256]{3,2,0,1:T(8,128)(2,1)}, u32[]{:S(2)}, u32[]{:S(2)}) collective-permute-start(bf16[2,2,256,256]{3,2,0,1:T(8,128)(2,1)} %get-tuple-element.105), channel_id=1, source_target_pairs={{0,48},{8,200},{16,0},{24,216},{32,16},{40,232},{48,32},{56,248},{... | collective-permute-start | bytes 1572872 | tf_op jit(solution)/shard_map/ppermute | solution.py:39
  164.5 15.3 %collective-permute-start.30 = (bf16[4,2,256,256]{3,2,0,1:T(8,128)(2,1)S(1)}, bf16[4,2,256,256]{3,2,0,1:T(8,128)(2,1)S(1)}, u32[]{:S(2)}, u32[]{:S(2)}) collective-permute-start(bf16[4,2,256,256]{3,2,0,1:T(8,128)(2,1)S(1)} %add_convert_fusion.1), channel_id=1, source_target_pairs={{0,16},{8,72},{16,32},{24,88},{32,48},{40,104},{48,0},{56,120},{64... | collective-permute-start | bytes 3145736 | tf_op jit(solution)/shard_map/ppermute | solution.py:39
  165.7 14.5 %collective-permute-start.32 = (bf16[4,2,256,256]{3,2,0,1:T(8,128)(2,1)S(1)}, bf16[4,2,256,256]{3,2,0,1:T(8,128)(2,1)S(1)}, u32[]{:S(2)}, u32[]{:S(2)}) collective-permute-start(bf16[4,2,256,256]{3,2,0,1:T(8,128)(2,1)S(1)} %add_convert_fusion), channel_id=1, source_target_pairs={{0,48},{8,200},{16,0},{24,216},{32,16},{40,232},{48,32},{56,248},{... | collective-permute-start | bytes 3145736 | tf_op jit(solution)/shard_map/ppermute | solution.py:39
  181.4 16.0 %copy-start.17 = (bf16[128,512]{1,0:T(8,128)(2,1)S(1)}, bf16[128,512]{1,0:T(8,128)(2,1)}, u32[]{:S(2)}) copy-start(bf16[128,512]{1,0:T(8,128)(2,1)} %iw.1) | copy-start | bytes 393220
  181.4 16.0 %copy-start.18 = (bf16[128,512]{1,0:T(8,128)(2,1)S(1)}, bf16[128,512]{1,0:T(8,128)(2,1)}, u32[]{:S(2)}) copy-start(bf16[128,512]{1,0:T(8,128)(2,1)} %ow.1) | copy-start | bytes 393220
  181.4 16.0 %copy-start.27 = (f32[512]{0:T(512)S(1)}, f32[512]{0:T(512)}, u32[]{:S(2)}) copy-start(f32[512]{0:T(512)} %param.12) | copy-start | bytes 6148
  181.4 7.1 %collective-permute-start.33 = (bf16[2,256,256]{2,1,0:T(8,128)(2,1)}, bf16[2,256,256]{2,1,0:T(8,128)(2,1)S(1)}, u32[]{:S(2)}, u32[]{:S(2)}) collective-permute-start(bf16[2,256,256]{2,1,0:T(8,128)(2,1)} %get-tuple-element.101), channel_id=1, source_target_pairs={{0,64},{8,24},{16,80},{24,40},{32,96},{40,56},{48,112},{56,8},{64,... | collective-permute-start | bytes 786440 | tf_op jit(solution)/shard_map/ppermute | solution.py:39
  181.6 9.3 %collective-permute-start.34 = (bf16[2,256,256]{2,1,0:T(8,128)(2,1)S(1)}, bf16[2,256,256]{2,1,0:T(8,128)(2,1)S(1)}, u32[]{:S(2)}, u32[]{:S(2)}) collective-permute-start(bf16[2,256,256]{2,1,0:T(8,128)(2,1)S(1)} %get-tuple-element.103), channel_id=1, source_target_pairs={{0,128},{8,40},{16,144},{24,56},{32,160},{40,8},{48,176},{56,24},{... | collective-permute-start | bytes 786440 | tf_op jit(solution)/shard_map/ppermute | solution.py:39
  184.0 7.7 %collective-permute-start.35 = (bf16[2,256,256]{2,1,0:T(8,128)(2,1)S(1)}, bf16[2,256,256]{2,1,0:T(8,128)(2,1)}, u32[]{:S(2)}, u32[]{:S(2)}) collective-permute-start(bf16[2,256,256]{2,1,0:T(8,128)(2,1)S(1)} %get-tuple-element.102), channel_id=1, source_target_pairs={{0,192},{8,56},{16,208},{24,8},{32,224},{40,24},{48,240},{56,40},{... | collective-permute-start | bytes 786440 | tf_op jit(solution)/shard_map/ppermute | solution.py:39
  192.8 4.5 %collective-permute-start.36 = (f32[2,128,256]{2,1,0:T(8,128)S(1)}, f32[2,128,256]{2,1,0:T(8,128)S(1)}, u32[]{:S(2)}, u32[]{:S(2)}) collective-permute-start(f32[2,128,256]{2,1,0:T(8,128)S(1)} %slice_select_fusion), channel_id=1, source_target_pairs={{0,8},{8,0},{16,24},{24,16},{32,40},{40,32},{48,56},{56,48},{64,72... | collective-permute-start | bytes 786440 | tf_op jit(solution)/shard_map/ppermute | solution.py:52
  198.4 2.4 %collective-permute-start.37 = (f32[1,512]{1,0:T(1,128)S(1)}, f32[1,512]{1,0:T(1,128)S(1)}, u32[]{:S(2)}, u32[]{:S(2)}) collective-permute-start(f32[1,512]{1,0:T(1,128)S(1)} %bitcast.82), channel_id=1, source_target_pairs={{0,16},{8,24},{16,0},{24,8},{32,48},{40,56},{48,32},{56,40},{64,80... | collective-permute-start | bytes 6152 | tf_op jit(solution)/shard_map/ppermute | solution.py:52
  198.4 2.4 %collective-permute-start.38 = (f32[1,128]{1,0:T(1,128)S(1)}, f32[1,128]{1,0:T(1,128)S(1)}, u32[]{:S(2)}, u32[]{:S(2)}) collective-permute-start(f32[1,128]{1,0:T(1,128)S(1)} %bitcast.85), channel_id=1, source_target_pairs={{0,1},{1,0},{2,3},{3,2},{4,5},{5,4},{6,7},{7,6},{8,9},{9,8},{10,11... | collective-permute-start | bytes 1544 | tf_op jit(solution)/shard_map/ppermute | solution.py:64
  200.9 7.9 %collective-permute-start.39 = (f32[1,512]{1,0:T(1,128)S(1)}, f32[1,512]{1,0:T(1,128)S(1)}, u32[]{:S(2)}, u32[]{:S(2)}) collective-permute-start(f32[1,512]{1,0:T(1,128)S(1)} %add.201), channel_id=1, source_target_pairs={{0,32},{8,40},{16,48},{24,56},{32,0},{40,8},{48,16},{56,24},{64,96... | collective-permute-start | bytes 6152 | tf_op jit(solution)/shard_map/ppermute | solution.py:52
  205.5 3.3 %collective-permute-start.40 = (f32[1,128]{1,0:T(1,128)S(1)}, f32[1,128]{1,0:T(1,128)S(1)}, u32[]{:S(2)}, u32[]{:S(2)}) collective-permute-start(f32[1,128]{1,0:T(1,128)S(1)} %bitcast_add_fusion), channel_id=1, source_target_pairs={{0,2},{1,3},{2,0},{3,1},{4,6},{5,7},{6,4},{7,5},{8,10},{9,11},{10,... | collective-permute-start | bytes 1544 | tf_op jit(solution)/shard_map/ppermute | solution.py:64
  208.8 6.5 %collective-permute-start.41 = (f32[1,512]{1,0:T(1,128)S(1)}, f32[1,512]{1,0:T(1,128)S(1)}, u32[]{:S(2)}, u32[]{:S(2)}) collective-permute-start(f32[1,512]{1,0:T(1,128)S(1)} %add.203), channel_id=1, source_target_pairs={{0,64},{8,72},{16,80},{24,88},{32,96},{40,104},{48,112},{56,120},{... | collective-permute-start | bytes 6152 | tf_op jit(solution)/shard_map/ppermute | solution.py:52
  208.9 6.4 %collective-permute-start.42 = (f32[1,128]{1,0:T(1,128)S(1)}, f32[1,128]{1,0:T(1,128)S(1)}, u32[]{:S(2)}, u32[]{:S(2)}) collective-permute-start(f32[1,128]{1,0:T(1,128)S(1)} %add.204), channel_id=1, source_target_pairs={{0,4},{1,5},{2,6},{3,7},{4,0},{5,1},{6,2},{7,3},{8,12},{9,13},{10,... | collective-permute-start | bytes 1544 | tf_op jit(solution)/shard_map/ppermute | solution.py:64
  215.3 4.5 %collective-permute-start.43 = (f32[1,512]{1,0:T(1,128)S(1)}, f32[1,512]{1,0:T(1,128)S(1)}, u32[]{:S(2)}, u32[]{:S(2)}) collective-permute-start(f32[1,512]{1,0:T(1,128)S(1)} %add.205), channel_id=1, source_target_pairs={{0,128},{8,136},{16,144},{24,152},{32,160},{40,168},{48,176},{56,1... | collective-permute-start | bytes 6152 | tf_op jit(solution)/shard_map/ppermute | solution.py:52
  219.8 6.4 %collective-permute-start.44 = (f32[1,512]{1,0:T(1,128)S(1)}, f32[1,512]{1,0:T(1,128)S(1)}, u32[]{:S(2)}, u32[]{:S(2)}) collective-permute-start(f32[1,512]{1,0:T(1,128)S(1)} %add.206), channel_id=1, source_target_pairs={{0,8},{8,0},{16,24},{24,16},{32,40},{40,32},{48,56},{56,48},{64,72... | collective-permute-start | bytes 6152 | tf_op jit(solution)/shard_map/ppermute | solution.py:52
  (11 other events, 9.9 us)
Sparse Core Ops, SparseCore 0:
  11.1 62.8 all-gather.1
  156.2 34.6 reduce-scatter.1
where the time goes:
time: 238 us; the launch traced here: 234 us
  starting transfers between devices  87.5 us (37%)
  waiting for transfers between devices  66.8 us (28%)
  Pallas kernels  46.4 us (19%)
  between operations  14.6 us (6%)
  other arithmetic  9.97 us (4%)
  local copies, waits for them, and re-layouts  8.35 us (4%)
    pallas_call x11, Pallas kernels, call(): pl.pallas_call(body, out_shape=outs, in_specs=[smem] + [anyw] * away + [v...  46.4 us
    ppermute x15, starting transfers between devices, seq_xor(): return lax.ppermute(v, 'seq', [(s, s ^ bits) for s in range(NY * NX * NC)])  40.2 us
    ppermute x13, waiting for transfers between devices, hop(): return lax.ppermute(v, 'seq', pairs)  30.1 us
    ppermute x8, waiting for transfers between devices, z_hop(): return lax.ppermute(v, 'tp', [(z, (z + d) % NZ) for z in range(NZ)])  16.8 us
    ppermute x13, starting transfers between devices, hop(): return lax.ppermute(v, 'seq', pairs)  16.6 us
    ppermute x8, starting transfers between devices, z_hop(): return lax.ppermute(v, 'tp', [(z, (z + d) % NZ) for z in range(NZ)])  15.5 us
    ppermute x6, starting transfers between devices, axis_hop(): return lax.ppermute(v, 'seq', pairs)  9.28 us
    ppermute x15, waiting for transfers between devices, seq_xor(): return lax.ppermute(v, 'seq', [(s, s ^ bits) for s in range(NY * NX * NC)])  7.77 us
  transfers between devices with their start and end apart: 47, of which 25 were waited for; matrix products, arithmetic and copies ran while one was open for 5% of the time, Pallas kernels for 7%

commit v1 on v0

--- a/solution.py
+++ b/solution.py
@@ -58,10 +58,6 @@
 
 def z_hop(v, d):
     return lax.ppermute(v, "tp", [(z, (z + d) % NZ) for z in range(NZ)])
-
-
-def z_xor(v, b):
-    return lax.ppermute(v, "tp", [(z, z ^ b) for z in range(NZ)])
 
 
 def gather_z(own):
@@ -519,6 +515,11 @@
     return whole[0], whole[1]
 
 
+def everyones(part, axis, count):
+    parts = jnp.broadcast_to(part, (count, part.shape[1]))
+    return jnp.sum(lax.all_to_all(parts, axis, 0, 0, tiled=True), axis=0)
+
+
 def slopes_of(weight, step):
     ratios = weight.astype(f32) / step
     levels = jnp.floor(jnp.clip(ratios, -QMAX, QMAX) + 0.5)
@@ -628,19 +629,14 @@
     out_slopes, out_inside = slopes_of(out_weight, scale_rows)
     in_sum = jnp.sum(in_total * in_slopes, axis=0)[None]
     out_sum = jnp.sum(out_total * out_slopes, axis=1)[None]
-    for seq_bits, z_bits in ((2, 1), (4, 2), (8, 4), (16, 0), (1, 0)):
-        came_in = seq_xor(in_sum, seq_bits)
-        if z_bits:
-            came_out = z_xor(out_sum, z_bits)
-            came_in, came_out = lax.optimization_barrier((came_in, came_out))
-            out_sum = out_sum + came_out
-        in_sum = in_sum + came_in
+    in_sum = everyones(in_sum, "seq", NY * NX * NC)
+    out_sum = everyones(out_sum, "tp", NZ)
     return (
         grad_tokens,
         in_total * in_inside,
-        in_sum[0] / jnp.sqrt(f32(D * QMAX)),
+        in_sum / jnp.sqrt(f32(D * QMAX)),
         out_total * out_inside,
-        out_sum[0] / jnp.sqrt(f32(HEADS * HEAD_DIM * QMAX)),
+        out_sum / jnp.sqrt(f32(HEADS * HEAD_DIM * QMAX)),
     )
 
 

time: 238 us -> 225 us (0.945); the launches traced: 234 us -> 224 us
  starting transfers between devices: 87.5 us -> 66.8 us
  blocking collectives: 0 us -> 11.2 us
    ppermute x15 -> x10, starting transfers between devices: 40.2 us -> 16.4 us  [seq_xor(): return lax.ppermute(v, 'seq', [(s, s ^ bits) for s in range(NY * NX * NC)])]
    all_to_all x0 -> x1, blocking collectives: none -> 11.2 us  [everyones(): return jnp.sum(lax.all_to_all(parts, axis, 0, 0, tiled=True), axis=0)]
    all_to_all x0 -> x1, starting transfers between devices: none -> 8.99 us  [everyones(): return jnp.sum(lax.all_to_all(parts, axis, 0, 0, tiled=True), axis=0)]
    all_to_all x0 -> x1, waiting for transfers between devices: none -> 6.79 us  [everyones(): return jnp.sum(lax.all_to_all(parts, axis, 0, 0, tiled=True), axis=0)]
    ppermute x3 -> x0, waiting for transfers between devices: 6.2 us -> none  [z_xor(): return lax.ppermute(v, 'tp', [(z, z ^ b) for z in range(NZ)])]
    ppermute x3 -> x0, starting transfers between devices: 5.87 us -> none  [z_xor(): return lax.ppermute(v, 'tp', [(z, z ^ b) for z in range(NZ)])]
    ppermute x15 -> x10, waiting for transfers between devices: 7.77 us -> 6.4 us  [seq_xor(): return lax.ppermute(v, 'seq', [(s, s ^ bits) for s in range(NY * NX * NC)])]
  transfers between devices with their start and end apart: 47 -> 40, of which waited for: 25 -> 21; matrix products, arithmetic and copies ran while one was open for 5% -> 5% of each run, Pallas kernels for 7% -> 7%
where the time goes in v1:
time: 225 us; the launch traced here: 224 us
  starting transfers between devices  66.8 us (30%)
  waiting for transfers between devices  66 us (29%)
  Pallas kernels  46.4 us (21%)
  between operations  14.4 us (6%)
  blocking collectives  11.2 us (5%)
  other arithmetic  10.2 us (5%)
  local copies, waits for them, and re-layouts  9.2 us (4%)
    pallas_call x11, Pallas kernels, call(): pl.pallas_call(body, out_shape=outs, in_specs=[smem] + [anyw] * away + [v...  46.4 us
    ppermute x13, waiting for transfers between devices, hop(): return lax.ppermute(v, 'seq', pairs)  29.9 us
    ppermute x8, waiting for transfers between devices, z_hop(): return lax.ppermute(v, 'tp', [(z, (z + d) % NZ) for z in range(NZ)])  17 us
    ppermute x13, starting transfers between devices, hop(): return lax.ppermute(v, 'seq', pairs)  16.6 us
    ppermute x10, starting transfers between devices, seq_xor(): return lax.ppermute(v, 'seq', [(s, s ^ bits) for s in range(NY * NX * NC)])  16.4 us
    ppermute x8, starting transfers between devices, z_hop(): return lax.ppermute(v, 'tp', [(z, (z + d) % NZ) for z in range(NZ)])  15.5 us
    all_to_all x1, blocking collectives, everyones(): return jnp.sum(lax.all_to_all(parts, axis, 0, 0, tiled=True), axis=0)  11.2 us
    ppermute x6, starting transfers between devices, axis_hop(): return lax.ppermute(v, 'seq', pairs)  9.29 us
  transfers between devices with their start and end apart: 40, of which 21 were waited for; matrix products, arithmetic and copies ran while one was open for 5% of the time, Pallas kernels for 7%

profile of v1, /device:TPU:1, one launch (start us, length us, event | category | flops | bytes accessed | tf_op | source)
XLA Modules:
  0.0 224.3 jit_solution(11421501532493208169)
XLA Ops:
  7.9 2.6 %prep.1 = (bf16[512,512]{1,0:T(8,128)(2,1)}, bf16[144,256]{1,0:T(8,128)(2,1)}, bf16[144,256]{1,0:T(8,128)(2,1)}, bf16[128,512]{1,0:T(8,128)(2,1)}, f32[256,8]{1,...) custom-call(s32[4]{0:T(128)} %pad_add_fusion.pos, ...), custom_call_target="tpu_custom_call" | custom-call | flops 1000000 | bytes 2058256 | tf_op jit(solution)/shard_map/prep/pallas_call | solution.py:88
  10.6 2.5 %collective-permute-start.3 = (bf16[512,512]{1,0:T(8,128)(2,1)}, bf16[512,512]{1,0:T(8,128)(2,1)S(1)}, u32[]{:S(2)}, u32[]{:S(2)}) collective-permute-start(bf16[512,512]{1,0:T(8,128)(2,1)} %get-tuple-element.42.refs_0_), channel_id=1, source_target_pairs={{0,1},{1,2},{2,3},{3,4},{4,5},{5,6},{6,7},{7,0},{8,9},{9,10},{10,1... | collective-permute-start | bytes 1572872 | tf_op jit(solution)/shard_map/ppermute | solution.py:60
  13.2 1.0 collective-permute-start.8
  14.1 3.8 %collective-permute-start = (bf16[512,512]{1,0:T(8,128)(2,1)}, bf16[512,512]{1,0:T(8,128)(2,1)S(1)}, u32[]{:S(2)}, u32[]{:S(2)}) collective-permute-start(bf16[512,512]{1,0:T(8,128)(2,1)} %get-tuple-element.42.refs_0_), channel_id=1, source_target_pairs={{0,7},{1,0},{2,1},{3,2},{4,3},{5,4},{6,5},{7,6},{8,15},{9,8},{10,9... | collective-permute-start | bytes 1572872 | tf_op jit(solution)/shard_map/ppermute | solution.py:60
  17.9 0.9 fusion.22
  18.8 2.8 %collective-permute-start.9 = (bf16[2,144,256]{2,1,0:T(8,128)(2,1)S(1)}, bf16[2,144,256]{2,1,0:T(8,128)(2,1)S(1)}, u32[]{:S(2)}, u32[]{:S(2)}) collective-permute-start(bf16[2,144,256]{2,1,0:T(8,128)(2,1)S(1)} %get-tuple-element.99), channel_id=1, source_target_pairs={{0,48},{8,200},{16,0},{24,216},{32,16},{40,232},{48,32},{56,248},{... | collective-permute-start | bytes 442376 | tf_op jit(solution)/shard_map/ppermute | solution.py:39
  22.0 0.7 collective-permute-start.11
  22.7 6.3 %collective-permute-done.3.refs_6_ = bf16[512,512]{1,0:T(8,128)(2,1)S(1)} collective-permute-done((bf16[512,512]{1,0:T(8,128)(2,1)}, bf16[512,512]{1,0:T(8,128)(2,1)S(1)}, u32[]{:S(2)}, u32[]{:S(2)}) %collective-permute-start.3) | collective-permute-done | bytes 524320 | tf_op jit(solution)/shard_map/ppermute | solution.py:60
  29.1 2.6 %collective-permute-start.12 = (bf16[4,2,144,256]{3,2,1,0:T(8,128)(2,1)S(1)}, bf16[4,2,144,256]{3,2,1,0:T(8,128)(2,1)S(1)}, u32[]{:S(2)}, u32[]{:S(2)}) collective-permute-start(bf16[4,2,144,256]{3,2,1,0:T(8,128)(2,1)S(1)} %pad_maximum_fusion.refs_0_), channel_id=1, source_target_pairs={{0,192},{8,56},{16,208},{24,8},{32,224},{40,24},{48,240},{56,40},{... | collective-permute-start | bytes 1769480 | tf_op jit(solution)/shard_map/ppermute | solution.py:39
  31.7 2.7 %collective-permute-start.1 = (bf16[512,512]{1,0:T(8,128)(2,1)S(1)}, bf16[512,512]{1,0:T(8,128)(2,1)S(1)}, u32[]{:S(2)}, u32[]{:S(2)}) collective-permute-start(bf16[512,512]{1,0:T(8,128)(2,1)S(1)} %collective-permute-done.refs_1_), channel_id=1, source_target_pairs={{0,7},{1,0},{2,1},{3,2},{4,3},{5,4},{6,5},{7,6},{8,15},{9,8},{10,9... | collective-permute-start | bytes 1572872 | tf_op jit(solution)/shard_map/ppermute | solution.py:60
  34.3 1.2 collective-permute-start.13
  35.9 6.6 %collective-permute-done.4.refs_5_ = bf16[512,512]{1,0:T(8,128)(2,1)S(1)} collective-permute-done((bf16[512,512]{1,0:T(8,128)(2,1)S(1)}, bf16[512,512]{1,0:T(8,128)(2,1)S(1)}, u32[]{:S(2)}, u32[]{:S(2)}) %collective-permute-start.4) | collective-permute-done | bytes 524320 | tf_op jit(solution)/shard_map/ppermute | solution.py:60
  42.5 3.7 %collective-permute-done.12.refs_1_ = bf16[4,2,144,256]{3,2,1,0:T(8,128)(2,1)S(1)} collective-permute-done((bf16[4,2,144,256]{3,2,1,0:T(8,128)(2,1)S(1)}, bf16[4,2,144,256]{3,2,1,0:T(8,128)(2,1)S(1)}, u32[]{:S(2)}, u32[]{:S(2)}) %collective-permute-start.12) | collective-permute-done | bytes 589856 | tf_op jit(solution)/shard_map/ppermute | solution.py:39
  46.2 1.7 collective-permute-start.15
  47.9 3.0 %collective-permute-start.2 = (bf16[512,512]{1,0:T(8,128)(2,1)S(1)}, bf16[512,512]{1,0:T(8,128)(2,1)S(1)}, u32[]{:S(2)}, u32[]{:S(2)}) collective-permute-start(bf16[512,512]{1,0:T(8,128)(2,1)S(1)} %collective-permute-done.1.refs_2_), channel_id=1, source_target_pairs={{0,7},{1,0},{2,1},{3,2},{4,3},{5,4},{6,5},{7,6},{8,15},{9,8},{10,9... | collective-permute-start | bytes 1572872 | tf_op jit(solution)/shard_map/ppermute | solution.py:60
  51.6 2.8 %collective-permute-start.17 = (bf16[4,2,144,256]{3,2,1,0:T(8,128)(2,1)S(1)}, bf16[4,2,144,256]{3,2,1,0:T(8,128)(2,1)S(1)}, u32[]{:S(2)}, u32[]{:S(2)}) collective-permute-start(bf16[4,2,144,256]{3,2,1,0:T(8,128)(2,1)S(1)} %collective-permute-done.13.refs_2_), channel_id=1, source_target_pairs={{0,8},{8,0},{16,24},{24,16},{32,40},{40,32},{48,56},{56,48},{64,72... | collective-permute-start | bytes 1769480 | tf_op jit(solution)/shard_map/ppermute | solution.py:52
  54.4 0.7 collective-permute-done.5.refs_4_
  55.1 3.0 %collective-permute-start.18 = (bf16[4,2,144,256]{3,2,1,0:T(8,128)(2,1)S(1)}, bf16[4,2,144,256]{3,2,1,0:T(8,128)(2,1)S(1)}, u32[]{:S(2)}, u32[]{:S(2)}) collective-permute-start(bf16[4,2,144,256]{3,2,1,0:T(8,128)(2,1)S(1)} %collective-permute-done.14.refs_3_), channel_id=1, source_target_pairs={{0,8},{8,0},{16,24},{24,16},{32,40},{40,32},{48,56},{56,48},{64,72... | collective-permute-start | bytes 1769480 | tf_op jit(solution)/shard_map/ppermute | solution.py:52
  58.0 0.7 slice.115
  58.8 3.4 %collective-permute-done.2.refs_3_ = bf16[512,512]{1,0:T(8,128)(2,1)S(1)} collective-permute-done((bf16[512,512]{1,0:T(8,128)(2,1)S(1)}, bf16[512,512]{1,0:T(8,128)(2,1)S(1)}, u32[]{:S(2)}, u32[]{:S(2)}) %collective-permute-start.2) | collective-permute-done | bytes 524320 | tf_op jit(solution)/shard_map/ppermute | solution.py:60
  62.4 0.7 slice.116
  63.1 3.3 %collective-permute-start.7 = (bf16[256,512]{1,0:T(8,128)(2,1)}, bf16[256,512]{1,0:T(8,128)(2,1)}, u32[]{:S(2)}, u32[]{:S(2)}) collective-permute-start(bf16[256,512]{1,0:T(8,128)(2,1)} %slice.116), channel_id=1, source_target_pairs={{0,7},{1,0},{2,1},{3,2},{4,3},{5,4},{6,5},{7,6},{8,15},{9,8},{10,9... | collective-permute-start | bytes 786440 | tf_op jit(solution)/shard_map/ppermute | solution.py:60
  66.5 0.8 copy-done.14
  67.5 0.8 copy-done.16
  68.4 5.2 %assemble.1 = (bf16[4096,512]{1,0:T(8,128)(2,1)}, f32[24,256]{1,0:T(8,128)}) custom-call(s32[4]{0:T(128)} %pad_add_fusion.pos, bf16[4,2,144,256]{3,2,1,0:T(8,128)(2,1)} %copy-done.6, bf16[4,2,144,256]{3,2,1,0:T(8,128)(2,1)} %copy-done.10, bf16[4,2,144,256]{3,2,1,0:T(8,128)(2,1)} %copy-done.11, bf16[4,2,144,256]{3,2,1,0:T(8,128)(2,1)} %copy-done.12, ...), custom_call_target="tpu_custom_call" | custom-call | flops 1000000 | bytes 8937488 | tf_op jit(solution)/shard_map/assemble/pallas_call | solution.py:88
  74.4 9.4 %project.1 = (bf16[256,512]{1,0:T(8,128)(2,1)}, bf16[256,512]{1,0:T(8,128)(2,1)}, bf16[4,128,128]{2,1,0:T(8,128)(2,1)}, bf16[4,128,128]{2,1,0:T(8,128)(2,1)}) custom-call(s32[4]{0:T(128)} %pad_add_fusion.pos, bf16[512,512]{1,0:T(8,128)(2,1)} %get-tuple-element.42.refs_0_, bf16[512,512]{1,0:T(8,128)(2,1)} %copy-done.3, bf16[512,512]{1,0:T(8,128)(2,1)} %copy-done.5, ...), custom_call_target="tpu_custom_call" | custom-call | flops 2147483648 | bytes 13649936 | tf_op jit(solution)/shard_map/project/pallas_call | solution.py:88
  83.8 1.1 collective-permute-start.19
  84.9 1.2 collective-permute-done.19.other
  86.7 1.7 join_chip.1.q
  88.4 1.1 collective-permute-start.20
  89.5 2.5 %collective-permute-start.21 = (bf16[4,128,128]{2,1,0:T(8,128)(2,1)}, bf16[4,128,128]{2,1,0:T(8,128)(2,1)S(1)}, u32[]{:S(2)}, u32[]{:S(2)}) collective-permute-start(bf16[4,128,128]{2,1,0:T(8,128)(2,1)} %join_chip.1.q), channel_id=1, source_target_pairs={{0,32},{8,40},{16,48},{24,56},{32,0},{40,8},{48,16},{56,24},{64,96... | collective-permute-start | bytes 393224 | tf_op jit(solution)/shard_map/ppermute | solution.py:48
  92.0 1.2 collective-permute-start.22
  93.1 2.5 %grad_local.1.local_ref = f32[256,512]{1,0:T(8,128)} custom-call(s32[4]{0:T(128)} %pad_add_fusion.pos, bf16[256,512]{1,0:T(8,128)(2,1)} %get-tuple-element.53.vals, bf16[256,128]{1,0:T(8,128)(2,1)} %x_ref.1, bf16[256,128]{1,0:T(8,128)(2,1)} %refs_10_.1, f32[256,8]{1,0:T(8,128)} %get-tuple-element.54.a_ref, f32[8,256]{1,0:T(8,128)} %get-tuple-element.55.at_ref), custom_call_target="tpu_custom_call" | custom-call | flops 1000000000 | bytes 933904 | tf_op jit(solution)/shard_map/grad_local/pallas_call | solution.py:88
  95.7 2.6 %collective-permute-done.21.g2 = bf16[4,128,128]{2,1,0:T(8,128)(2,1)S(1)} collective-permute-done((bf16[4,128,128]{2,1,0:T(8,128)(2,1)}, bf16[4,128,128]{2,1,0:T(8,128)(2,1)S(1)}, u32[]{:S(2)}, u32[]{:S(2)}) %collective-permute-start.21) | collective-permute-done | bytes 131104 | tf_op jit(solution)/shard_map/ppermute | solution.py:48
  99.6 2.0 join_row.1
  101.8 4.3 %collective-permute-start.24 = (bf16[4,128,128]{2,1,0:T(8,128)(2,1)}, bf16[4,128,128]{2,1,0:T(8,128)(2,1)S(1)}, u32[]{:S(2)}, u32[]{:S(2)}) collective-permute-start(bf16[4,128,128]{2,1,0:T(8,128)(2,1)} %get-tuple-element.62), channel_id=1, source_target_pairs={{0,128},{8,136},{16,144},{24,152},{32,160},{40,168},{48,176},{56,1... | collective-permute-start | bytes 393224 | tf_op jit(solution)/shard_map/ppermute | solution.py:48
  106.1 2.5 %mixed_local.1.refs_9_ = f32[256,512]{1,0:T(8,128)} custom-call(s32[4]{0:T(128)} %pad_add_fusion.pos, bf16[256,512]{1,0:T(8,128)(2,1)} %get-tuple-element.63.vals, bf16[256,128]{1,0:T(8,128)(2,1)} %x_ref.1, bf16[256,128]{1,0:T(8,128)(2,1)} %refs_10_.1, f32[256,8]{1,0:T(8,128)} %get-tuple-element.54.a_ref, f32[8,256]{1,0:T(8,128)} %get-tuple-element.55.at_ref), custom_call_target="tpu_custom_call" | custom-call | flops 1000000000 | bytes 933904 | tf_op jit(solution)/shard_map/mixed_local/pallas_call | solution.py:88
  108.6 2.6 %collective-permute-done.24.g2 = bf16[4,128,128]{2,1,0:T(8,128)(2,1)S(1)} collective-permute-done((bf16[4,128,128]{2,1,0:T(8,128)(2,1)}, bf16[4,128,128]{2,1,0:T(8,128)(2,1)S(1)}, u32[]{:S(2)}, u32[]{:S(2)}) %collective-permute-start.24) | collective-permute-done | bytes 131104 | tf_op jit(solution)/shard_map/ppermute | solution.py:48
  112.2 2.1 join_rows.1
  114.3 2.1 collective-permute-start.26
  116.4 1.2 collective-permute-done.26.sib_ref.refs_13_
  118.3 6.5 %token_parts.1 = (bf16[8,256,512]{2,1,0:T(8,128)(2,1)}, bf16[256,512]{1,0:T(8,128)(2,1)}) custom-call(s32[4]{0:T(128)} %pad_add_fusion.pos, bf16[4096,512]{1,0:T(8,128)(2,1)} %all-gather.2.cloned.1.call-done.refs_10_.w_in, f32[256,512]{1,0:T(8,128)} %grad_local.1.local_ref, bf16[256,128]{1,0:T(8,128)(2,1)} %x_ref.1, f32[256,8]{1,0:T(8,128)} %get-tuple-element.57.eo_ref, ...), custom_call_target="tpu_custom_call" | custom-call | flops 1073741824 | bytes 7415824 | tf_op jit(solution)/shard_map/token_parts/pallas_call | solution.py:88
  124.8 5.8 %in_parts.1 = (bf16[4,4,256,256]{3,2,1,0:T(8,128)(2,1)}, bf16[4,4,256,256]{3,2,1,0:T(8,128)(2,1)}) custom-call(s32[4]{0:T(128)} %pad_add_fusion.pos, bf16[512,512]{1,0:T(8,128)(2,1)} %get-tuple-element.42.refs_0_, bf16[512,512]{1,0:T(8,128)(2,1)} %copy-done.3, bf16[512,512]{1,0:T(8,128)(2,1)} %copy-done.5, bf16[512,512]{1,0:T(8,128)(2,1)} %copy-done.1, ...), custom_call_target="tpu_custom_call" | custom-call | flops 1073741824 | bytes 8650768 | tf_op jit(solution)/shard_map/in_parts/pallas_call | solution.py:88
  131.2 6.1 %out_parts.1 = (bf16[4,4,256,256]{3,2,1,0:T(8,128)(2,1)}, bf16[4,4,256,256]{3,2,1,0:T(8,128)(2,1)}) custom-call(s32[4]{0:T(128)} %pad_add_fusion.pos, bf16[512,512]{1,0:T(8,128)(2,1)} %get-tuple-element.42.refs_0_, bf16[512,512]{1,0:T(8,128)(2,1)} %copy-done.3, bf16[512,512]{1,0:T(8,128)(2,1)} %copy-done.5, bf16[512,512]{1,0:T(8,128)(2,1)} %copy-done.1, ...), custom_call_target="tpu_custom_call" | custom-call | flops 1073741824 | bytes 9248784 | tf_op jit(solution)/shard_map/out_parts/pallas_call | solution.py:88
  138.2 3.6 %collective-permute-done.28 = bf16[4,4,256,256]{3,2,1,0:T(8,128)(2,1)S(1)} collective-permute-done((bf16[4,4,256,256]{3,2,1,0:T(8,128)(2,1)}, bf16[4,4,256,256]{3,2,1,0:T(8,128)(2,1)S(1)}, u32[]{:S(2)}, u32[]{:S(2)}) %collective-permute-start.28) | collective-permute-done | bytes 2097184 | tf_op jit(solution)/shard_map/ppermute | solution.py:52
  142.4 1.1 fusion.8
  143.5 2.7 %collective-permute-start.31 = (bf16[2,2,256,256]{3,2,0,1:T(8,128)(2,1)}, bf16[2,2,256,256]{3,2,0,1:T(8,128)(2,1)}, u32[]{:S(2)}, u32[]{:S(2)}) collective-permute-start(bf16[2,2,256,256]{3,2,0,1:T(8,128)(2,1)} %get-tuple-element.93), channel_id=1, source_target_pairs={{0,48},{8,200},{16,0},{24,216},{32,16},{40,232},{48,32},{56,248},{... | collective-permute-start | bytes 1572872 | tf_op jit(solution)/shard_map/ppermute | solution.py:39
  146.2 7.2 %collective-permute-done.29 = bf16[2,2,256,256]{3,2,0,1:T(8,128)(2,1)} collective-permute-done((bf16[2,2,256,256]{3,2,0,1:T(8,128)(2,1)}, bf16[2,2,256,256]{3,2,0,1:T(8,128)(2,1)}, u32[]{:S(2)}, u32[]{:S(2)}) %collective-permute-start.29) | collective-permute-done | bytes 524320 | tf_op jit(solution)/shard_map/ppermute | solution.py:39
  153.4 1.2 add_convert_fusion.1
  154.7 1.2 add_convert_fusion
  155.9 2.7 %collective-permute-start.32 = (bf16[4,2,256,256]{3,2,0,1:T(8,128)(2,1)S(1)}, bf16[4,2,256,256]{3,2,0,1:T(8,128)(2,1)S(1)}, u32[]{:S(2)}, u32[]{:S(2)}) collective-permute-start(bf16[4,2,256,256]{3,2,0,1:T(8,128)(2,1)S(1)} %add_convert_fusion), channel_id=1, source_target_pairs={{0,48},{8,200},{16,0},{24,216},{32,16},{40,232},{48,32},{56,248},{... | collective-permute-start | bytes 3145736 | tf_op jit(solution)/shard_map/ppermute | solution.py:39
  158.6 11.3 %collective-permute-done.30 = bf16[4,2,256,256]{3,2,0,1:T(8,128)(2,1)S(1)} collective-permute-done((bf16[4,2,256,256]{3,2,0,1:T(8,128)(2,1)S(1)}, bf16[4,2,256,256]{3,2,0,1:T(8,128)(2,1)S(1)}, u32[]{:S(2)}, u32[]{:S(2)}) %collective-permute-start.30) | collective-permute-done | bytes 1048608 | tf_op jit(solution)/shard_map/ppermute | solution.py:39
  170.8 0.8 slice_bitcast_fusion.3
  171.7 2.5 %collective-permute-start.34 = (bf16[2,256,256]{2,1,0:T(8,128)(2,1)S(1)}, bf16[2,256,256]{2,1,0:T(8,128)(2,1)S(1)}, u32[]{:S(2)}, u32[]{:S(2)}) collective-permute-start(bf16[2,256,256]{2,1,0:T(8,128)(2,1)S(1)} %get-tuple-element.91), channel_id=1, source_target_pairs={{0,128},{8,40},{16,144},{24,56},{32,160},{40,8},{48,176},{56,24},{... | collective-permute-start | bytes 786440 | tf_op jit(solution)/shard_map/ppermute | solution.py:39
  174.8 3.8 %collective-permute-done.33 = bf16[2,256,256]{2,1,0:T(8,128)(2,1)S(1)} collective-permute-done((bf16[2,256,256]{2,1,0:T(8,128)(2,1)}, bf16[2,256,256]{2,1,0:T(8,128)(2,1)S(1)}, u32[]{:S(2)}, u32[]{:S(2)}) %collective-permute-start.33) | collective-permute-done | bytes 262176 | tf_op jit(solution)/shard_map/ppermute | solution.py:39
  178.5 2.5 %collective-permute-done.34 = bf16[2,256,256]{2,1,0:T(8,128)(2,1)S(1)} collective-permute-done((bf16[2,256,256]{2,1,0:T(8,128)(2,1)S(1)}, bf16[2,256,256]{2,1,0:T(8,128)(2,1)S(1)}, u32[]{:S(2)}, u32[]{:S(2)}) %collective-permute-start.34) | collective-permute-done | bytes 262176 | tf_op jit(solution)/shard_map/ppermute | solution.py:39
  181.0 0.7 collective-permute-done.35
  181.7 1.1 fusion.11
  182.8 3.5 %collective-permute-start.36 = (f32[2,128,256]{2,1,0:T(8,128)S(1)}, f32[2,128,256]{2,1,0:T(8,128)S(1)}, u32[]{:S(2)}, u32[]{:S(2)}) collective-permute-start(f32[2,128,256]{2,1,0:T(8,128)S(1)} %slice_select_fusion), channel_id=1, source_target_pairs={{0,8},{8,0},{16,24},{24,16},{32,40},{40,32},{48,56},{56,48},{64,72... | collective-permute-start | bytes 786440 | tf_op jit(solution)/shard_map/ppermute | solution.py:52
  186.3 0.8 dynamic_slice.3
  187.6 1.0 fusion.15
  188.6 11.2 %all_to_all.12 = f32[8,1,128]{2,1,0:T(1,128)S(1)} all-to-all(f32[8,1,128]{2,1,0:T(1,128)S(1)} %broadcast_in_dim.8), channel_id=1, replica_groups=mesh['seq'=32,'tp'=8] {'tp'}, dimensions={0} | all-to-all | bytes 8192 | tf_op jit(solution)/shard_map/all_to_all | solution.py:520
  200.5 9.0 %all-to-all-start = ((f32[32,1,512]{2,1,0:T(1,128)}), f32[32,1,512]{2,1,0:T(1,128)S(1)}, u32[]{:S(2)}, u32[]{:S(2)}) async-start(f32[32,1,512]{2,1,0:T(1,128)} %broadcast_in_dim.7), calls=%async_computation.1 | async-start | bytes 131072 | tf_op jit(solution)/shard_map/all_to_all | solution.py:520
  210.0 6.8 %all-to-all-done = f32[32,1,512]{2,1,0:T(1,128)S(1)} async-done(((f32[32,1,512]{2,1,0:T(1,128)}), f32[32,1,512]{2,1,0:T(1,128)S(1)}, u32[]{:S(2)}, u32[]{:S(2)}) %all-to-all-start) | async-done | bytes 65568 | tf_op jit(solution)/shard_map/all_to_all | solution.py:520
  (109 shorter events, 13.6 us)
Async XLA Ops:
  7.2 66.8 %all-gather.2.cloned.1.call-start = ((), (), s32[]{:S(2)}) async-start(), calls=%async_computation.3 | async-start | bytes 4325376 | tf_op jit(solution)/shard_map/all_gather | solution.py:551
  10.6 206.9 %reduce-scatter.2.cloned.1.call-start = ((), (), s32[]{:S(2)}) async-start(), calls=%async_computation.4 | async-start | bytes 2359296 | tf_op jit(solution)/shard_map/reduce_scatter | solution.py:602
  10.6 18.3 %collective-permute-start.3 = (bf16[512,512]{1,0:T(8,128)(2,1)}, bf16[512,512]{1,0:T(8,128)(2,1)S(1)}, u32[]{:S(2)}, u32[]{:S(2)}) collective-permute-start(bf16[512,512]{1,0:T(8,128)(2,1)} %get-tuple-element.42.refs_0_), channel_id=1, source_target_pairs={{0,1},{1,2},{2,3},{3,4},{4,5},{5,6},{6,7},{7,0},{8,9},{9,10},{10,1... | collective-permute-start | bytes 1572872 | tf_op jit(solution)/shard_map/ppermute | solution.py:60
  13.2 4.7 %collective-permute-start.8 = (bf16[144,256]{1,0:T(8,128)(2,1)}, bf16[144,256]{1,0:T(8,128)(2,1)S(1)}, u32[]{:S(2)}, u32[]{:S(2)}) collective-permute-start(bf16[144,256]{1,0:T(8,128)(2,1)} %get-tuple-element.44), channel_id=1, source_target_pairs={{0,8},{8,0},{16,24},{24,16},{32,40},{40,32},{48,56},{56,48},{64,72... | collective-permute-start | bytes 221192 | tf_op jit(solution)/shard_map/ppermute | solution.py:52
  14.1 17.5 %collective-permute-start = (bf16[512,512]{1,0:T(8,128)(2,1)}, bf16[512,512]{1,0:T(8,128)(2,1)S(1)}, u32[]{:S(2)}, u32[]{:S(2)}) collective-permute-start(bf16[512,512]{1,0:T(8,128)(2,1)} %get-tuple-element.42.refs_0_), channel_id=1, source_target_pairs={{0,7},{1,0},{2,1},{3,2},{4,3},{5,4},{6,5},{7,6},{8,15},{9,8},{10,9... | collective-permute-start | bytes 1572872 | tf_op jit(solution)/shard_map/ppermute | solution.py:60
  18.8 10.2 %collective-permute-start.9 = (bf16[2,144,256]{2,1,0:T(8,128)(2,1)S(1)}, bf16[2,144,256]{2,1,0:T(8,128)(2,1)S(1)}, u32[]{:S(2)}, u32[]{:S(2)}) collective-permute-start(bf16[2,144,256]{2,1,0:T(8,128)(2,1)S(1)} %get-tuple-element.99), channel_id=1, source_target_pairs={{0,48},{8,200},{16,0},{24,216},{32,16},{40,232},{48,32},{56,248},{... | collective-permute-start | bytes 442376 | tf_op jit(solution)/shard_map/ppermute | solution.py:39
  21.6 7.4 %collective-permute-start.10 = (bf16[2,144,256]{2,1,0:T(8,128)(2,1)S(1)}, bf16[2,144,256]{2,1,0:T(8,128)(2,1)S(1)}, u32[]{:S(2)}, u32[]{:S(2)}) collective-permute-start(bf16[2,144,256]{2,1,0:T(8,128)(2,1)S(1)} %get-tuple-element.99), channel_id=1, source_target_pairs={{0,32},{8,136},{16,48},{24,152},{32,0},{40,168},{48,16},{56,184},{... | collective-permute-start | bytes 442376 | tf_op jit(solution)/shard_map/ppermute | solution.py:39
  22.0 7.0 %collective-permute-start.11 = (bf16[2,144,256]{2,1,0:T(8,128)(2,1)S(1)}, bf16[2,144,256]{2,1,0:T(8,128)(2,1)S(1)}, u32[]{:S(2)}, u32[]{:S(2)}) collective-permute-start(bf16[2,144,256]{2,1,0:T(8,128)(2,1)S(1)} %get-tuple-element.99), channel_id=1, source_target_pairs={{0,16},{8,72},{16,32},{24,88},{32,48},{40,104},{48,0},{56,120},{64... | collective-permute-start | bytes 442376 | tf_op jit(solution)/shard_map/ppermute | solution.py:39
  29.0 44.6 %copy-start.2 = (bf16[512,512]{1,0:T(8,128)(2,1)}, bf16[512,512]{1,0:T(8,128)(2,1)S(1)}, u32[]{:S(2)}) copy-start(bf16[512,512]{1,0:T(8,128)(2,1)S(1)} %collective-permute-done.3.refs_6_) | copy-start | bytes 1572868
  29.0 13.5 %collective-permute-start.4 = (bf16[512,512]{1,0:T(8,128)(2,1)S(1)}, bf16[512,512]{1,0:T(8,128)(2,1)S(1)}, u32[]{:S(2)}, u32[]{:S(2)}) collective-permute-start(bf16[512,512]{1,0:T(8,128)(2,1)S(1)} %collective-permute-done.3.refs_6_), channel_id=1, source_target_pairs={{0,1},{1,2},{2,3},{3,4},{4,5},{5,6},{6,7},{7,0},{8,9},{9,10},{10,1... | collective-permute-start | bytes 1572872 | tf_op jit(solution)/shard_map/ppermute | solution.py:60
  29.1 37.4 %copy-start.6 = (bf16[4,2,144,256]{3,2,1,0:T(8,128)(2,1)}, bf16[4,2,144,256]{3,2,1,0:T(8,128)(2,1)S(1)}, u32[]{:S(2)}) copy-start(bf16[4,2,144,256]{3,2,1,0:T(8,128)(2,1)S(1)} %pad_maximum_fusion.refs_0_) | copy-start | bytes 1769476
  29.1 17.1 %collective-permute-start.12 = (bf16[4,2,144,256]{3,2,1,0:T(8,128)(2,1)S(1)}, bf16[4,2,144,256]{3,2,1,0:T(8,128)(2,1)S(1)}, u32[]{:S(2)}, u32[]{:S(2)}) collective-permute-start(bf16[4,2,144,256]{3,2,1,0:T(8,128)(2,1)S(1)} %pad_maximum_fusion.refs_0_), channel_id=1, source_target_pairs={{0,192},{8,56},{16,208},{24,8},{32,224},{40,24},{48,240},{56,40},{... | collective-permute-start | bytes 1769480 | tf_op jit(solution)/shard_map/ppermute | solution.py:39
  31.7 41.9 %copy-start.3 = (bf16[512,512]{1,0:T(8,128)(2,1)}, bf16[512,512]{1,0:T(8,128)(2,1)S(1)}, u32[]{:S(2)}) copy-start(bf16[512,512]{1,0:T(8,128)(2,1)S(1)} %collective-permute-done.refs_1_) | copy-start | bytes 1572868
  31.7 16.2 %collective-permute-start.1 = (bf16[512,512]{1,0:T(8,128)(2,1)S(1)}, bf16[512,512]{1,0:T(8,128)(2,1)S(1)}, u32[]{:S(2)}, u32[]{:S(2)}) collective-permute-start(bf16[512,512]{1,0:T(8,128)(2,1)S(1)} %collective-permute-done.refs_1_), channel_id=1, source_target_pairs={{0,7},{1,0},{2,1},{3,2},{4,3},{5,4},{6,5},{7,6},{8,15},{9,8},{10,9... | collective-permute-start | bytes 1572872 | tf_op jit(solution)/shard_map/ppermute | solution.py:60
  34.3 16.5 %collective-permute-start.13 = (bf16[4,2,144,256]{3,2,1,0:T(8,128)(2,1)S(1)}, bf16[4,2,144,256]{3,2,1,0:T(8,128)(2,1)S(1)}, u32[]{:S(2)}, u32[]{:S(2)}) collective-permute-start(bf16[4,2,144,256]{3,2,1,0:T(8,128)(2,1)S(1)} %pad_maximum_fusion.refs_0_), channel_id=1, source_target_pairs={{0,128},{8,40},{16,144},{24,56},{32,160},{40,8},{48,176},{56,24},{... | collective-permute-start | bytes 1769480 | tf_op jit(solution)/shard_map/ppermute | solution.py:39
  35.5 16.0 %collective-permute-start.14 = (bf16[4,2,144,256]{3,2,1,0:T(8,128)(2,1)S(1)}, bf16[4,2,144,256]{3,2,1,0:T(8,128)(2,1)S(1)}, u32[]{:S(2)}, u32[]{:S(2)}) collective-permute-start(bf16[4,2,144,256]{3,2,1,0:T(8,128)(2,1)S(1)} %pad_maximum_fusion.refs_0_), channel_id=1, source_target_pairs={{0,64},{8,24},{16,80},{24,40},{32,96},{40,56},{48,112},{56,8},{64,... | collective-permute-start | bytes 1769480 | tf_op jit(solution)/shard_map/ppermute | solution.py:39
  42.5 31.1 %copy-start.4 = (bf16[512,512]{1,0:T(8,128)(2,1)}, bf16[512,512]{1,0:T(8,128)(2,1)S(1)}, u32[]{:S(2)}) copy-start(bf16[512,512]{1,0:T(8,128)(2,1)S(1)} %collective-permute-done.4.refs_5_) | copy-start | bytes 1572868
  42.5 12.6 %collective-permute-start.5 = (bf16[512,512]{1,0:T(8,128)(2,1)S(1)}, bf16[512,512]{1,0:T(8,128)(2,1)S(1)}, u32[]{:S(2)}, u32[]{:S(2)}) collective-permute-start(bf16[512,512]{1,0:T(8,128)(2,1)S(1)} %collective-permute-done.4.refs_5_), channel_id=1, source_target_pairs={{0,1},{1,2},{2,3},{3,4},{4,5},{5,6},{6,7},{7,0},{8,9},{9,10},{10,1... | collective-permute-start | bytes 1572872 | tf_op jit(solution)/shard_map/ppermute | solution.py:60
  46.2 20.3 %copy-start.10 = (bf16[4,2,144,256]{3,2,1,0:T(8,128)(2,1)}, bf16[4,2,144,256]{3,2,1,0:T(8,128)(2,1)S(1)}, u32[]{:S(2)}) copy-start(bf16[4,2,144,256]{3,2,1,0:T(8,128)(2,1)S(1)} %collective-permute-done.12.refs_1_) | copy-start | bytes 1769476
  46.2 16.9 %collective-permute-start.15 = (bf16[4,2,144,256]{3,2,1,0:T(8,128)(2,1)S(1)}, bf16[4,2,144,256]{3,2,1,0:T(8,128)(2,1)S(1)}, u32[]{:S(2)}, u32[]{:S(2)}) collective-permute-start(bf16[4,2,144,256]{3,2,1,0:T(8,128)(2,1)S(1)} %pad_maximum_fusion.refs_0_), channel_id=1, source_target_pairs={{0,8},{8,0},{16,24},{24,16},{32,40},{40,32},{48,56},{56,48},{64,72... | collective-permute-start | bytes 1769480 | tf_op jit(solution)/shard_map/ppermute | solution.py:52
  47.9 25.7 %copy-start.5 = (bf16[512,512]{1,0:T(8,128)(2,1)}, bf16[512,512]{1,0:T(8,128)(2,1)S(1)}, u32[]{:S(2)}) copy-start(bf16[512,512]{1,0:T(8,128)(2,1)S(1)} %collective-permute-done.1.refs_2_) | copy-start | bytes 1572868
  47.9 14.2 %collective-permute-start.2 = (bf16[512,512]{1,0:T(8,128)(2,1)S(1)}, bf16[512,512]{1,0:T(8,128)(2,1)S(1)}, u32[]{:S(2)}, u32[]{:S(2)}) collective-permute-start(bf16[512,512]{1,0:T(8,128)(2,1)S(1)} %collective-permute-done.1.refs_2_), channel_id=1, source_target_pairs={{0,7},{1,0},{2,1},{3,2},{4,3},{5,4},{6,5},{7,6},{8,15},{9,8},{10,9... | collective-permute-start | bytes 1572872 | tf_op jit(solution)/shard_map/ppermute | solution.py:60
  50.8 15.6 %copy-start.11 = (bf16[4,2,144,256]{3,2,1,0:T(8,128)(2,1)}, bf16[4,2,144,256]{3,2,1,0:T(8,128)(2,1)S(1)}, u32[]{:S(2)}) copy-start(bf16[4,2,144,256]{3,2,1,0:T(8,128)(2,1)S(1)} %collective-permute-done.13.refs_2_) | copy-start | bytes 1769476
  50.8 15.6 %collective-permute-start.16 = (bf16[4,2,144,256]{3,2,1,0:T(8,128)(2,1)S(1)}, bf16[4,2,144,256]{3,2,1,0:T(8,128)(2,1)S(1)}, u32[]{:S(2)}, u32[]{:S(2)}) collective-permute-start(bf16[4,2,144,256]{3,2,1,0:T(8,128)(2,1)S(1)} %collective-permute-done.12.refs_1_), channel_id=1, source_target_pairs={{0,8},{8,0},{16,24},{24,16},{32,40},{40,32},{48,56},{56,48},{64,72... | collective-permute-start | bytes 1769480 | tf_op jit(solution)/shard_map/ppermute | solution.py:52
  51.6 14.9 %copy-start.12 = (bf16[4,2,144,256]{3,2,1,0:T(8,128)(2,1)}, bf16[4,2,144,256]{3,2,1,0:T(8,128)(2,1)S(1)}, u32[]{:S(2)}) copy-start(bf16[4,2,144,256]{3,2,1,0:T(8,128)(2,1)S(1)} %collective-permute-done.14.refs_3_) | copy-start | bytes 1769476
  51.6 14.9 %collective-permute-start.17 = (bf16[4,2,144,256]{3,2,1,0:T(8,128)(2,1)S(1)}, bf16[4,2,144,256]{3,2,1,0:T(8,128)(2,1)S(1)}, u32[]{:S(2)}, u32[]{:S(2)}) collective-permute-start(bf16[4,2,144,256]{3,2,1,0:T(8,128)(2,1)S(1)} %collective-permute-done.13.refs_2_), channel_id=1, source_target_pairs={{0,8},{8,0},{16,24},{24,16},{32,40},{40,32},{48,56},{56,48},{64,72... | collective-permute-start | bytes 1769480 | tf_op jit(solution)/shard_map/ppermute | solution.py:52
  55.1 18.6 %copy-start = (bf16[512,512]{1,0:T(8,128)(2,1)}, bf16[512,512]{1,0:T(8,128)(2,1)S(1)}, u32[]{:S(2)}) copy-start(bf16[512,512]{1,0:T(8,128)(2,1)S(1)} %collective-permute-done.5.refs_4_) | copy-start | bytes 1572868
  55.1 11.4 %collective-permute-start.18 = (bf16[4,2,144,256]{3,2,1,0:T(8,128)(2,1)S(1)}, bf16[4,2,144,256]{3,2,1,0:T(8,128)(2,1)S(1)}, u32[]{:S(2)}, u32[]{:S(2)}) collective-permute-start(bf16[4,2,144,256]{3,2,1,0:T(8,128)(2,1)S(1)} %collective-permute-done.14.refs_3_), channel_id=1, source_target_pairs={{0,8},{8,0},{16,24},{24,16},{32,40},{40,32},{48,56},{56,48},{64,72... | collective-permute-start | bytes 1769480 | tf_op jit(solution)/shard_map/ppermute | solution.py:52
  62.1 11.5 %copy-start.1 = (bf16[512,512]{1,0:T(8,128)(2,1)}, bf16[512,512]{1,0:T(8,128)(2,1)S(1)}, u32[]{:S(2)}) copy-start(bf16[512,512]{1,0:T(8,128)(2,1)S(1)} %collective-permute-done.2.refs_3_) | copy-start | bytes 1572868
  62.1 11.5 %collective-permute-start.6 = (bf16[256,512]{1,0:T(8,128)(2,1)}, bf16[256,512]{1,0:T(8,128)(2,1)S(1)}, u32[]{:S(2)}, u32[]{:S(2)}) collective-permute-start(bf16[256,512]{1,0:T(8,128)(2,1)} %slice.115), channel_id=1, source_target_pairs={{0,1},{1,2},{2,3},{3,4},{4,5},{5,6},{6,7},{7,0},{8,9},{9,10},{10,1... | collective-permute-start | bytes 786440 | tf_op jit(solution)/shard_map/ppermute | solution.py:60
  63.1 3.4 %copy-start.13 = (bf16[4,2,144,256]{3,2,1,0:T(8,128)(2,1)}, bf16[4,2,144,256]{3,2,1,0:T(8,128)(2,1)S(1)}, u32[]{:S(2)}) copy-start(bf16[4,2,144,256]{3,2,1,0:T(8,128)(2,1)S(1)} %collective-permute-done.15.refs_4_) | copy-start | bytes 1769476
  63.1 10.6 %collective-permute-start.7 = (bf16[256,512]{1,0:T(8,128)(2,1)}, bf16[256,512]{1,0:T(8,128)(2,1)}, u32[]{:S(2)}, u32[]{:S(2)}) collective-permute-start(bf16[256,512]{1,0:T(8,128)(2,1)} %slice.116), channel_id=1, source_target_pairs={{0,7},{1,0},{2,1},{3,2},{4,3},{5,4},{6,5},{7,6},{8,15},{9,8},{10,9... | collective-permute-start | bytes 786440 | tf_op jit(solution)/shard_map/ppermute | solution.py:60
  66.4 0.8 copy-start.14
  66.4 1.1 copy-start.15
  67.5 0.8 copy-start.16
  73.7 0.7 copy-start.7
  83.8 2.3 %collective-permute-start.19 = (bf16[4,128,128]{2,1,0:T(8,128)(2,1)}, bf16[4,128,128]{2,1,0:T(8,128)(2,1)S(1)}, u32[]{:S(2)}, u32[]{:S(2)}) collective-permute-start(bf16[4,128,128]{2,1,0:T(8,128)(2,1)} %get-tuple-element.51), channel_id=1, source_target_pairs={{0,8},{8,0},{16,24},{24,16},{32,40},{40,32},{48,56},{56,48},{64,72... | collective-permute-start | bytes 393224 | tf_op jit(solution)/shard_map/ppermute | solution.py:52
  86.1 0.7 copy-start.20
  88.4 7.3 %collective-permute-start.20 = (bf16[4,128,128]{2,1,0:T(8,128)(2,1)}, bf16[4,128,128]{2,1,0:T(8,128)(2,1)S(1)}, u32[]{:S(2)}, u32[]{:S(2)}) collective-permute-start(bf16[4,128,128]{2,1,0:T(8,128)(2,1)} %join_chip.1.q), channel_id=1, source_target_pairs={{0,16},{8,24},{16,32},{24,40},{32,48},{40,56},{48,0},{56,8},{64,80... | collective-permute-start | bytes 393224 | tf_op jit(solution)/shard_map/ppermute | solution.py:48
  89.5 8.7 %collective-permute-start.21 = (bf16[4,128,128]{2,1,0:T(8,128)(2,1)}, bf16[4,128,128]{2,1,0:T(8,128)(2,1)S(1)}, u32[]{:S(2)}, u32[]{:S(2)}) collective-permute-start(bf16[4,128,128]{2,1,0:T(8,128)(2,1)} %join_chip.1.q), channel_id=1, source_target_pairs={{0,32},{8,40},{16,48},{24,56},{32,0},{40,8},{48,16},{56,24},{64,96... | collective-permute-start | bytes 393224 | tf_op jit(solution)/shard_map/ppermute | solution.py:48
  92.0 6.3 %collective-permute-start.22 = (bf16[4,128,128]{2,1,0:T(8,128)(2,1)}, bf16[4,128,128]{2,1,0:T(8,128)(2,1)S(1)}, u32[]{:S(2)}, u32[]{:S(2)}) collective-permute-start(bf16[4,128,128]{2,1,0:T(8,128)(2,1)} %join_chip.1.q), channel_id=1, source_target_pairs={{0,48},{8,56},{16,0},{24,8},{32,16},{40,24},{48,32},{56,40},{64,11... | collective-permute-start | bytes 393224 | tf_op jit(solution)/shard_map/ppermute | solution.py:48
  95.7 2.6 %copy-start.24 = (bf16[4,128,128]{2,1,0:T(8,128)(2,1)}, bf16[4,128,128]{2,1,0:T(8,128)(2,1)S(1)}, u32[]{:S(2)}) copy-start(bf16[4,128,128]{2,1,0:T(8,128)(2,1)S(1)} %collective-permute-done.20.g1) | copy-start | bytes 393220
  98.3 0.7 copy-start.25
  101.6 7.1 %collective-permute-start.23 = (bf16[4,128,128]{2,1,0:T(8,128)(2,1)}, bf16[4,128,128]{2,1,0:T(8,128)(2,1)S(1)}, u32[]{:S(2)}, u32[]{:S(2)}) collective-permute-start(bf16[4,128,128]{2,1,0:T(8,128)(2,1)} %get-tuple-element.62), channel_id=1, source_target_pairs={{0,64},{8,72},{16,80},{24,88},{32,96},{40,104},{48,112},{56,120},{... | collective-permute-start | bytes 393224 | tf_op jit(solution)/shard_map/ppermute | solution.py:48
  101.8 9.4 %collective-permute-start.24 = (bf16[4,128,128]{2,1,0:T(8,128)(2,1)}, bf16[4,128,128]{2,1,0:T(8,128)(2,1)S(1)}, u32[]{:S(2)}, u32[]{:S(2)}) collective-permute-start(bf16[4,128,128]{2,1,0:T(8,128)(2,1)} %get-tuple-element.62), channel_id=1, source_target_pairs={{0,128},{8,136},{16,144},{24,152},{32,160},{40,168},{48,176},{56,1... | collective-permute-start | bytes 393224 | tf_op jit(solution)/shard_map/ppermute | solution.py:48
  106.1 5.4 %collective-permute-start.25 = (bf16[4,128,128]{2,1,0:T(8,128)(2,1)}, bf16[4,128,128]{2,1,0:T(8,128)(2,1)S(1)}, u32[]{:S(2)}, u32[]{:S(2)}) collective-permute-start(bf16[4,128,128]{2,1,0:T(8,128)(2,1)} %get-tuple-element.62), channel_id=1, source_target_pairs={{0,192},{8,200},{16,208},{24,216},{32,224},{40,232},{48,240},{56,2... | collective-permute-start | bytes 393224 | tf_op jit(solution)/shard_map/ppermute | solution.py:48
  108.6 2.9 %copy-start.21 = (bf16[4,128,128]{2,1,0:T(8,128)(2,1)}, bf16[4,128,128]{2,1,0:T(8,128)(2,1)S(1)}, u32[]{:S(2)}) copy-start(bf16[4,128,128]{2,1,0:T(8,128)(2,1)S(1)} %collective-permute-done.23.g1) | copy-start | bytes 393220
  114.3 3.3 %collective-permute-start.26 = (bf16[4,128,128]{2,1,0:T(8,128)(2,1)}, bf16[4,128,128]{2,1,0:T(8,128)(2,1)S(1)}, u32[]{:S(2)}, u32[]{:S(2)}) collective-permute-start(bf16[4,128,128]{2,1,0:T(8,128)(2,1)} %get-tuple-element.68), channel_id=1, source_target_pairs={{0,8},{8,0},{16,24},{24,16},{32,40},{40,32},{48,56},{56,48},{64,72... | collective-permute-start | bytes 393224 | tf_op jit(solution)/shard_map/ppermute | solution.py:52
  130.5 7.0 %collective-permute-start.27 = (bf16[4,4,256,256]{3,2,1,0:T(8,128)(2,1)}, bf16[4,4,256,256]{3,2,1,0:T(8,128)(2,1)S(1)}, u32[]{:S(2)}, u32[]{:S(2)}) collective-permute-start(bf16[4,4,256,256]{3,2,1,0:T(8,128)(2,1)} %get-tuple-element.72), channel_id=1, source_target_pairs={{0,8},{8,0},{16,24},{24,16},{32,40},{40,32},{48,56},{56,48},{64,72... | collective-permute-start | bytes 6291464 | tf_op jit(solution)/shard_map/ppermute | solution.py:52
  131.2 6.4 %copy-start.9 = (bf16[4,4,256,256]{3,2,1,0:T(8,128)(2,1)S(1)}, bf16[4,4,256,256]{3,2,1,0:T(8,128)(2,1)}, u32[]{:S(2)}) copy-start(bf16[4,4,256,256]{3,2,1,0:T(8,128)(2,1)} %get-tuple-element.71) | copy-start | bytes 6291460
  137.3 4.5 %collective-permute-start.28 = (bf16[4,4,256,256]{3,2,1,0:T(8,128)(2,1)}, bf16[4,4,256,256]{3,2,1,0:T(8,128)(2,1)S(1)}, u32[]{:S(2)}, u32[]{:S(2)}) collective-permute-start(bf16[4,4,256,256]{3,2,1,0:T(8,128)(2,1)} %get-tuple-element.76), channel_id=1, source_target_pairs={{0,8},{8,0},{16,24},{24,16},{32,40},{40,32},{48,56},{56,48},{64,72... | collective-permute-start | bytes 6291464 | tf_op jit(solution)/shard_map/ppermute | solution.py:52
  137.5 4.2 %copy-start.8 = (bf16[4,4,256,256]{3,2,1,0:T(8,128)(2,1)S(1)}, bf16[4,4,256,256]{3,2,1,0:T(8,128)(2,1)}, u32[]{:S(2)}) copy-start(bf16[4,4,256,256]{3,2,1,0:T(8,128)(2,1)} %get-tuple-element.75) | copy-start | bytes 6291460
  143.5 9.9 %collective-permute-start.29 = (bf16[2,2,256,256]{3,2,0,1:T(8,128)(2,1)}, bf16[2,2,256,256]{3,2,0,1:T(8,128)(2,1)}, u32[]{:S(2)}, u32[]{:S(2)}) collective-permute-start(bf16[2,2,256,256]{3,2,0,1:T(8,128)(2,1)} %get-tuple-element.92), channel_id=1, source_target_pairs={{0,16},{8,72},{16,32},{24,88},{32,48},{40,104},{48,0},{56,120},{64... | collective-permute-start | bytes 1572872 | tf_op jit(solution)/shard_map/ppermute | solution.py:39
  143.5 11.2 %collective-permute-start.31 = (bf16[2,2,256,256]{3,2,0,1:T(8,128)(2,1)}, bf16[2,2,256,256]{3,2,0,1:T(8,128)(2,1)}, u32[]{:S(2)}, u32[]{:S(2)}) collective-permute-start(bf16[2,2,256,256]{3,2,0,1:T(8,128)(2,1)} %get-tuple-element.93), channel_id=1, source_target_pairs={{0,48},{8,200},{16,0},{24,216},{32,16},{40,232},{48,32},{56,248},{... | collective-permute-start | bytes 1572872 | tf_op jit(solution)/shard_map/ppermute | solution.py:39
  154.6 15.3 %collective-permute-start.30 = (bf16[4,2,256,256]{3,2,0,1:T(8,128)(2,1)S(1)}, bf16[4,2,256,256]{3,2,0,1:T(8,128)(2,1)S(1)}, u32[]{:S(2)}, u32[]{:S(2)}) collective-permute-start(bf16[4,2,256,256]{3,2,0,1:T(8,128)(2,1)S(1)} %add_convert_fusion.1), channel_id=1, source_target_pairs={{0,16},{8,72},{16,32},{24,88},{32,48},{40,104},{48,0},{56,120},{64... | collective-permute-start | bytes 3145736 | tf_op jit(solution)/shard_map/ppermute | solution.py:39
  155.9 14.5 %collective-permute-start.32 = (bf16[4,2,256,256]{3,2,0,1:T(8,128)(2,1)S(1)}, bf16[4,2,256,256]{3,2,0,1:T(8,128)(2,1)S(1)}, u32[]{:S(2)}, u32[]{:S(2)}) collective-permute-start(bf16[4,2,256,256]{3,2,0,1:T(8,128)(2,1)S(1)} %add_convert_fusion), channel_id=1, source_target_pairs={{0,48},{8,200},{16,0},{24,216},{32,16},{40,232},{48,32},{56,248},{... | collective-permute-start | bytes 3145736 | tf_op jit(solution)/shard_map/ppermute | solution.py:39
  171.6 16.0 %copy-start.17 = (bf16[128,512]{1,0:T(8,128)(2,1)S(1)}, bf16[128,512]{1,0:T(8,128)(2,1)}, u32[]{:S(2)}) copy-start(bf16[128,512]{1,0:T(8,128)(2,1)} %iw.1) | copy-start | bytes 393220
  171.6 16.0 %copy-start.18 = (bf16[128,512]{1,0:T(8,128)(2,1)S(1)}, bf16[128,512]{1,0:T(8,128)(2,1)}, u32[]{:S(2)}) copy-start(bf16[128,512]{1,0:T(8,128)(2,1)} %ow.1) | copy-start | bytes 393220
  171.6 16.0 %copy-start.27 = (f32[512]{0:T(512)S(1)}, f32[512]{0:T(512)}, u32[]{:S(2)}) copy-start(f32[512]{0:T(512)} %param.12) | copy-start | bytes 6148
  171.6 6.9 %collective-permute-start.33 = (bf16[2,256,256]{2,1,0:T(8,128)(2,1)}, bf16[2,256,256]{2,1,0:T(8,128)(2,1)S(1)}, u32[]{:S(2)}, u32[]{:S(2)}) collective-permute-start(bf16[2,256,256]{2,1,0:T(8,128)(2,1)} %get-tuple-element.89), channel_id=1, source_target_pairs={{0,64},{8,24},{16,80},{24,40},{32,96},{40,56},{48,112},{56,8},{64,... | collective-permute-start | bytes 786440 | tf_op jit(solution)/shard_map/ppermute | solution.py:39
  171.7 9.3 %collective-permute-start.34 = (bf16[2,256,256]{2,1,0:T(8,128)(2,1)S(1)}, bf16[2,256,256]{2,1,0:T(8,128)(2,1)S(1)}, u32[]{:S(2)}, u32[]{:S(2)}) collective-permute-start(bf16[2,256,256]{2,1,0:T(8,128)(2,1)S(1)} %get-tuple-element.91), channel_id=1, source_target_pairs={{0,128},{8,40},{16,144},{24,56},{32,160},{40,8},{48,176},{56,24},{... | collective-permute-start | bytes 786440 | tf_op jit(solution)/shard_map/ppermute | solution.py:39
  174.2 7.5 %collective-permute-start.35 = (bf16[2,256,256]{2,1,0:T(8,128)(2,1)S(1)}, bf16[2,256,256]{2,1,0:T(8,128)(2,1)}, u32[]{:S(2)}, u32[]{:S(2)}) collective-permute-start(bf16[2,256,256]{2,1,0:T(8,128)(2,1)S(1)} %get-tuple-element.90), channel_id=1, source_target_pairs={{0,192},{8,56},{16,208},{24,8},{32,224},{40,24},{48,240},{56,40},{... | collective-permute-start | bytes 786440 | tf_op jit(solution)/shard_map/ppermute | solution.py:39
  182.8 4.7 %collective-permute-start.36 = (f32[2,128,256]{2,1,0:T(8,128)S(1)}, f32[2,128,256]{2,1,0:T(8,128)S(1)}, u32[]{:S(2)}, u32[]{:S(2)}) collective-permute-start(f32[2,128,256]{2,1,0:T(8,128)S(1)} %slice_select_fusion), channel_id=1, source_target_pairs={{0,8},{8,0},{16,24},{24,16},{32,40},{40,32},{48,56},{56,48},{64,72... | collective-permute-start | bytes 786440 | tf_op jit(solution)/shard_map/ppermute | solution.py:52
  200.5 16.3 %all-to-all-start = ((f32[32,1,512]{2,1,0:T(1,128)}), f32[32,1,512]{2,1,0:T(1,128)S(1)}, u32[]{:S(2)}, u32[]{:S(2)}) async-start(f32[32,1,512]{2,1,0:T(1,128)} %broadcast_in_dim.7), calls=%async_computation.1 | async-start | bytes 131072 | tf_op jit(solution)/shard_map/all_to_all | solution.py:520
  (4 other events, 2.6 us)
Sparse Core Ops, SparseCore 0:
  11.1 62.8 all-gather.1
  146.3 34.5 reduce-scatter.1

commit v2 on v1

--- a/solution.py
+++ b/solution.py
@@ -58,6 +58,10 @@
 
 def z_hop(v, d):
     return lax.ppermute(v, "tp", [(z, (z + d) % NZ) for z in range(NZ)])
+
+
+def after(v, other):
+    return lax.optimization_barrier((v, other))[0]
 
 
 def gather_z(own):
@@ -402,17 +406,9 @@
     return local_ref[:, 128 * j : 128 * j + 128] + eo * dot(x_ref[...], state)
 
 
-def tokens_body(
-    pos, w_in, local_ref, x_ref, eo_ref, mine_ref, sib_ref, isc,
-    out, gb_ref, gs_ref, held, buf, in_sems, out_sems,
-):
-    c, z = pos[2], pos[3]
+def tokens_body(pos, w_in, gs_ref, out, held, buf, in_sems, out_sems):
+    z = pos[3]
     wait = fetch_rows(z, w_in, held, in_sems)
-    for j in range(PAIRS):
-        vals = finish(c, 2, local_ref, x_ref, eo_ref, mine_ref, sib_ref, j)
-        at = slice(128 * j, 128 * j + 128)
-        gb_ref[:, at] = vals.astype(bf16)
-        gs_ref[:, at] = (vals * isc[:, at]).astype(bf16)
 
     def back(k):
         return pltpu.make_async_copy(buf.at[k], out.at[lax.rem(z + k, NZ)], out_sems.at[k])
@@ -466,8 +462,14 @@
 
 
 def in_total_body(pos, *refs):
-    gb, keep, send, held, buf, sems, out_sems = refs[9:]
+    local_ref, x_ref, eo_ref, mine_ref, sib_ref, isc, keep, send, gs_ref = refs[9:18]
+    held, buf, sems, out_sems, gb = refs[18:]
     wait = fetch(refs[:9], held, sems, T, T)
+    for j in range(PAIRS):
+        at = slice(128 * j, 128 * j + 128)
+        vals = finish(pos[2], 2, local_ref, x_ref, eo_ref, mine_ref, sib_ref, j)
+        gb[:, at] = vals.astype(bf16)
+        gs_ref[:, at] = (vals * isc[:, at]).astype(bf16)
     store_total(pos, wait, held, gb, keep, send, buf, out_sems)
 
 
@@ -492,8 +494,8 @@
     return total
 
 
-def scatter_seq(c, first, second):
-    pairs = [(keep, swap(send)) for keep, send in (first, second)]
+def scatter_seq(c, first, second, meanwhile):
+    pairs = [(keep, after(swap(send), meanwhile)) for keep, send in (first, second)]
 
     def own(d):
         return jnp.stack([add(keep[d], came[d]) for keep, came in pairs], axis=1).astype(bf16)
@@ -515,9 +517,9 @@
     return whole[0], whole[1]
 
 
-def everyones(part, axis, count):
-    parts = jnp.broadcast_to(part, (count, part.shape[1]))
-    return jnp.sum(lax.all_to_all(parts, axis, 0, 0, tiled=True), axis=0)
+def everyones(part, axis, count, copies):
+    parts = jnp.broadcast_to(part, (count, copies, part.shape[1]))
+    return jnp.sum(lax.all_to_all(parts, axis, 0, 0, tiled=True)[:, 0], axis=0)
 
 
 def slopes_of(weight, step):
@@ -589,29 +591,23 @@
     )
     wide = [pltpu.VMEM((T, W), bf16)]
     sems = [pltpu.SemaphoreType.DMA((NZ,))] * 2
-    parts, gb = call(
-        tokens_body,
-        "token_parts",
-        [sds((NZ, T, W), bf16), sds((T, W), bf16)],
-        (pos, w_in, grad, state_in, down, own, came, scale),
-        MATMUL,
-        wide + [pltpu.VMEM((NZ, W, W), bf16), pltpu.VMEM((NZ, T, W), bf16)] + sems,
-        away=1,
-        out_away=(0,),
-    )
-    grad_tokens = lax.psum_scatter(
-        parts.reshape(NZ * T, W), "tp", scatter_dimension=0, tiled=True
-    )
     held = [
         pltpu.VMEM((NZ, T, W), bf16),
         pltpu.VMEM((NZ, W, W), bf16),
         pltpu.SemaphoreType.DMA((NZ,)),
         pltpu.SemaphoreType.DMA((NZ, 4)),
     ]
-    in_parts = call(
-        in_total_body, "in_parts", TOTALS, (pos, *blocks, gb), MATMUL, held, 9, (0, 1)
-    )
-    out_parts = call(
+    in_keep, in_send, gs = call(
+        in_total_body,
+        "in_parts",
+        TOTALS + [sds((T, W), bf16)],
+        (pos, *blocks, grad, state_in, down, own, came, scale),
+        MATMUL,
+        held + wide,
+        9,
+        (0, 1),
+    )
+    out_keep, out_send = call(
         out_total_body,
         "out_parts",
         TOTALS,
@@ -621,7 +617,20 @@
         9,
         (0, 1),
     )
-    in_total, out_total = scatter_seq(c, in_parts, out_parts)
+    (parts,) = call(
+        tokens_body,
+        "token_parts",
+        [sds((NZ, T, W), bf16)],
+        (pos, w_in, after(gs, out_keep)),
+        MATMUL,
+        [pltpu.VMEM((NZ, W, W), bf16), pltpu.VMEM((NZ, T, W), bf16)] + sems,
+        away=1,
+        out_away=(0,),
+    )
+    grad_tokens = lax.psum_scatter(
+        parts.reshape(NZ * T, W), "tp", scatter_dimension=0, tiled=True
+    )
+    in_total, out_total = scatter_seq(c, (in_keep, in_send), (out_keep, out_send), parts)
     scale_rows = lax.dynamic_slice_in_dim(out_scale, s * R, R)[:, None]
     out_total = out_total / scale_rows
 
@@ -629,8 +638,8 @@
     out_slopes, out_inside = slopes_of(out_weight, scale_rows)
     in_sum = jnp.sum(in_total * in_slopes, axis=0)[None]
     out_sum = jnp.sum(out_total * out_slopes, axis=1)[None]
-    in_sum = everyones(in_sum, "seq", NY * NX * NC)
-    out_sum = everyones(out_sum, "tp", NZ)
+    in_sum = everyones(in_sum, "seq", NY * NX * NC, 8)
+    out_sum = everyones(out_sum, "tp", NZ, 1)
     return (
         grad_tokens,
         in_total * in_inside,

time: 225 us -> 228 us (1.013)
  waiting for transfers between devices: 66 us -> 69.3 us
    all_to_all x1, waiting for transfers between devices: 6.79 us -> 11 us  [everyones(): return jnp.sum(lax.all_to_all(parts, axis, 0, 0, tiled=True)[:, 0], axis=0)]
    ppermute x10, waiting for transfers between devices: 6.4 us -> 2.93 us  [seq_xor(): return lax.ppermute(v, 'seq', [(s, s ^ bits) for s in range(NY * NX * NC)])]
    unnamed x56 -> x54, local copies, waits for them, and re-layouts: 5.58 us -> 5.63 us
  transfers between devices with their start and end apart: 40 -> 40, of which waited for: 21 -> 19; matrix products, arithmetic and copies ran while one was open for 5% -> 4% of each run, Pallas kernels for 7% -> 10%
where the time goes in v2:
time: 228 us; the launch traced here: 227 us
  waiting for transfers between devices  69.3 us (30%)
  starting transfers between devices  65.5 us (29%)
  Pallas kernels  46.5 us (20%)
  between operations  14.5 us (6%)
  blocking collectives  11.9 us (5%)
  other arithmetic  11.6 us (5%)
  local copies, waits for them, and re-layouts  8.06 us (4%)
    pallas_call x11, Pallas kernels, call(): pl.pallas_call(body, out_shape=outs, in_specs=[smem] + [anyw] * away + [v...  46.5 us
    ppermute x13, waiting for transfers between devices, hop(): return lax.ppermute(v, 'seq', pairs)  30 us
    ppermute x8, waiting for transfers between devices, z_hop(): return lax.ppermute(v, 'tp', [(z, (z + d) % NZ) for z in range(NZ)])  17.7 us
    ppermute x13, starting transfers between devices, hop(): return lax.ppermute(v, 'seq', pairs)  16.7 us
    ppermute x10, starting transfers between devices, seq_xor(): return lax.ppermute(v, 'seq', [(s, s ^ bits) for s in range(NY * NX * NC)])  15.7 us
    ppermute x8, starting transfers between devices, z_hop(): return lax.ppermute(v, 'tp', [(z, (z + d) % NZ) for z in range(NZ)])  15.5 us
    all_to_all x1, blocking collectives, everyones(): return jnp.sum(lax.all_to_all(parts, axis, 0, 0, tiled=True)[:, 0], axis=0)  11.9 us
    all_to_all x1, waiting for transfers between devices, everyones(): return jnp.sum(lax.all_to_all(parts, axis, 0, 0, tiled=True)[:, 0], axis=0)  11 us
  transfers between devices with their start and end apart: 40, of which 19 were waited for; matrix products, arithmetic and copies ran while one was open for 4% of the time, Pallas kernels for 10%

profile of v2, /device:TPU:1, one launch (start us, length us, event | category | flops | bytes accessed | tf_op | source)
XLA Modules:
  0.0 227.3 jit_solution(1910720458856240349)
XLA Ops:
  7.9 2.6 %prep.1 = (bf16[512,512]{1,0:T(8,128)(2,1)}, bf16[144,256]{1,0:T(8,128)(2,1)}, bf16[144,256]{1,0:T(8,128)(2,1)}, bf16[128,512]{1,0:T(8,128)(2,1)}, f32[256,8]{1,...) custom-call(s32[4]{0:T(128)} %pad_add_fusion.pos, ...), custom_call_target="tpu_custom_call" | custom-call | flops 1000000 | bytes 2058256 | tf_op jit(solution)/shard_map/prep/pallas_call | solution.py:92
  10.6 2.5 %collective-permute-start.3 = (bf16[512,512]{1,0:T(8,128)(2,1)}, bf16[512,512]{1,0:T(8,128)(2,1)S(1)}, u32[]{:S(2)}, u32[]{:S(2)}) collective-permute-start(bf16[512,512]{1,0:T(8,128)(2,1)} %get-tuple-element.44.refs_0_), channel_id=1, source_target_pairs={{0,1},{1,2},{2,3},{3,4},{4,5},{5,6},{6,7},{7,0},{8,9},{9,10},{10,1... | collective-permute-start | bytes 1572872 | tf_op jit(solution)/shard_map/ppermute | solution.py:60
  13.2 1.0 collective-permute-start.8
  14.1 3.8 %collective-permute-start = (bf16[512,512]{1,0:T(8,128)(2,1)}, bf16[512,512]{1,0:T(8,128)(2,1)S(1)}, u32[]{:S(2)}, u32[]{:S(2)}) collective-permute-start(bf16[512,512]{1,0:T(8,128)(2,1)} %get-tuple-element.44.refs_0_), channel_id=1, source_target_pairs={{0,7},{1,0},{2,1},{3,2},{4,3},{5,4},{6,5},{7,6},{8,15},{9,8},{10,9... | collective-permute-start | bytes 1572872 | tf_op jit(solution)/shard_map/ppermute | solution.py:60
  17.9 0.9 fusion.22
  18.8 2.8 %collective-permute-start.9 = (bf16[2,144,256]{2,1,0:T(8,128)(2,1)S(1)}, bf16[2,144,256]{2,1,0:T(8,128)(2,1)S(1)}, u32[]{:S(2)}, u32[]{:S(2)}) collective-permute-start(bf16[2,144,256]{2,1,0:T(8,128)(2,1)S(1)} %get-tuple-element.103), channel_id=1, source_target_pairs={{0,48},{8,200},{16,0},{24,216},{32,16},{40,232},{48,32},{56,248},{... | collective-permute-start | bytes 442376 | tf_op jit(solution)/shard_map/ppermute | solution.py:39
  22.0 0.7 collective-permute-start.11
  22.7 6.3 %collective-permute-done.3.refs_6_ = bf16[512,512]{1,0:T(8,128)(2,1)S(1)} collective-permute-done((bf16[512,512]{1,0:T(8,128)(2,1)}, bf16[512,512]{1,0:T(8,128)(2,1)S(1)}, u32[]{:S(2)}, u32[]{:S(2)}) %collective-permute-start.3) | collective-permute-done | bytes 524320 | tf_op jit(solution)/shard_map/ppermute | solution.py:60
  29.1 2.6 %collective-permute-start.12 = (bf16[4,2,144,256]{3,2,1,0:T(8,128)(2,1)S(1)}, bf16[4,2,144,256]{3,2,1,0:T(8,128)(2,1)S(1)}, u32[]{:S(2)}, u32[]{:S(2)}) collective-permute-start(bf16[4,2,144,256]{3,2,1,0:T(8,128)(2,1)S(1)} %pad_maximum_fusion.refs_0_), channel_id=1, source_target_pairs={{0,192},{8,56},{16,208},{24,8},{32,224},{40,24},{48,240},{56,40},{... | collective-permute-start | bytes 1769480 | tf_op jit(solution)/shard_map/ppermute | solution.py:39
  31.7 2.7 %collective-permute-start.1 = (bf16[512,512]{1,0:T(8,128)(2,1)S(1)}, bf16[512,512]{1,0:T(8,128)(2,1)S(1)}, u32[]{:S(2)}, u32[]{:S(2)}) collective-permute-start(bf16[512,512]{1,0:T(8,128)(2,1)S(1)} %collective-permute-done.refs_1_), channel_id=1, source_target_pairs={{0,7},{1,0},{2,1},{3,2},{4,3},{5,4},{6,5},{7,6},{8,15},{9,8},{10,9... | collective-permute-start | bytes 1572872 | tf_op jit(solution)/shard_map/ppermute | solution.py:60
  34.3 1.2 collective-permute-start.13
  35.9 6.6 %collective-permute-done.4.refs_5_ = bf16[512,512]{1,0:T(8,128)(2,1)S(1)} collective-permute-done((bf16[512,512]{1,0:T(8,128)(2,1)S(1)}, bf16[512,512]{1,0:T(8,128)(2,1)S(1)}, u32[]{:S(2)}, u32[]{:S(2)}) %collective-permute-start.4) | collective-permute-done | bytes 524320 | tf_op jit(solution)/shard_map/ppermute | solution.py:60
  42.5 3.7 %collective-permute-done.12.refs_1_ = bf16[4,2,144,256]{3,2,1,0:T(8,128)(2,1)S(1)} collective-permute-done((bf16[4,2,144,256]{3,2,1,0:T(8,128)(2,1)S(1)}, bf16[4,2,144,256]{3,2,1,0:T(8,128)(2,1)S(1)}, u32[]{:S(2)}, u32[]{:S(2)}) %collective-permute-start.12) | collective-permute-done | bytes 589856 | tf_op jit(solution)/shard_map/ppermute | solution.py:39
  46.2 1.7 collective-permute-start.15
  47.9 3.0 %collective-permute-start.2 = (bf16[512,512]{1,0:T(8,128)(2,1)S(1)}, bf16[512,512]{1,0:T(8,128)(2,1)S(1)}, u32[]{:S(2)}, u32[]{:S(2)}) collective-permute-start(bf16[512,512]{1,0:T(8,128)(2,1)S(1)} %collective-permute-done.1.refs_2_), channel_id=1, source_target_pairs={{0,7},{1,0},{2,1},{3,2},{4,3},{5,4},{6,5},{7,6},{8,15},{9,8},{10,9... | collective-permute-start | bytes 1572872 | tf_op jit(solution)/shard_map/ppermute | solution.py:60
  51.6 2.8 %collective-permute-start.17 = (bf16[4,2,144,256]{3,2,1,0:T(8,128)(2,1)S(1)}, bf16[4,2,144,256]{3,2,1,0:T(8,128)(2,1)S(1)}, u32[]{:S(2)}, u32[]{:S(2)}) collective-permute-start(bf16[4,2,144,256]{3,2,1,0:T(8,128)(2,1)S(1)} %collective-permute-done.13.refs_2_), channel_id=1, source_target_pairs={{0,8},{8,0},{16,24},{24,16},{32,40},{40,32},{48,56},{56,48},{64,72... | collective-permute-start | bytes 1769480 | tf_op jit(solution)/shard_map/ppermute | solution.py:52
  54.4 0.7 collective-permute-done.5.refs_4_
  55.1 3.0 %collective-permute-start.18 = (bf16[4,2,144,256]{3,2,1,0:T(8,128)(2,1)S(1)}, bf16[4,2,144,256]{3,2,1,0:T(8,128)(2,1)}, u32[]{:S(2)}, u32[]{:S(2)}) collective-permute-start(bf16[4,2,144,256]{3,2,1,0:T(8,128)(2,1)S(1)} %collective-permute-done.14.refs_3_), channel_id=1, source_target_pairs={{0,8},{8,0},{16,24},{24,16},{32,40},{40,32},{48,56},{56,48},{64,72... | collective-permute-start | bytes 1769480 | tf_op jit(solution)/shard_map/ppermute | solution.py:52
  58.1 4.1 %collective-permute-done.2.refs_3_ = bf16[512,512]{1,0:T(8,128)(2,1)S(1)} collective-permute-done((bf16[512,512]{1,0:T(8,128)(2,1)S(1)}, bf16[512,512]{1,0:T(8,128)(2,1)S(1)}, u32[]{:S(2)}, u32[]{:S(2)}) %collective-permute-start.2) | collective-permute-done | bytes 524320 | tf_op jit(solution)/shard_map/ppermute | solution.py:60
  62.4 3.3 %collective-permute-start.7 = (bf16[256,512]{1,0:T(8,128)(2,1)S(1)}, bf16[256,512]{1,0:T(8,128)(2,1)}, u32[]{:S(2)}, u32[]{:S(2)}) collective-permute-start(bf16[256,512]{1,0:T(8,128)(2,1)S(1)} %slice.120), channel_id=1, source_target_pairs={{0,7},{1,0},{2,1},{3,2},{4,3},{5,4},{6,5},{7,6},{8,15},{9,8},{10,9... | collective-permute-start | bytes 786440 | tf_op jit(solution)/shard_map/ppermute | solution.py:60
  65.8 0.8 copy-done.14
  66.8 5.3 %assemble.1 = (bf16[4096,512]{1,0:T(8,128)(2,1)}, f32[24,256]{1,0:T(8,128)}) custom-call(s32[4]{0:T(128)} %pad_add_fusion.pos, bf16[4,2,144,256]{3,2,1,0:T(8,128)(2,1)} %copy-done.6, bf16[4,2,144,256]{3,2,1,0:T(8,128)(2,1)} %copy-done.10, bf16[4,2,144,256]{3,2,1,0:T(8,128)(2,1)} %copy-done.11, bf16[4,2,144,256]{3,2,1,0:T(8,128)(2,1)} %copy-done.12, ...), custom_call_target="tpu_custom_call" | custom-call | flops 1000000 | bytes 8937488 | tf_op jit(solution)/shard_map/assemble/pallas_call | solution.py:92
  72.1 1.9 all-gather.2.cloned.1.call-done.refs_10_.w_in
  74.0 9.4 %project.1 = (bf16[256,512]{1,0:T(8,128)(2,1)}, bf16[256,512]{1,0:T(8,128)(2,1)}, bf16[4,128,128]{2,1,0:T(8,128)(2,1)}, bf16[4,128,128]{2,1,0:T(8,128)(2,1)}) custom-call(s32[4]{0:T(128)} %pad_add_fusion.pos, bf16[512,512]{1,0:T(8,128)(2,1)} %get-tuple-element.44.refs_0_, bf16[512,512]{1,0:T(8,128)(2,1)} %copy-done.3, bf16[512,512]{1,0:T(8,128)(2,1)} %copy-done.5, ...), custom_call_target="tpu_custom_call" | custom-call | flops 2147483648 | bytes 13649936 | tf_op jit(solution)/shard_map/project/pallas_call | solution.py:92
  83.7 1.3 collective-permute-done.19.other
  85.7 1.7 join_chip.1.q
  87.4 0.9 collective-permute-start.20
  88.3 2.4 %collective-permute-start.21 = (bf16[4,128,128]{2,1,0:T(8,128)(2,1)}, bf16[4,128,128]{2,1,0:T(8,128)(2,1)S(1)}, u32[]{:S(2)}, u32[]{:S(2)}) collective-permute-start(bf16[4,128,128]{2,1,0:T(8,128)(2,1)} %join_chip.1.q), channel_id=1, source_target_pairs={{0,32},{8,40},{16,48},{24,56},{32,0},{40,8},{48,16},{56,24},{64,96... | collective-permute-start | bytes 393224 | tf_op jit(solution)/shard_map/ppermute | solution.py:48
  90.6 1.0 collective-permute-start.22
  91.7 2.5 %grad_local.1.refs_9_ = f32[256,512]{1,0:T(8,128)} custom-call(s32[4]{0:T(128)} %pad_add_fusion.pos, bf16[256,512]{1,0:T(8,128)(2,1)} %get-tuple-element.55.vals, bf16[256,128]{1,0:T(8,128)(2,1)} %refs_10_.2, bf16[256,128]{1,0:T(8,128)(2,1)} %refs_10_.3, f32[256,8]{1,0:T(8,128)} %get-tuple-element.56.a_ref, f32[8,256]{1,0:T(8,128)} %get-tuple-element.57.at_ref), custom_call_target="tpu_custom_call" | custom-call | flops 1000000000 | bytes 933904 | tf_op jit(solution)/shard_map/grad_local/pallas_call | solution.py:92
  94.2 2.8 %collective-permute-done.21.g2 = bf16[4,128,128]{2,1,0:T(8,128)(2,1)S(1)} collective-permute-done((bf16[4,128,128]{2,1,0:T(8,128)(2,1)}, bf16[4,128,128]{2,1,0:T(8,128)(2,1)S(1)}, u32[]{:S(2)}, u32[]{:S(2)}) %collective-permute-start.21) | collective-permute-done | bytes 131104 | tf_op jit(solution)/shard_map/ppermute | solution.py:48
  97.7 0.7 copy-done.25
  98.3 2.0 join_row.1
  100.4 4.3 %collective-permute-start.24 = (bf16[4,128,128]{2,1,0:T(8,128)(2,1)}, bf16[4,128,128]{2,1,0:T(8,128)(2,1)S(1)}, u32[]{:S(2)}, u32[]{:S(2)}) collective-permute-start(bf16[4,128,128]{2,1,0:T(8,128)(2,1)} %get-tuple-element.64), channel_id=1, source_target_pairs={{0,128},{8,136},{16,144},{24,152},{32,160},{40,168},{48,176},{56,1... | collective-permute-start | bytes 393224 | tf_op jit(solution)/shard_map/ppermute | solution.py:48
  104.7 2.5 %mixed_local.1.refs_9_ = f32[256,512]{1,0:T(8,128)} custom-call(s32[4]{0:T(128)} %pad_add_fusion.pos, bf16[256,512]{1,0:T(8,128)(2,1)} %get-tuple-element.65.vals, bf16[256,128]{1,0:T(8,128)(2,1)} %refs_10_.2, bf16[256,128]{1,0:T(8,128)(2,1)} %refs_10_.3, f32[256,8]{1,0:T(8,128)} %get-tuple-element.56.a_ref, f32[8,256]{1,0:T(8,128)} %get-tuple-element.57.at_ref), custom_call_target="tpu_custom_call" | custom-call | flops 1000000000 | bytes 933904 | tf_op jit(solution)/shard_map/mixed_local/pallas_call | solution.py:92
  107.2 2.5 %collective-permute-done.24.g2 = bf16[4,128,128]{2,1,0:T(8,128)(2,1)S(1)} collective-permute-done((bf16[4,128,128]{2,1,0:T(8,128)(2,1)}, bf16[4,128,128]{2,1,0:T(8,128)(2,1)S(1)}, u32[]{:S(2)}, u32[]{:S(2)}) %collective-permute-start.24) | collective-permute-done | bytes 131104 | tf_op jit(solution)/shard_map/ppermute | solution.py:48
  110.7 2.1 join_rows.1
  112.8 2.1 collective-permute-start.26
  114.9 1.2 collective-permute-done.26.refs_13_
  116.8 6.0 %out_parts.1 = (bf16[4,4,256,256]{3,2,1,0:T(8,128)(2,1)}, bf16[4,4,256,256]{3,2,1,0:T(8,128)(2,1)}) custom-call(s32[4]{0:T(128)} %pad_add_fusion.pos, bf16[512,512]{1,0:T(8,128)(2,1)} %get-tuple-element.44.refs_0_, bf16[512,512]{1,0:T(8,128)(2,1)} %copy-done.3, bf16[512,512]{1,0:T(8,128)(2,1)} %copy-done.5, bf16[512,512]{1,0:T(8,128)(2,1)} %copy-done.1, ...), custom_call_target="tpu_custom_call" | custom-call | flops 1073741824 | bytes 9248784 | tf_op jit(solution)/shard_map/out_parts/pallas_call | solution.py:92
  122.7 0.7 collective-permute-start.28
  123.4 6.7 %in_parts.1 = (bf16[4,4,256,256]{3,2,1,0:T(8,128)(2,1)}, bf16[4,4,256,256]{3,2,1,0:T(8,128)(2,1)}, bf16[256,512]{1,0:T(8,128)(2,1)}) custom-call(s32[4]{0:T(128)} %pad_add_fusion.pos, bf16[512,512]{1,0:T(8,128)(2,1)} %get-tuple-element.44.refs_0_, bf16[512,512]{1,0:T(8,128)(2,1)} %copy-done.3, bf16[512,512]{1,0:T(8,128)(2,1)} %copy-done.5, ...), custom_call_target="tpu_custom_call" | custom-call | flops 1073741824 | bytes 9512976 | tf_op jit(solution)/shard_map/in_parts/pallas_call | solution.py:92
  130.3 5.7 %token_parts.1 = bf16[8,256,512]{2,1,0:T(8,128)(2,1)} custom-call(s32[4]{0:T(128)} %pad_add_fusion.pos, bf16[4096,512]{1,0:T(8,128)(2,1)} %all-gather.2.cloned.1.call-done.refs_10_.w_in, bf16[256,512]{1,0:T(8,128)(2,1)} %get-tuple-element.75.gs_ref), custom_call_target="tpu_custom_call" | custom-call | flops 1073741824 | bytes 6553616 | tf_op jit(solution)/shard_map/token_parts/pallas_call | solution.py:92
  136.1 1.4 copy-done.9
  137.4 2.8 %fusion = (bf16[4,1,256,256]{3,2,0,1:T(8,128)(2,1)S(1)}, bf16[4,1,256,256]{3,2,0,1:T(8,128)(2,1)S(1)}, bf16[4,1,256,256]{3,2,0,1:T(8,128)(2,1)S(1)}, bf16[4,1,25...) fusion(bf16[4,4,256,256]{3,2,1,0:T(8,128)(2,1)} %copy-done.9, ...), kind=kLoop, calls=%fused_computation.14 | loop fusion | flops 8388608 | bytes 12582912 | tf_op jit(solution)/shard_map/add | solution.py:493
  140.2 1.1 fusion.8
  141.3 2.7 %collective-permute-start.31 = (bf16[2,2,256,256]{3,2,0,1:T(8,128)(2,1)}, bf16[2,2,256,256]{3,2,0,1:T(8,128)(2,1)}, u32[]{:S(2)}, u32[]{:S(2)}) collective-permute-start(bf16[2,2,256,256]{3,2,0,1:T(8,128)(2,1)} %get-tuple-element.97), channel_id=1, source_target_pairs={{0,48},{8,200},{16,0},{24,216},{32,16},{40,232},{48,32},{56,248},{... | collective-permute-start | bytes 1572872 | tf_op jit(solution)/shard_map/ppermute | solution.py:39
  144.0 7.2 %collective-permute-done.29 = bf16[2,2,256,256]{3,2,0,1:T(8,128)(2,1)} collective-permute-done((bf16[2,2,256,256]{3,2,0,1:T(8,128)(2,1)}, bf16[2,2,256,256]{3,2,0,1:T(8,128)(2,1)}, u32[]{:S(2)}, u32[]{:S(2)}) %collective-permute-start.29) | collective-permute-done | bytes 524320 | tf_op jit(solution)/shard_map/ppermute | solution.py:39
  151.2 1.2 add_convert_fusion.1
  152.5 1.2 add_convert_fusion
  153.6 2.7 %collective-permute-start.32 = (bf16[4,2,256,256]{3,2,0,1:T(8,128)(2,1)S(1)}, bf16[4,2,256,256]{3,2,0,1:T(8,128)(2,1)S(1)}, u32[]{:S(2)}, u32[]{:S(2)}) collective-permute-start(bf16[4,2,256,256]{3,2,0,1:T(8,128)(2,1)S(1)} %add_convert_fusion), channel_id=1, source_target_pairs={{0,48},{8,200},{16,0},{24,216},{32,16},{40,232},{48,32},{56,248},{... | collective-permute-start | bytes 3145736 | tf_op jit(solution)/shard_map/ppermute | solution.py:39
  156.4 11.3 %collective-permute-done.30 = bf16[4,2,256,256]{3,2,0,1:T(8,128)(2,1)S(1)} collective-permute-done((bf16[4,2,256,256]{3,2,0,1:T(8,128)(2,1)S(1)}, bf16[4,2,256,256]{3,2,0,1:T(8,128)(2,1)S(1)}, u32[]{:S(2)}, u32[]{:S(2)}) %collective-permute-start.30) | collective-permute-done | bytes 1048608 | tf_op jit(solution)/shard_map/ppermute | solution.py:39
  168.6 0.8 slice_bitcast_fusion.3
  169.4 2.5 %collective-permute-start.34 = (bf16[2,256,256]{2,1,0:T(8,128)(2,1)S(1)}, bf16[2,256,256]{2,1,0:T(8,128)(2,1)S(1)}, u32[]{:S(2)}, u32[]{:S(2)}) collective-permute-start(bf16[2,256,256]{2,1,0:T(8,128)(2,1)S(1)} %get-tuple-element.95), channel_id=1, source_target_pairs={{0,128},{8,40},{16,144},{24,56},{32,160},{40,8},{48,176},{56,24},{... | collective-permute-start | bytes 786440 | tf_op jit(solution)/shard_map/ppermute | solution.py:39
  171.9 0.7 collective-permute-start.35
  172.6 6.6 %collective-permute-done.33 = bf16[2,256,256]{2,1,0:T(8,128)(2,1)S(1)} collective-permute-done((bf16[2,256,256]{2,1,0:T(8,128)(2,1)}, bf16[2,256,256]{2,1,0:T(8,128)(2,1)S(1)}, u32[]{:S(2)}, u32[]{:S(2)}) %collective-permute-start.33) | collective-permute-done | bytes 262176 | tf_op jit(solution)/shard_map/ppermute | solution.py:39
  179.6 1.1 fusion.11
  180.7 3.6 %collective-permute-start.36 = (f32[2,128,256]{2,1,0:T(8,128)S(1)}, f32[2,128,256]{2,1,0:T(8,128)S(1)}, u32[]{:S(2)}, u32[]{:S(2)}) collective-permute-start(f32[2,128,256]{2,1,0:T(8,128)S(1)} %slice_select_fusion), channel_id=1, source_target_pairs={{0,8},{8,0},{16,24},{24,16},{32,40},{40,32},{48,56},{56,48},{64,72... | collective-permute-start | bytes 786440 | tf_op jit(solution)/shard_map/ppermute | solution.py:52
  184.3 0.8 dynamic_slice.3
  185.6 1.0 fusion.15
  186.6 11.9 %all_to_all.10 = f32[8,1,128]{2,1,0:T(1,128)S(1)} all-to-all(f32[8,1,128]{2,1,0:T(1,128)S(1)} %broadcast_in_dim.16), channel_id=1, replica_groups=mesh['seq'=32,'tp'=8] {'tp'}, dimensions={0} | all-to-all | bytes 8192 | tf_op jit(solution)/shard_map/all_to_all | solution.py:522
  198.5 0.9 broadcast_in_dim.7
  199.3 8.9 %all-to-all-start = ((f32[32,8,512]{2,1,0:T(8,128)}), f32[32,8,512]{2,1,0:T(8,128)S(1)}, u32[]{:S(2)}, u32[]{:S(2)}) async-start(f32[32,8,512]{2,1,0:T(8,128)} %broadcast_in_dim.7), calls=%async_computation.1 | async-start | bytes 1048576 | tf_op jit(solution)/shard_map/all_to_all | solution.py:522
  208.8 11.0 %all-to-all-done = f32[32,8,512]{2,1,0:T(8,128)S(1)} async-done(((f32[32,8,512]{2,1,0:T(8,128)}), f32[32,8,512]{2,1,0:T(8,128)S(1)}, u32[]{:S(2)}, u32[]{:S(2)}) %all-to-all-start) | async-done | bytes 524320 | tf_op jit(solution)/shard_map/all_to_all | solution.py:522
  (106 shorter events, 9.4 us)
Async XLA Ops:
  7.2 66.8 %all-gather.2.cloned.1.call-start = ((), (), s32[]{:S(2)}) async-start(), calls=%async_computation.3 | async-start | bytes 4325376 | tf_op jit(solution)/shard_map/all_gather | solution.py:553
  10.6 209.9 %reduce-scatter.2.cloned.1.call-start = ((), (), s32[]{:S(2)}) async-start(), calls=%async_computation.4 | async-start | bytes 2359296 | tf_op jit(solution)/shard_map/reduce_scatter | solution.py:630
  10.6 18.3 %collective-permute-start.3 = (bf16[512,512]{1,0:T(8,128)(2,1)}, bf16[512,512]{1,0:T(8,128)(2,1)S(1)}, u32[]{:S(2)}, u32[]{:S(2)}) collective-permute-start(bf16[512,512]{1,0:T(8,128)(2,1)} %get-tuple-element.44.refs_0_), channel_id=1, source_target_pairs={{0,1},{1,2},{2,3},{3,4},{4,5},{5,6},{6,7},{7,0},{8,9},{9,10},{10,1... | collective-permute-start | bytes 1572872 | tf_op jit(solution)/shard_map/ppermute | solution.py:60
  13.2 4.7 %collective-permute-start.8 = (bf16[144,256]{1,0:T(8,128)(2,1)}, bf16[144,256]{1,0:T(8,128)(2,1)S(1)}, u32[]{:S(2)}, u32[]{:S(2)}) collective-permute-start(bf16[144,256]{1,0:T(8,128)(2,1)} %get-tuple-element.46), channel_id=1, source_target_pairs={{0,8},{8,0},{16,24},{24,16},{32,40},{40,32},{48,56},{56,48},{64,72... | collective-permute-start | bytes 221192 | tf_op jit(solution)/shard_map/ppermute | solution.py:52
  14.1 17.5 %collective-permute-start = (bf16[512,512]{1,0:T(8,128)(2,1)}, bf16[512,512]{1,0:T(8,128)(2,1)S(1)}, u32[]{:S(2)}, u32[]{:S(2)}) collective-permute-start(bf16[512,512]{1,0:T(8,128)(2,1)} %get-tuple-element.44.refs_0_), channel_id=1, source_target_pairs={{0,7},{1,0},{2,1},{3,2},{4,3},{5,4},{6,5},{7,6},{8,15},{9,8},{10,9... | collective-permute-start | bytes 1572872 | tf_op jit(solution)/shard_map/ppermute | solution.py:60
  18.8 10.2 %collective-permute-start.9 = (bf16[2,144,256]{2,1,0:T(8,128)(2,1)S(1)}, bf16[2,144,256]{2,1,0:T(8,128)(2,1)S(1)}, u32[]{:S(2)}, u32[]{:S(2)}) collective-permute-start(bf16[2,144,256]{2,1,0:T(8,128)(2,1)S(1)} %get-tuple-element.103), channel_id=1, source_target_pairs={{0,48},{8,200},{16,0},{24,216},{32,16},{40,232},{48,32},{56,248},{... | collective-permute-start | bytes 442376 | tf_op jit(solution)/shard_map/ppermute | solution.py:39
  21.6 7.4 %collective-permute-start.10 = (bf16[2,144,256]{2,1,0:T(8,128)(2,1)S(1)}, bf16[2,144,256]{2,1,0:T(8,128)(2,1)S(1)}, u32[]{:S(2)}, u32[]{:S(2)}) collective-permute-start(bf16[2,144,256]{2,1,0:T(8,128)(2,1)S(1)} %get-tuple-element.103), channel_id=1, source_target_pairs={{0,32},{8,136},{16,48},{24,152},{32,0},{40,168},{48,16},{56,184},{... | collective-permute-start | bytes 442376 | tf_op jit(solution)/shard_map/ppermute | solution.py:39
  22.0 7.0 %collective-permute-start.11 = (bf16[2,144,256]{2,1,0:T(8,128)(2,1)S(1)}, bf16[2,144,256]{2,1,0:T(8,128)(2,1)S(1)}, u32[]{:S(2)}, u32[]{:S(2)}) collective-permute-start(bf16[2,144,256]{2,1,0:T(8,128)(2,1)S(1)} %get-tuple-element.103), channel_id=1, source_target_pairs={{0,16},{8,72},{16,32},{24,88},{32,48},{40,104},{48,0},{56,120},{64... | collective-permute-start | bytes 442376 | tf_op jit(solution)/shard_map/ppermute | solution.py:39
  29.0 43.1 %copy-start.2 = (bf16[512,512]{1,0:T(8,128)(2,1)}, bf16[512,512]{1,0:T(8,128)(2,1)S(1)}, u32[]{:S(2)}) copy-start(bf16[512,512]{1,0:T(8,128)(2,1)S(1)} %collective-permute-done.3.refs_6_) | copy-start | bytes 1572868
  29.0 13.5 %collective-permute-start.4 = (bf16[512,512]{1,0:T(8,128)(2,1)S(1)}, bf16[512,512]{1,0:T(8,128)(2,1)S(1)}, u32[]{:S(2)}, u32[]{:S(2)}) collective-permute-start(bf16[512,512]{1,0:T(8,128)(2,1)S(1)} %collective-permute-done.3.refs_6_), channel_id=1, source_target_pairs={{0,1},{1,2},{2,3},{3,4},{4,5},{5,6},{6,7},{7,0},{8,9},{9,10},{10,1... | collective-permute-start | bytes 1572872 | tf_op jit(solution)/shard_map/ppermute | solution.py:60
  29.1 36.7 %copy-start.6 = (bf16[4,2,144,256]{3,2,1,0:T(8,128)(2,1)}, bf16[4,2,144,256]{3,2,1,0:T(8,128)(2,1)S(1)}, u32[]{:S(2)}) copy-start(bf16[4,2,144,256]{3,2,1,0:T(8,128)(2,1)S(1)} %pad_maximum_fusion.refs_0_) | copy-start | bytes 1769476
  29.1 17.1 %collective-permute-start.12 = (bf16[4,2,144,256]{3,2,1,0:T(8,128)(2,1)S(1)}, bf16[4,2,144,256]{3,2,1,0:T(8,128)(2,1)S(1)}, u32[]{:S(2)}, u32[]{:S(2)}) collective-permute-start(bf16[4,2,144,256]{3,2,1,0:T(8,128)(2,1)S(1)} %pad_maximum_fusion.refs_0_), channel_id=1, source_target_pairs={{0,192},{8,56},{16,208},{24,8},{32,224},{40,24},{48,240},{56,40},{... | collective-permute-start | bytes 1769480 | tf_op jit(solution)/shard_map/ppermute | solution.py:39
  31.7 40.4 %copy-start.3 = (bf16[512,512]{1,0:T(8,128)(2,1)}, bf16[512,512]{1,0:T(8,128)(2,1)S(1)}, u32[]{:S(2)}) copy-start(bf16[512,512]{1,0:T(8,128)(2,1)S(1)} %collective-permute-done.refs_1_) | copy-start | bytes 1572868
  31.7 16.2 %collective-permute-start.1 = (bf16[512,512]{1,0:T(8,128)(2,1)S(1)}, bf16[512,512]{1,0:T(8,128)(2,1)S(1)}, u32[]{:S(2)}, u32[]{:S(2)}) collective-permute-start(bf16[512,512]{1,0:T(8,128)(2,1)S(1)} %collective-permute-done.refs_1_), channel_id=1, source_target_pairs={{0,7},{1,0},{2,1},{3,2},{4,3},{5,4},{6,5},{7,6},{8,15},{9,8},{10,9... | collective-permute-start | bytes 1572872 | tf_op jit(solution)/shard_map/ppermute | solution.py:60
  34.3 16.5 %collective-permute-start.13 = (bf16[4,2,144,256]{3,2,1,0:T(8,128)(2,1)S(1)}, bf16[4,2,144,256]{3,2,1,0:T(8,128)(2,1)S(1)}, u32[]{:S(2)}, u32[]{:S(2)}) collective-permute-start(bf16[4,2,144,256]{3,2,1,0:T(8,128)(2,1)S(1)} %pad_maximum_fusion.refs_0_), channel_id=1, source_target_pairs={{0,128},{8,40},{16,144},{24,56},{32,160},{40,8},{48,176},{56,24},{... | collective-permute-start | bytes 1769480 | tf_op jit(solution)/shard_map/ppermute | solution.py:39
  35.5 16.0 %collective-permute-start.14 = (bf16[4,2,144,256]{3,2,1,0:T(8,128)(2,1)S(1)}, bf16[4,2,144,256]{3,2,1,0:T(8,128)(2,1)S(1)}, u32[]{:S(2)}, u32[]{:S(2)}) collective-permute-start(bf16[4,2,144,256]{3,2,1,0:T(8,128)(2,1)S(1)} %pad_maximum_fusion.refs_0_), channel_id=1, source_target_pairs={{0,64},{8,24},{16,80},{24,40},{32,96},{40,56},{48,112},{56,8},{64,... | collective-permute-start | bytes 1769480 | tf_op jit(solution)/shard_map/ppermute | solution.py:39
  42.5 29.6 %copy-start.4 = (bf16[512,512]{1,0:T(8,128)(2,1)}, bf16[512,512]{1,0:T(8,128)(2,1)S(1)}, u32[]{:S(2)}) copy-start(bf16[512,512]{1,0:T(8,128)(2,1)S(1)} %collective-permute-done.4.refs_5_) | copy-start | bytes 1572868
  42.5 12.6 %collective-permute-start.5 = (bf16[512,512]{1,0:T(8,128)(2,1)S(1)}, bf16[512,512]{1,0:T(8,128)(2,1)S(1)}, u32[]{:S(2)}, u32[]{:S(2)}) collective-permute-start(bf16[512,512]{1,0:T(8,128)(2,1)S(1)} %collective-permute-done.4.refs_5_), channel_id=1, source_target_pairs={{0,1},{1,2},{2,3},{3,4},{4,5},{5,6},{6,7},{7,0},{8,9},{9,10},{10,1... | collective-permute-start | bytes 1572872 | tf_op jit(solution)/shard_map/ppermute | solution.py:60
  46.2 19.6 %copy-start.10 = (bf16[4,2,144,256]{3,2,1,0:T(8,128)(2,1)}, bf16[4,2,144,256]{3,2,1,0:T(8,128)(2,1)S(1)}, u32[]{:S(2)}) copy-start(bf16[4,2,144,256]{3,2,1,0:T(8,128)(2,1)S(1)} %collective-permute-done.12.refs_1_) | copy-start | bytes 1769476
  46.2 16.2 %collective-permute-start.15 = (bf16[4,2,144,256]{3,2,1,0:T(8,128)(2,1)S(1)}, bf16[4,2,144,256]{3,2,1,0:T(8,128)(2,1)S(1)}, u32[]{:S(2)}, u32[]{:S(2)}) collective-permute-start(bf16[4,2,144,256]{3,2,1,0:T(8,128)(2,1)S(1)} %pad_maximum_fusion.refs_0_), channel_id=1, source_target_pairs={{0,8},{8,0},{16,24},{24,16},{32,40},{40,32},{48,56},{56,48},{64,72... | collective-permute-start | bytes 1769480 | tf_op jit(solution)/shard_map/ppermute | solution.py:52
  47.9 24.2 %copy-start.5 = (bf16[512,512]{1,0:T(8,128)(2,1)}, bf16[512,512]{1,0:T(8,128)(2,1)S(1)}, u32[]{:S(2)}) copy-start(bf16[512,512]{1,0:T(8,128)(2,1)S(1)} %collective-permute-done.1.refs_2_) | copy-start | bytes 1572868
  47.9 14.2 %collective-permute-start.2 = (bf16[512,512]{1,0:T(8,128)(2,1)S(1)}, bf16[512,512]{1,0:T(8,128)(2,1)S(1)}, u32[]{:S(2)}, u32[]{:S(2)}) collective-permute-start(bf16[512,512]{1,0:T(8,128)(2,1)S(1)} %collective-permute-done.1.refs_2_), channel_id=1, source_target_pairs={{0,7},{1,0},{2,1},{3,2},{4,3},{5,4},{6,5},{7,6},{8,15},{9,8},{10,9... | collective-permute-start | bytes 1572872 | tf_op jit(solution)/shard_map/ppermute | solution.py:60
  50.8 15.0 %copy-start.11 = (bf16[4,2,144,256]{3,2,1,0:T(8,128)(2,1)}, bf16[4,2,144,256]{3,2,1,0:T(8,128)(2,1)S(1)}, u32[]{:S(2)}) copy-start(bf16[4,2,144,256]{3,2,1,0:T(8,128)(2,1)S(1)} %collective-permute-done.13.refs_2_) | copy-start | bytes 1769476
  50.8 14.9 %collective-permute-start.16 = (bf16[4,2,144,256]{3,2,1,0:T(8,128)(2,1)S(1)}, bf16[4,2,144,256]{3,2,1,0:T(8,128)(2,1)S(1)}, u32[]{:S(2)}, u32[]{:S(2)}) collective-permute-start(bf16[4,2,144,256]{3,2,1,0:T(8,128)(2,1)S(1)} %collective-permute-done.12.refs_1_), channel_id=1, source_target_pairs={{0,8},{8,0},{16,24},{24,16},{32,40},{40,32},{48,56},{56,48},{64,72... | collective-permute-start | bytes 1769480 | tf_op jit(solution)/shard_map/ppermute | solution.py:52
  51.6 14.3 %copy-start.12 = (bf16[4,2,144,256]{3,2,1,0:T(8,128)(2,1)}, bf16[4,2,144,256]{3,2,1,0:T(8,128)(2,1)S(1)}, u32[]{:S(2)}) copy-start(bf16[4,2,144,256]{3,2,1,0:T(8,128)(2,1)S(1)} %collective-permute-done.14.refs_3_) | copy-start | bytes 1769476
  51.6 14.2 %collective-permute-start.17 = (bf16[4,2,144,256]{3,2,1,0:T(8,128)(2,1)S(1)}, bf16[4,2,144,256]{3,2,1,0:T(8,128)(2,1)S(1)}, u32[]{:S(2)}, u32[]{:S(2)}) collective-permute-start(bf16[4,2,144,256]{3,2,1,0:T(8,128)(2,1)S(1)} %collective-permute-done.13.refs_2_), channel_id=1, source_target_pairs={{0,8},{8,0},{16,24},{24,16},{32,40},{40,32},{48,56},{56,48},{64,72... | collective-permute-start | bytes 1769480 | tf_op jit(solution)/shard_map/ppermute | solution.py:52
  55.1 17.0 %copy-start = (bf16[512,512]{1,0:T(8,128)(2,1)}, bf16[512,512]{1,0:T(8,128)(2,1)S(1)}, u32[]{:S(2)}) copy-start(bf16[512,512]{1,0:T(8,128)(2,1)S(1)} %collective-permute-done.5.refs_4_) | copy-start | bytes 1572868
  55.1 10.7 %collective-permute-start.18 = (bf16[4,2,144,256]{3,2,1,0:T(8,128)(2,1)S(1)}, bf16[4,2,144,256]{3,2,1,0:T(8,128)(2,1)}, u32[]{:S(2)}, u32[]{:S(2)}) collective-permute-start(bf16[4,2,144,256]{3,2,1,0:T(8,128)(2,1)S(1)} %collective-permute-done.14.refs_3_), channel_id=1, source_target_pairs={{0,8},{8,0},{16,24},{24,16},{32,40},{40,32},{48,56},{56,48},{64,72... | collective-permute-start | bytes 1769480 | tf_op jit(solution)/shard_map/ppermute | solution.py:52
  62.1 10.0 %copy-start.1 = (bf16[512,512]{1,0:T(8,128)(2,1)}, bf16[512,512]{1,0:T(8,128)(2,1)S(1)}, u32[]{:S(2)}) copy-start(bf16[512,512]{1,0:T(8,128)(2,1)S(1)} %collective-permute-done.2.refs_3_) | copy-start | bytes 1572868
  62.1 10.0 %collective-permute-start.6 = (bf16[256,512]{1,0:T(8,128)(2,1)S(1)}, bf16[256,512]{1,0:T(8,128)(2,1)S(1)}, u32[]{:S(2)}, u32[]{:S(2)}) collective-permute-start(bf16[256,512]{1,0:T(8,128)(2,1)S(1)} %slice.119), channel_id=1, source_target_pairs={{0,1},{1,2},{2,3},{3,4},{4,5},{5,6},{6,7},{7,0},{8,9},{9,10},{10,1... | collective-permute-start | bytes 786440 | tf_op jit(solution)/shard_map/ppermute | solution.py:60
  62.4 3.4 %copy-start.13 = (bf16[4,2,144,256]{3,2,1,0:T(8,128)(2,1)}, bf16[4,2,144,256]{3,2,1,0:T(8,128)(2,1)S(1)}, u32[]{:S(2)}) copy-start(bf16[4,2,144,256]{3,2,1,0:T(8,128)(2,1)S(1)} %collective-permute-done.15.refs_4_) | copy-start | bytes 1769476
  62.4 9.7 %collective-permute-start.7 = (bf16[256,512]{1,0:T(8,128)(2,1)S(1)}, bf16[256,512]{1,0:T(8,128)(2,1)}, u32[]{:S(2)}, u32[]{:S(2)}) collective-permute-start(bf16[256,512]{1,0:T(8,128)(2,1)S(1)} %slice.120), channel_id=1, source_target_pairs={{0,7},{1,0},{2,1},{3,2},{4,3},{5,4},{6,5},{7,6},{8,15},{9,8},{10,9... | collective-permute-start | bytes 786440 | tf_op jit(solution)/shard_map/ppermute | solution.py:60
  65.8 0.8 copy-start.14
  65.8 1.0 copy-start.15
  72.1 1.9 copy-start.7
  83.4 1.6 collective-permute-start.19
  87.4 6.8 %collective-permute-start.20 = (bf16[4,128,128]{2,1,0:T(8,128)(2,1)}, bf16[4,128,128]{2,1,0:T(8,128)(2,1)S(1)}, u32[]{:S(2)}, u32[]{:S(2)}) collective-permute-start(bf16[4,128,128]{2,1,0:T(8,128)(2,1)} %join_chip.1.q), channel_id=1, source_target_pairs={{0,16},{8,24},{16,32},{24,40},{32,48},{40,56},{48,0},{56,8},{64,80... | collective-permute-start | bytes 393224 | tf_op jit(solution)/shard_map/ppermute | solution.py:48
  88.3 8.7 %collective-permute-start.21 = (bf16[4,128,128]{2,1,0:T(8,128)(2,1)}, bf16[4,128,128]{2,1,0:T(8,128)(2,1)S(1)}, u32[]{:S(2)}, u32[]{:S(2)}) collective-permute-start(bf16[4,128,128]{2,1,0:T(8,128)(2,1)} %join_chip.1.q), channel_id=1, source_target_pairs={{0,32},{8,40},{16,48},{24,56},{32,0},{40,8},{48,16},{56,24},{64,96... | collective-permute-start | bytes 393224 | tf_op jit(solution)/shard_map/ppermute | solution.py:48
  90.6 6.4 %collective-permute-start.22 = (bf16[4,128,128]{2,1,0:T(8,128)(2,1)}, bf16[4,128,128]{2,1,0:T(8,128)(2,1)S(1)}, u32[]{:S(2)}, u32[]{:S(2)}) collective-permute-start(bf16[4,128,128]{2,1,0:T(8,128)(2,1)} %join_chip.1.q), channel_id=1, source_target_pairs={{0,48},{8,56},{16,0},{24,8},{32,16},{40,24},{48,32},{56,40},{64,11... | collective-permute-start | bytes 393224 | tf_op jit(solution)/shard_map/ppermute | solution.py:48
  94.2 2.8 %copy-start.23 = (bf16[4,128,128]{2,1,0:T(8,128)(2,1)}, bf16[4,128,128]{2,1,0:T(8,128)(2,1)S(1)}, u32[]{:S(2)}) copy-start(bf16[4,128,128]{2,1,0:T(8,128)(2,1)S(1)} %collective-permute-done.20.g1) | copy-start | bytes 393220
  97.7 0.7 copy-start.25
  100.3 6.9 %collective-permute-start.23 = (bf16[4,128,128]{2,1,0:T(8,128)(2,1)}, bf16[4,128,128]{2,1,0:T(8,128)(2,1)S(1)}, u32[]{:S(2)}, u32[]{:S(2)}) collective-permute-start(bf16[4,128,128]{2,1,0:T(8,128)(2,1)} %get-tuple-element.64), channel_id=1, source_target_pairs={{0,64},{8,72},{16,80},{24,88},{32,96},{40,104},{48,112},{56,120},{... | collective-permute-start | bytes 393224 | tf_op jit(solution)/shard_map/ppermute | solution.py:48
  100.4 9.3 %collective-permute-start.24 = (bf16[4,128,128]{2,1,0:T(8,128)(2,1)}, bf16[4,128,128]{2,1,0:T(8,128)(2,1)S(1)}, u32[]{:S(2)}, u32[]{:S(2)}) collective-permute-start(bf16[4,128,128]{2,1,0:T(8,128)(2,1)} %get-tuple-element.64), channel_id=1, source_target_pairs={{0,128},{8,136},{16,144},{24,152},{32,160},{40,168},{48,176},{56,1... | collective-permute-start | bytes 393224 | tf_op jit(solution)/shard_map/ppermute | solution.py:48
  104.7 5.4 %collective-permute-start.25 = (bf16[4,128,128]{2,1,0:T(8,128)(2,1)}, bf16[4,128,128]{2,1,0:T(8,128)(2,1)S(1)}, u32[]{:S(2)}, u32[]{:S(2)}) collective-permute-start(bf16[4,128,128]{2,1,0:T(8,128)(2,1)} %get-tuple-element.64), channel_id=1, source_target_pairs={{0,192},{8,200},{16,208},{24,216},{32,224},{40,232},{48,240},{56,2... | collective-permute-start | bytes 393224 | tf_op jit(solution)/shard_map/ppermute | solution.py:48
  107.2 2.9 %copy-start.20 = (bf16[4,128,128]{2,1,0:T(8,128)(2,1)}, bf16[4,128,128]{2,1,0:T(8,128)(2,1)S(1)}, u32[]{:S(2)}) copy-start(bf16[4,128,128]{2,1,0:T(8,128)(2,1)S(1)} %collective-permute-done.23.g1) | copy-start | bytes 393220
  109.7 0.7 copy-start.21
  112.8 3.3 %collective-permute-start.26 = (bf16[4,128,128]{2,1,0:T(8,128)(2,1)}, bf16[4,128,128]{2,1,0:T(8,128)(2,1)S(1)}, u32[]{:S(2)}, u32[]{:S(2)}) collective-permute-start(bf16[4,128,128]{2,1,0:T(8,128)(2,1)} %get-tuple-element.70), channel_id=1, source_target_pairs={{0,8},{8,0},{16,24},{24,16},{32,40},{40,32},{48,56},{56,48},{64,72... | collective-permute-start | bytes 393224 | tf_op jit(solution)/shard_map/ppermute | solution.py:52
  116.1 0.7 copy-start.18
  122.7 13.3 %collective-permute-start.28 = (bf16[4,4,256,256]{3,2,1,0:T(8,128)(2,1)}, bf16[4,4,256,256]{3,2,1,0:T(8,128)(2,1)S(1)}, u32[]{:S(2)}, u32[]{:S(2)}) collective-permute-start(bf16[4,4,256,256]{3,2,1,0:T(8,128)(2,1)} %get-tuple-element.79), channel_id=1, source_target_pairs={{0,8},{8,0},{16,24},{24,16},{32,40},{40,32},{48,56},{56,48},{64,72... | collective-permute-start | bytes 6291464 | tf_op jit(solution)/shard_map/ppermute | solution.py:52
  130.1 5.9 %collective-permute-start.27 = (bf16[4,4,256,256]{3,2,1,0:T(8,128)(2,1)}, bf16[4,4,256,256]{3,2,1,0:T(8,128)(2,1)S(1)}, u32[]{:S(2)}, u32[]{:S(2)}) collective-permute-start(bf16[4,4,256,256]{3,2,1,0:T(8,128)(2,1)} %get-tuple-element.77), channel_id=1, source_target_pairs={{0,8},{8,0},{16,24},{24,16},{32,40},{40,32},{48,56},{56,48},{64,72... | collective-permute-start | bytes 6291464 | tf_op jit(solution)/shard_map/ppermute | solution.py:52
  130.3 7.1 %copy-start.8 = (bf16[4,4,256,256]{3,2,1,0:T(8,128)(2,1)S(1)}, bf16[4,4,256,256]{3,2,1,0:T(8,128)(2,1)}, u32[]{:S(2)}) copy-start(bf16[4,4,256,256]{3,2,1,0:T(8,128)(2,1)} %get-tuple-element.74) | copy-start | bytes 6291460
  136.0 1.4 copy-start.9
  141.3 9.9 %collective-permute-start.29 = (bf16[2,2,256,256]{3,2,0,1:T(8,128)(2,1)}, bf16[2,2,256,256]{3,2,0,1:T(8,128)(2,1)}, u32[]{:S(2)}, u32[]{:S(2)}) collective-permute-start(bf16[2,2,256,256]{3,2,0,1:T(8,128)(2,1)} %get-tuple-element.96), channel_id=1, source_target_pairs={{0,16},{8,72},{16,32},{24,88},{32,48},{40,104},{48,0},{56,120},{64... | collective-permute-start | bytes 1572872 | tf_op jit(solution)/shard_map/ppermute | solution.py:39
  141.3 11.1 %collective-permute-start.31 = (bf16[2,2,256,256]{3,2,0,1:T(8,128)(2,1)}, bf16[2,2,256,256]{3,2,0,1:T(8,128)(2,1)}, u32[]{:S(2)}, u32[]{:S(2)}) collective-permute-start(bf16[2,2,256,256]{3,2,0,1:T(8,128)(2,1)} %get-tuple-element.97), channel_id=1, source_target_pairs={{0,48},{8,200},{16,0},{24,216},{32,16},{40,232},{48,32},{56,248},{... | collective-permute-start | bytes 1572872 | tf_op jit(solution)/shard_map/ppermute | solution.py:39
  152.4 15.3 %collective-permute-start.30 = (bf16[4,2,256,256]{3,2,0,1:T(8,128)(2,1)S(1)}, bf16[4,2,256,256]{3,2,0,1:T(8,128)(2,1)S(1)}, u32[]{:S(2)}, u32[]{:S(2)}) collective-permute-start(bf16[4,2,256,256]{3,2,0,1:T(8,128)(2,1)S(1)} %add_convert_fusion.1), channel_id=1, source_target_pairs={{0,16},{8,72},{16,32},{24,88},{32,48},{40,104},{48,0},{56,120},{64... | collective-permute-start | bytes 3145736 | tf_op jit(solution)/shard_map/ppermute | solution.py:39
  153.6 14.5 %collective-permute-start.32 = (bf16[4,2,256,256]{3,2,0,1:T(8,128)(2,1)S(1)}, bf16[4,2,256,256]{3,2,0,1:T(8,128)(2,1)S(1)}, u32[]{:S(2)}, u32[]{:S(2)}) collective-permute-start(bf16[4,2,256,256]{3,2,0,1:T(8,128)(2,1)S(1)} %add_convert_fusion), channel_id=1, source_target_pairs={{0,48},{8,200},{16,0},{24,216},{32,16},{40,232},{48,32},{56,248},{... | collective-permute-start | bytes 3145736 | tf_op jit(solution)/shard_map/ppermute | solution.py:39
  169.3 16.2 %copy-start.16 = (bf16[128,512]{1,0:T(8,128)(2,1)S(1)}, bf16[128,512]{1,0:T(8,128)(2,1)}, u32[]{:S(2)}) copy-start(bf16[128,512]{1,0:T(8,128)(2,1)} %iw.1) | copy-start | bytes 393220
  169.3 16.2 %copy-start.17 = (bf16[128,512]{1,0:T(8,128)(2,1)S(1)}, bf16[128,512]{1,0:T(8,128)(2,1)}, u32[]{:S(2)}) copy-start(bf16[128,512]{1,0:T(8,128)(2,1)} %ow.1) | copy-start | bytes 393220
  169.3 16.2 %copy-start.26 = (f32[512]{0:T(512)S(1)}, f32[512]{0:T(512)}, u32[]{:S(2)}) copy-start(f32[512]{0:T(512)} %param.12) | copy-start | bytes 6148
  169.3 9.9 %collective-permute-start.33 = (bf16[2,256,256]{2,1,0:T(8,128)(2,1)}, bf16[2,256,256]{2,1,0:T(8,128)(2,1)S(1)}, u32[]{:S(2)}, u32[]{:S(2)}) collective-permute-start(bf16[2,256,256]{2,1,0:T(8,128)(2,1)} %get-tuple-element.93), channel_id=1, source_target_pairs={{0,64},{8,24},{16,80},{24,40},{32,96},{40,56},{48,112},{56,8},{64,... | collective-permute-start | bytes 786440 | tf_op jit(solution)/shard_map/ppermute | solution.py:39
  169.4 9.8 %collective-permute-start.34 = (bf16[2,256,256]{2,1,0:T(8,128)(2,1)S(1)}, bf16[2,256,256]{2,1,0:T(8,128)(2,1)S(1)}, u32[]{:S(2)}, u32[]{:S(2)}) collective-permute-start(bf16[2,256,256]{2,1,0:T(8,128)(2,1)S(1)} %get-tuple-element.95), channel_id=1, source_target_pairs={{0,128},{8,40},{16,144},{24,56},{32,160},{40,8},{48,176},{56,24},{... | collective-permute-start | bytes 786440 | tf_op jit(solution)/shard_map/ppermute | solution.py:39
  171.9 7.7 %collective-permute-start.35 = (bf16[2,256,256]{2,1,0:T(8,128)(2,1)S(1)}, bf16[2,256,256]{2,1,0:T(8,128)(2,1)}, u32[]{:S(2)}, u32[]{:S(2)}) collective-permute-start(bf16[2,256,256]{2,1,0:T(8,128)(2,1)S(1)} %get-tuple-element.94), channel_id=1, source_target_pairs={{0,192},{8,56},{16,208},{24,8},{32,224},{40,24},{48,240},{56,40},{... | collective-permute-start | bytes 786440 | tf_op jit(solution)/shard_map/ppermute | solution.py:39
  180.7 4.8 %collective-permute-start.36 = (f32[2,128,256]{2,1,0:T(8,128)S(1)}, f32[2,128,256]{2,1,0:T(8,128)S(1)}, u32[]{:S(2)}, u32[]{:S(2)}) collective-permute-start(f32[2,128,256]{2,1,0:T(8,128)S(1)} %slice_select_fusion), channel_id=1, source_target_pairs={{0,8},{8,0},{16,24},{24,16},{32,40},{40,32},{48,56},{56,48},{64,72... | collective-permute-start | bytes 786440 | tf_op jit(solution)/shard_map/ppermute | solution.py:52
  199.3 20.5 %all-to-all-start = ((f32[32,8,512]{2,1,0:T(8,128)}), f32[32,8,512]{2,1,0:T(8,128)S(1)}, u32[]{:S(2)}, u32[]{:S(2)}) async-start(f32[32,8,512]{2,1,0:T(8,128)} %broadcast_in_dim.7), calls=%async_computation.1 | async-start | bytes 1048576 | tf_op jit(solution)/shard_map/all_to_all | solution.py:522
  (3 other events, 1.9 us)
Sparse Core Ops, SparseCore 0:
  11.1 62.8 all-gather.1
  144.1 36.3 reduce-scatter.1

commit v3 on v2

--- a/solution.py
+++ b/solution.py
@@ -58,6 +58,10 @@
 
 def z_hop(v, d):
     return lax.ppermute(v, "tp", [(z, (z + d) % NZ) for z in range(NZ)])
+
+
+def z_xor(v, b):
+    return lax.ppermute(v, "tp", [(z, z ^ b) for z in range(NZ)])
 
 
 def after(v, other):
@@ -184,8 +188,8 @@
 
 
 def assemble_body(pos, *refs):
-    mine, theirs = refs[:4], refs[4:8]
-    w_out, coef, table = refs[8:]
+    mine, theirs = refs[:4], [refs[4]] + [refs[5].at[i] for i in range(3)]
+    w_out, coef, table = refs[6:]
     y, x, c = pos[0], pos[1], pos[2]
 
     def copy(side, pieces, half):
@@ -553,13 +557,15 @@
     w_in = lax.all_gather(i_levels, "seq", axis=0, tiled=True)
     out_own = jnp.stack([o_keep, swap(o_give)])
     out_row = jnp.stack([out_own] + [hop(out_own, -d) for d in (1, 2, 3)])
+    blocks = gather_z(merged)
+    out_row = after(out_row, (blocks[1], blocks[6]))
     out_all = [out_row] + [hop(out_row, -d, True) for d in (1, 2, 3)]
-    blocks = gather_z(merged)
+    rest = jnp.stack(after(out_all[1:], (blocks[3], blocks[4])))
     w_out, coef = call(
         assemble_body,
         "assemble",
         [sds((D, W), bf16), sds((24, 256), f32)],
-        (pos, *out_all, *[swap(v) for v in out_all]),
+        (pos, *out_all, swap(out_row), swap(rest)),
         10**6,
         [pltpu.VMEM((32, 256), f32)],
     )
@@ -639,7 +645,9 @@
     in_sum = jnp.sum(in_total * in_slopes, axis=0)[None]
     out_sum = jnp.sum(out_total * out_slopes, axis=1)[None]
     in_sum = everyones(in_sum, "seq", NY * NX * NC, 8)
-    out_sum = everyones(out_sum, "tp", NZ, 1)
+    for bits in (1, 2, 4):
+        out_sum = out_sum + z_xor(out_sum, bits)
+    out_sum = out_sum[0]
     return (
         grad_tokens,
         in_total * in_inside,

time: 228 us -> 230 us (level); the launches traced: 227 us -> 227 us
  waiting for transfers between devices: 69.3 us -> 84.3 us
  blocking collectives: 11.9 us -> 0 us
  starting transfers between devices: 65.5 us -> 60.4 us
    ppermute x13, waiting for transfers between devices: 30 us -> 53.3 us  [hop(): return lax.ppermute(v, 'seq', pairs)]
    all_to_all x1 -> x0, blocking collectives: 11.9 us -> none  [everyones(): return jnp.sum(lax.all_to_all(parts, axis, 0, 0, tiled=True)[:, 0], axis=0)]
    all_to_all x1, waiting for transfers between devices: 11 us -> 0.01 us  [everyones(): return jnp.sum(lax.all_to_all(parts, axis, 0, 0, tiled=True)[:, 0], axis=0)]
    ppermute x0 -> x3, waiting for transfers between devices: none -> 9.66 us  [z_xor(): return lax.ppermute(v, 'tp', [(z, z ^ b) for z in range(NZ)])]
    ppermute x8, waiting for transfers between devices: 17.7 us -> 9.97 us  [z_hop(): return lax.ppermute(v, 'tp', [(z, (z + d) % NZ) for z in range(NZ)])]
    ppermute x10 -> x8, starting transfers between devices: 15.7 us -> 12.4 us  [seq_xor(): return lax.ppermute(v, 'seq', [(s, s ^ bits) for s in range(NY * NX * NC)])]
    ppermute x6, starting transfers between devices: 8.61 us -> 5.36 us  [axis_hop(): return lax.ppermute(v, 'seq', pairs)]
    ppermute x0 -> x3, starting transfers between devices: none -> 2.99 us  [z_xor(): return lax.ppermute(v, 'tp', [(z, z ^ b) for z in range(NZ)])]
  transfers between devices with their start and end apart: 40 -> 41, of which waited for: 19 -> 22; matrix products, arithmetic and copies ran while one was open for 4% -> 4% of each run, Pallas kernels for 10% -> 10%
where the time goes in v3:
time: 230 us; the launch traced here: 227 us
  waiting for transfers between devices  84.3 us (37%)
  starting transfers between devices  60.4 us (26%)
  Pallas kernels  46.3 us (20%)
  between operations  14.5 us (6%)
  other arithmetic  11.8 us (5%)
  local copies, waits for them, and re-layouts  9.68 us (4%)
    ppermute x13, waiting for transfers between devices, hop(): return lax.ppermute(v, 'seq', pairs)  53.3 us
    pallas_call x11, Pallas kernels, call(): pl.pallas_call(body, out_shape=outs, in_specs=[smem] + [anyw] * away + [v...  46.3 us
    ppermute x13, starting transfers between devices, hop(): return lax.ppermute(v, 'seq', pairs)  16.4 us
    ppermute x8, starting transfers between devices, z_hop(): return lax.ppermute(v, 'tp', [(z, (z + d) % NZ) for z in range(NZ)])  15.6 us
    ppermute x8, starting transfers between devices, seq_xor(): return lax.ppermute(v, 'seq', [(s, s ^ bits) for s in range(NY * NX * NC)])  12.4 us
    ppermute x8, waiting for transfers between devices, z_hop(): return lax.ppermute(v, 'tp', [(z, (z + d) % NZ) for z in range(NZ)])  9.97 us
    ppermute x3, waiting for transfers between devices, z_xor(): return lax.ppermute(v, 'tp', [(z, z ^ b) for z in range(NZ)])  9.66 us
    ppermute x6, waiting for transfers between devices, axis_hop(): return lax.ppermute(v, 'seq', pairs)  7.73 us
  transfers between devices with their start and end apart: 41, of which 22 were waited for; matrix products, arithmetic and copies ran while one was open for 4% of the time, Pallas kernels for 10%

profile of v3, /device:TPU:1, one launch (start us, length us, event | category | flops | bytes accessed | tf_op | source)
XLA Modules:
  0.0 227.0 jit_solution(17163461088954739516)
XLA Ops:
  7.8 2.6 %prep.1 = (bf16[512,512]{1,0:T(8,128)(2,1)}, bf16[144,256]{1,0:T(8,128)(2,1)}, bf16[144,256]{1,0:T(8,128)(2,1)}, bf16[128,512]{1,0:T(8,128)(2,1)}, f32[256,8]{1,...) custom-call(s32[4]{0:T(128)} %pad_add_fusion.pos, ...), custom_call_target="tpu_custom_call" | custom-call | flops 1000000 | bytes 2058256 | tf_op jit(solution)/shard_map/prep/pallas_call | solution.py:96
  10.6 6.5 %collective-permute-start = (bf16[512,512]{1,0:T(8,128)(2,1)}, bf16[512,512]{1,0:T(8,128)(2,1)S(1)}, u32[]{:S(2)}, u32[]{:S(2)}) collective-permute-start(bf16[512,512]{1,0:T(8,128)(2,1)} %get-tuple-element.48.refs_0_), channel_id=1, source_target_pairs={{0,7},{1,0},{2,1},{3,2},{4,3},{5,4},{6,5},{7,6},{8,15},{9,8},{10,9... | collective-permute-start | bytes 1572872 | tf_op jit(solution)/shard_map/ppermute | solution.py:60
  17.0 1.0 collective-permute-start.8
  18.0 10.0 %collective-permute-done.refs_1_ = bf16[512,512]{1,0:T(8,128)(2,1)S(1)} collective-permute-done((bf16[512,512]{1,0:T(8,128)(2,1)}, bf16[512,512]{1,0:T(8,128)(2,1)S(1)}, u32[]{:S(2)}, u32[]{:S(2)}) %collective-permute-start) | collective-permute-done | bytes 524320 | tf_op jit(solution)/shard_map/ppermute | solution.py:60
  27.9 3.3 %collective-permute-start.1 = (bf16[512,512]{1,0:T(8,128)(2,1)S(1)}, bf16[512,512]{1,0:T(8,128)(2,1)S(1)}, u32[]{:S(2)}, u32[]{:S(2)}) collective-permute-start(bf16[512,512]{1,0:T(8,128)(2,1)S(1)} %collective-permute-done.refs_1_), channel_id=1, source_target_pairs={{0,7},{1,0},{2,1},{3,2},{4,3},{5,4},{6,5},{7,6},{8,15},{9,8},{10,9... | collective-permute-start | bytes 1572872 | tf_op jit(solution)/shard_map/ppermute | solution.py:60
  31.3 1.0 fusion.22
  32.3 2.8 %collective-permute-start.9 = (bf16[2,144,256]{2,1,0:T(8,128)(2,1)S(1)}, bf16[2,144,256]{2,1,0:T(8,128)(2,1)S(1)}, u32[]{:S(2)}, u32[]{:S(2)}) collective-permute-start(bf16[2,144,256]{2,1,0:T(8,128)(2,1)S(1)} %get-tuple-element.111), channel_id=1, source_target_pairs={{0,48},{8,200},{16,0},{24,216},{32,16},{40,232},{48,32},{56,248},{... | collective-permute-start | bytes 442376 | tf_op jit(solution)/shard_map/ppermute | solution.py:39
  35.4 0.7 collective-permute-start.11
  36.1 3.3 %collective-permute-done.9 = bf16[2,144,256]{2,1,0:T(8,128)(2,1)S(1)} collective-permute-done((bf16[2,144,256]{2,1,0:T(8,128)(2,1)S(1)}, bf16[2,144,256]{2,1,0:T(8,128)(2,1)S(1)}, u32[]{:S(2)}, u32[]{:S(2)}) %collective-permute-start.9) | collective-permute-done | bytes 147488 | tf_op jit(solution)/shard_map/ppermute | solution.py:39
  39.5 1.5 collective-permute-done.10
  41.0 1.8 collective-permute-done.11
  42.9 2.4 %collective-permute-start.12 = (bf16[4,2,144,256]{3,2,1,0:T(8,128)(2,1)S(1)}, bf16[4,2,144,256]{3,2,1,0:T(8,128)(2,1)S(1)}, u32[]{:S(2)}, u32[]{:S(2)}) collective-permute-start(bf16[4,2,144,256]{3,2,1,0:T(8,128)(2,1)S(1)} %pad_maximum_fusion.1.refs_0_), channel_id=1, source_target_pairs={{0,192},{8,56},{16,208},{24,8},{32,224},{40,24},{48,240},{56,40},{... | collective-permute-start | bytes 1769480 | tf_op jit(solution)/shard_map/ppermute | solution.py:39
  46.4 2.7 %collective-permute-start.2 = (bf16[512,512]{1,0:T(8,128)(2,1)S(1)}, bf16[512,512]{1,0:T(8,128)(2,1)S(1)}, u32[]{:S(2)}, u32[]{:S(2)}) collective-permute-start(bf16[512,512]{1,0:T(8,128)(2,1)S(1)} %collective-permute-done.1.refs_2_), channel_id=1, source_target_pairs={{0,7},{1,0},{2,1},{3,2},{4,3},{5,4},{6,5},{7,6},{8,15},{9,8},{10,9... | collective-permute-start | bytes 1572872 | tf_op jit(solution)/shard_map/ppermute | solution.py:60
  49.1 7.3 %collective-permute-done.12.refs_1_ = bf16[4,2,144,256]{3,2,1,0:T(8,128)(2,1)S(1)} collective-permute-done((bf16[4,2,144,256]{3,2,1,0:T(8,128)(2,1)S(1)}, bf16[4,2,144,256]{3,2,1,0:T(8,128)(2,1)S(1)}, u32[]{:S(2)}, u32[]{:S(2)}) %collective-permute-start.12) | collective-permute-done | bytes 589856 | tf_op jit(solution)/shard_map/ppermute | solution.py:39
  56.4 1.2 collective-permute-done.13.refs_2_
  57.6 12.2 %collective-permute-done.14.refs_3_ = bf16[4,2,144,256]{3,2,1,0:T(8,128)(2,1)S(1)} collective-permute-done((bf16[4,2,144,256]{3,2,1,0:T(8,128)(2,1)S(1)}, bf16[4,2,144,256]{3,2,1,0:T(8,128)(2,1)S(1)}, u32[]{:S(2)}, u32[]{:S(2)}) %collective-permute-start.14) | collective-permute-done | bytes 589856 | tf_op jit(solution)/shard_map/ppermute | solution.py:39
  70.0 4.8 %collective-permute-start.16 = (bf16[3,4,2,144,256]{4,3,2,1,0:T(8,128)(2,1)S(1)}, bf16[3,4,2,144,256]{4,3,2,1,0:T(8,128)(2,1)S(1)}, u32[]{:S(2)}, u32[]{:S(2)}) collective-permute-start(bf16[3,4,2,144,256]{4,3,2,1,0:T(8,128)(2,1)S(1)} %pad_maximum_fusion), channel_id=1, source_target_pairs={{0,8},{8,0},{16,24},{24,16},{32,40},{40,32},{48,56},{56,48},{64,72... | collective-permute-start | bytes 5308424 | tf_op jit(solution)/shard_map/ppermute | solution.py:52
  75.3 2.9 %collective-permute-start.7 = (bf16[256,512]{1,0:T(8,128)(2,1)S(1)}, bf16[256,512]{1,0:T(8,128)(2,1)S(1)}, u32[]{:S(2)}, u32[]{:S(2)}) collective-permute-start(bf16[256,512]{1,0:T(8,128)(2,1)S(1)} %slice.120), channel_id=1, source_target_pairs={{0,7},{1,0},{2,1},{3,2},{4,3},{5,4},{6,5},{7,6},{8,15},{9,8},{10,9... | collective-permute-start | bytes 786440 | tf_op jit(solution)/shard_map/ppermute | solution.py:60
  78.2 0.7 collective-permute-done.15.refs_4_
  79.0 0.8 copy-done.15
  79.8 1.2 copy-done.14
  81.0 5.2 %assemble.1 = (bf16[4096,512]{1,0:T(8,128)(2,1)}, f32[24,256]{1,0:T(8,128)}) custom-call(s32[4]{0:T(128)} %pad_add_fusion.pos, bf16[4,2,144,256]{3,2,1,0:T(8,128)(2,1)} %copy-done.9, bf16[4,2,144,256]{3,2,1,0:T(8,128)(2,1)} %copy-done.6, bf16[4,2,144,256]{3,2,1,0:T(8,128)(2,1)} %copy-done.7, bf16[4,2,144,256]{3,2,1,0:T(8,128)(2,1)} %copy-done.8, ...), custom_call_target="tpu_custom_call" | custom-call | flops 1000000 | bytes 8937488 | tf_op jit(solution)/shard_map/assemble/pallas_call | solution.py:96
  87.0 9.4 %project.1 = (bf16[256,512]{1,0:T(8,128)(2,1)}, bf16[256,512]{1,0:T(8,128)(2,1)}, bf16[4,128,128]{2,1,0:T(8,128)(2,1)}, bf16[4,128,128]{2,1,0:T(8,128)(2,1)}) custom-call(s32[4]{0:T(128)} %pad_add_fusion.pos, bf16[512,512]{1,0:T(8,128)(2,1)} %get-tuple-element.48.refs_0_, bf16[512,512]{1,0:T(8,128)(2,1)} %copy-done.2, bf16[512,512]{1,0:T(8,128)(2,1)} %copy-done.4, ...), custom_call_target="tpu_custom_call" | custom-call | flops 2147483648 | bytes 13649936 | tf_op jit(solution)/shard_map/project/pallas_call | solution.py:96
  96.9 1.2 collective-permute-done.17.other
  98.7 1.7 join_chip.1.q
  100.4 1.5 collective-permute-start.19
  101.9 1.2 collective-permute-start.20
  103.1 2.5 %grad_local.1.refs_9_ = f32[256,512]{1,0:T(8,128)} custom-call(s32[4]{0:T(128)} %pad_add_fusion.pos, bf16[256,512]{1,0:T(8,128)(2,1)} %get-tuple-element.63.vals, bf16[256,128]{1,0:T(8,128)(2,1)} %refs_10_.2, bf16[256,128]{1,0:T(8,128)(2,1)} %refs_10_.3, f32[256,8]{1,0:T(8,128)} %get-tuple-element.64.a_ref, f32[8,256]{1,0:T(8,128)} %get-tuple-element.65.at_ref), custom_call_target="tpu_custom_call" | custom-call | flops 1000000000 | bytes 933904 | tf_op jit(solution)/shard_map/grad_local/pallas_call | solution.py:96
  105.6 3.8 %collective-permute-done.18.g1 = bf16[4,128,128]{2,1,0:T(8,128)(2,1)S(1)} collective-permute-done((bf16[4,128,128]{2,1,0:T(8,128)(2,1)}, bf16[4,128,128]{2,1,0:T(8,128)(2,1)S(1)}, u32[]{:S(2)}, u32[]{:S(2)}) %collective-permute-start.18) | collective-permute-done | bytes 131104 | tf_op jit(solution)/shard_map/ppermute | solution.py:48
  110.1 0.7 copy-done.25
  110.7 2.0 join_row.1
  112.8 1.5 collective-permute-start.22
  114.2 1.2 collective-permute-start.23
  115.4 2.5 %mixed_local.1.refs_9_ = f32[256,512]{1,0:T(8,128)} custom-call(s32[4]{0:T(128)} %pad_add_fusion.pos, bf16[256,512]{1,0:T(8,128)(2,1)} %get-tuple-element.73.vals, bf16[256,128]{1,0:T(8,128)(2,1)} %refs_10_.2, bf16[256,128]{1,0:T(8,128)(2,1)} %refs_10_.3, f32[256,8]{1,0:T(8,128)} %get-tuple-element.64.a_ref, f32[8,256]{1,0:T(8,128)} %get-tuple-element.65.at_ref), custom_call_target="tpu_custom_call" | custom-call | flops 1000000000 | bytes 933904 | tf_op jit(solution)/shard_map/mixed_local/pallas_call | solution.py:96
  117.9 3.6 %collective-permute-done.21.g1 = bf16[4,128,128]{2,1,0:T(8,128)(2,1)S(1)} collective-permute-done((bf16[4,128,128]{2,1,0:T(8,128)(2,1)}, bf16[4,128,128]{2,1,0:T(8,128)(2,1)S(1)}, u32[]{:S(2)}, u32[]{:S(2)}) %collective-permute-start.21) | collective-permute-done | bytes 131104 | tf_op jit(solution)/shard_map/ppermute | solution.py:48
  122.3 2.1 join_rows.1
  124.4 1.9 collective-permute-start.24
  126.2 1.2 collective-permute-done.24.refs_13_
  128.1 5.9 %out_parts.1 = (bf16[4,4,256,256]{3,2,1,0:T(8,128)(2,1)}, bf16[4,4,256,256]{3,2,1,0:T(8,128)(2,1)}) custom-call(s32[4]{0:T(128)} %pad_add_fusion.pos, bf16[512,512]{1,0:T(8,128)(2,1)} %get-tuple-element.48.refs_0_, bf16[512,512]{1,0:T(8,128)(2,1)} %copy-done.2, bf16[512,512]{1,0:T(8,128)(2,1)} %copy-done.4, bf16[512,512]{1,0:T(8,128)(2,1)} %copy-done, ...), custom_call_target="tpu_custom_call" | custom-call | flops 1073741824 | bytes 9248784 | tf_op jit(solution)/shard_map/out_parts/pallas_call | solution.py:96
  134.5 6.6 %in_parts.1 = (bf16[4,4,256,256]{3,2,1,0:T(8,128)(2,1)}, bf16[4,4,256,256]{3,2,1,0:T(8,128)(2,1)}, bf16[256,512]{1,0:T(8,128)(2,1)}) custom-call(s32[4]{0:T(128)} %pad_add_fusion.pos, bf16[512,512]{1,0:T(8,128)(2,1)} %get-tuple-element.48.refs_0_, bf16[512,512]{1,0:T(8,128)(2,1)} %copy-done.2, bf16[512,512]{1,0:T(8,128)(2,1)} %copy-done.4, ...), custom_call_target="tpu_custom_call" | custom-call | flops 1073741824 | bytes 9512976 | tf_op jit(solution)/shard_map/in_parts/pallas_call | solution.py:96
  141.6 5.7 %token_parts.1 = bf16[8,256,512]{2,1,0:T(8,128)(2,1)} custom-call(s32[4]{0:T(128)} %pad_add_fusion.pos, bf16[4096,512]{1,0:T(8,128)(2,1)} %all-gather.2.cloned.1.call-done.refs_10_.w_in, bf16[256,512]{1,0:T(8,128)(2,1)} %get-tuple-element.83.gs_ref), custom_call_target="tpu_custom_call" | custom-call | flops 1073741824 | bytes 6553616 | tf_op jit(solution)/shard_map/token_parts/pallas_call | solution.py:96
  147.3 1.4 copy-done.13
  148.7 2.8 %fusion = (bf16[4,1,256,256]{3,2,0,1:T(8,128)(2,1)S(1)}, bf16[4,1,256,256]{3,2,0,1:T(8,128)(2,1)S(1)}, bf16[4,1,256,256]{3,2,0,1:T(8,128)(2,1)S(1)}, bf16[4,1,25...) fusion(bf16[4,4,256,256]{3,2,1,0:T(8,128)(2,1)} %copy-done.13, ...), kind=kLoop, calls=%fused_computation.15 | loop fusion | flops 8388608 | bytes 12582912 | tf_op jit(solution)/shard_map/add | solution.py:497
  151.5 1.1 fusion.8
  152.6 2.7 %collective-permute-start.29 = (bf16[2,2,256,256]{3,2,0,1:T(8,128)(2,1)}, bf16[2,2,256,256]{3,2,0,1:T(8,128)(2,1)}, u32[]{:S(2)}, u32[]{:S(2)}) collective-permute-start(bf16[2,2,256,256]{3,2,0,1:T(8,128)(2,1)} %get-tuple-element.105), channel_id=1, source_target_pairs={{0,48},{8,200},{16,0},{24,216},{32,16},{40,232},{48,32},{56,248},{... | collective-permute-start | bytes 1572872 | tf_op jit(solution)/shard_map/ppermute | solution.py:39
  155.3 7.2 %collective-permute-done.27 = bf16[2,2,256,256]{3,2,0,1:T(8,128)(2,1)} collective-permute-done((bf16[2,2,256,256]{3,2,0,1:T(8,128)(2,1)}, bf16[2,2,256,256]{3,2,0,1:T(8,128)(2,1)}, u32[]{:S(2)}, u32[]{:S(2)}) %collective-permute-start.27) | collective-permute-done | bytes 524320 | tf_op jit(solution)/shard_map/ppermute | solution.py:39
  162.4 1.2 add_convert_fusion.1
  163.7 1.2 add_convert_fusion
  164.9 2.7 %collective-permute-start.30 = (bf16[4,2,256,256]{3,2,0,1:T(8,128)(2,1)S(1)}, bf16[4,2,256,256]{3,2,0,1:T(8,128)(2,1)S(1)}, u32[]{:S(2)}, u32[]{:S(2)}) collective-permute-start(bf16[4,2,256,256]{3,2,0,1:T(8,128)(2,1)S(1)} %add_convert_fusion), channel_id=1, source_target_pairs={{0,48},{8,200},{16,0},{24,216},{32,16},{40,232},{48,32},{56,248},{... | collective-permute-start | bytes 3145736 | tf_op jit(solution)/shard_map/ppermute | solution.py:39
  167.7 11.3 %collective-permute-done.28 = bf16[4,2,256,256]{3,2,0,1:T(8,128)(2,1)S(1)} collective-permute-done((bf16[4,2,256,256]{3,2,0,1:T(8,128)(2,1)S(1)}, bf16[4,2,256,256]{3,2,0,1:T(8,128)(2,1)S(1)}, u32[]{:S(2)}, u32[]{:S(2)}) %collective-permute-start.28) | collective-permute-done | bytes 1048608 | tf_op jit(solution)/shard_map/ppermute | solution.py:39
  179.9 0.8 slice_bitcast_fusion.3
  180.6 3.5 %collective-permute-start.32 = (bf16[2,256,256]{2,1,0:T(8,128)(2,1)S(1)}, bf16[2,256,256]{2,1,0:T(8,128)(2,1)S(1)}, u32[]{:S(2)}, u32[]{:S(2)}) collective-permute-start(bf16[2,256,256]{2,1,0:T(8,128)(2,1)S(1)} %get-tuple-element.103), channel_id=1, source_target_pairs={{0,128},{8,40},{16,144},{24,56},{32,160},{40,8},{48,176},{56,24},{... | collective-permute-start | bytes 786440 | tf_op jit(solution)/shard_map/ppermute | solution.py:39
  184.2 3.5 %collective-permute-done.31 = bf16[2,256,256]{2,1,0:T(8,128)(2,1)S(1)} collective-permute-done((bf16[2,256,256]{2,1,0:T(8,128)(2,1)}, bf16[2,256,256]{2,1,0:T(8,128)(2,1)S(1)}, u32[]{:S(2)}, u32[]{:S(2)}) %collective-permute-start.31) | collective-permute-done | bytes 262176 | tf_op jit(solution)/shard_map/ppermute | solution.py:39
  187.7 3.6 %collective-permute-done.32 = bf16[2,256,256]{2,1,0:T(8,128)(2,1)S(1)} collective-permute-done((bf16[2,256,256]{2,1,0:T(8,128)(2,1)S(1)}, bf16[2,256,256]{2,1,0:T(8,128)(2,1)S(1)}, u32[]{:S(2)}, u32[]{:S(2)}) %collective-permute-start.32) | collective-permute-done | bytes 262176 | tf_op jit(solution)/shard_map/ppermute | solution.py:39
  191.2 1.1 fusion.11
  192.3 3.3 %collective-permute-start.34 = (f32[2,128,256]{2,1,0:T(8,128)S(1)}, f32[2,128,256]{2,1,0:T(8,128)S(1)}, u32[]{:S(2)}, u32[]{:S(2)}) collective-permute-start(f32[2,128,256]{2,1,0:T(8,128)S(1)} %slice_select_fusion), channel_id=1, source_target_pairs={{0,8},{8,0},{16,24},{24,16},{32,40},{40,32},{48,56},{56,48},{64,72... | collective-permute-start | bytes 786440 | tf_op jit(solution)/shard_map/ppermute | solution.py:52
  195.6 0.8 dynamic_slice.3
  196.9 1.0 fusion.15
  197.9 0.9 broadcast_in_dim.14
  198.7 7.6 %all-to-all-start = ((f32[32,8,512]{2,1,0:T(8,128)}), f32[32,8,512]{2,1,0:T(8,128)S(1)}, u32[]{:S(2)}, u32[]{:S(2)}) async-start(f32[32,8,512]{2,1,0:T(8,128)} %broadcast_in_dim.14), calls=%async_computation.1 | async-start | bytes 1048576 | tf_op jit(solution)/shard_map/all_to_all | solution.py:526
  206.4 2.7 %collective-permute-done.35 = f32[1,128]{1,0:T(1,128)S(1)} collective-permute-done((f32[1,128]{1,0:T(1,128)S(1)}, f32[1,128]{1,0:T(1,128)S(1)}, u32[]{:S(2)}, u32[]{:S(2)}) %collective-permute-start.35) | collective-permute-done | bytes 544 | tf_op jit(solution)/shard_map/ppermute | solution.py:64
  209.7 3.0 %collective-permute-done.36 = f32[1,128]{1,0:T(1,128)S(1)} collective-permute-done((f32[1,128]{1,0:T(1,128)S(1)}, f32[1,128]{1,0:T(1,128)S(1)}, u32[]{:S(2)}, u32[]{:S(2)}) %collective-permute-start.36) | collective-permute-done | bytes 544 | tf_op jit(solution)/shard_map/ppermute | solution.py:64
  212.7 2.3 %collective-permute-start.37 = (f32[1,128]{1,0:T(1,128)S(1)}, f32[1,128]{1,0:T(1,128)S(1)}, u32[]{:S(2)}, u32[]{:S(2)}) collective-permute-start(f32[1,128]{1,0:T(1,128)S(1)} %add.187), channel_id=1, source_target_pairs={{0,4},{1,5},{2,6},{3,7},{4,0},{5,1},{6,2},{7,3},{8,12},{9,13},{10,... | collective-permute-start | bytes 1544 | tf_op jit(solution)/shard_map/ppermute | solution.py:64
  215.0 4.0 %collective-permute-done.37 = f32[1,128]{1,0:T(1,128)S(1)} collective-permute-done((f32[1,128]{1,0:T(1,128)S(1)}, f32[1,128]{1,0:T(1,128)S(1)}, u32[]{:S(2)}, u32[]{:S(2)}) %collective-permute-start.37) | collective-permute-done | bytes 544 | tf_op jit(solution)/shard_map/ppermute | solution.py:64
  (108 shorter events, 11.2 us)
Async XLA Ops:
  7.2 79.1 %all-gather.2.cloned.1.call-start = ((), (), s32[]{:S(2)}) async-start(), calls=%async_computation.2 | async-start | bytes 4325376 | tf_op jit(solution)/shard_map/all_gather | solution.py:557
  10.5 209.6 %reduce-scatter.2.cloned.1.call-start = ((), (), s32[]{:S(2)}) async-start(), calls=%async_computation.3 | async-start | bytes 2359296 | tf_op jit(solution)/shard_map/reduce_scatter | solution.py:636
  10.6 17.4 %collective-permute-start = (bf16[512,512]{1,0:T(8,128)(2,1)}, bf16[512,512]{1,0:T(8,128)(2,1)S(1)}, u32[]{:S(2)}, u32[]{:S(2)}) collective-permute-start(bf16[512,512]{1,0:T(8,128)(2,1)} %get-tuple-element.48.refs_0_), channel_id=1, source_target_pairs={{0,7},{1,0},{2,1},{3,2},{4,3},{5,4},{6,5},{7,6},{8,15},{9,8},{10,9... | collective-permute-start | bytes 1572872 | tf_op jit(solution)/shard_map/ppermute | solution.py:60
  17.0 14.2 %collective-permute-start.3 = (bf16[512,512]{1,0:T(8,128)(2,1)}, bf16[512,512]{1,0:T(8,128)(2,1)S(1)}, u32[]{:S(2)}, u32[]{:S(2)}) collective-permute-start(bf16[512,512]{1,0:T(8,128)(2,1)} %get-tuple-element.48.refs_0_), channel_id=1, source_target_pairs={{0,1},{1,2},{2,3},{3,4},{4,5},{5,6},{6,7},{7,0},{8,9},{9,10},{10,1... | collective-permute-start | bytes 1572872 | tf_op jit(solution)/shard_map/ppermute | solution.py:60
  17.0 14.2 %collective-permute-start.8 = (bf16[144,256]{1,0:T(8,128)(2,1)}, bf16[144,256]{1,0:T(8,128)(2,1)S(1)}, u32[]{:S(2)}, u32[]{:S(2)}) collective-permute-start(bf16[144,256]{1,0:T(8,128)(2,1)} %get-tuple-element.50), channel_id=1, source_target_pairs={{0,8},{8,0},{16,24},{24,16},{32,40},{40,32},{48,56},{56,48},{64,72... | collective-permute-start | bytes 221192 | tf_op jit(solution)/shard_map/ppermute | solution.py:52
  27.9 42.1 %copy-start.2 = (bf16[512,512]{1,0:T(8,128)(2,1)}, bf16[512,512]{1,0:T(8,128)(2,1)S(1)}, u32[]{:S(2)}) copy-start(bf16[512,512]{1,0:T(8,128)(2,1)S(1)} %collective-permute-done.refs_1_) | copy-start | bytes 1572868
  27.9 18.5 %collective-permute-start.1 = (bf16[512,512]{1,0:T(8,128)(2,1)S(1)}, bf16[512,512]{1,0:T(8,128)(2,1)S(1)}, u32[]{:S(2)}, u32[]{:S(2)}) collective-permute-start(bf16[512,512]{1,0:T(8,128)(2,1)S(1)} %collective-permute-done.refs_1_), channel_id=1, source_target_pairs={{0,7},{1,0},{2,1},{3,2},{4,3},{5,4},{6,5},{7,6},{8,15},{9,8},{10,9... | collective-permute-start | bytes 1572872 | tf_op jit(solution)/shard_map/ppermute | solution.py:60
  31.3 38.8 %copy-start.3 = (bf16[512,512]{1,0:T(8,128)(2,1)}, bf16[512,512]{1,0:T(8,128)(2,1)S(1)}, u32[]{:S(2)}) copy-start(bf16[512,512]{1,0:T(8,128)(2,1)S(1)} %collective-permute-done.3.refs_6_) | copy-start | bytes 1572868
  31.3 17.8 %collective-permute-start.4 = (bf16[512,512]{1,0:T(8,128)(2,1)S(1)}, bf16[512,512]{1,0:T(8,128)(2,1)S(1)}, u32[]{:S(2)}, u32[]{:S(2)}) collective-permute-start(bf16[512,512]{1,0:T(8,128)(2,1)S(1)} %collective-permute-done.3.refs_6_), channel_id=1, source_target_pairs={{0,1},{1,2},{2,3},{3,4},{4,5},{5,6},{6,7},{7,0},{8,9},{9,10},{10,1... | collective-permute-start | bytes 1572872 | tf_op jit(solution)/shard_map/ppermute | solution.py:60
  32.3 7.2 %collective-permute-start.9 = (bf16[2,144,256]{2,1,0:T(8,128)(2,1)S(1)}, bf16[2,144,256]{2,1,0:T(8,128)(2,1)S(1)}, u32[]{:S(2)}, u32[]{:S(2)}) collective-permute-start(bf16[2,144,256]{2,1,0:T(8,128)(2,1)S(1)} %get-tuple-element.111), channel_id=1, source_target_pairs={{0,48},{8,200},{16,0},{24,216},{32,16},{40,232},{48,32},{56,248},{... | collective-permute-start | bytes 442376 | tf_op jit(solution)/shard_map/ppermute | solution.py:39
  35.1 5.9 %collective-permute-start.10 = (bf16[2,144,256]{2,1,0:T(8,128)(2,1)S(1)}, bf16[2,144,256]{2,1,0:T(8,128)(2,1)S(1)}, u32[]{:S(2)}, u32[]{:S(2)}) collective-permute-start(bf16[2,144,256]{2,1,0:T(8,128)(2,1)S(1)} %get-tuple-element.111), channel_id=1, source_target_pairs={{0,32},{8,136},{16,48},{24,152},{32,0},{40,168},{48,16},{56,184},{... | collective-permute-start | bytes 442376 | tf_op jit(solution)/shard_map/ppermute | solution.py:39
  35.4 7.4 %collective-permute-start.11 = (bf16[2,144,256]{2,1,0:T(8,128)(2,1)S(1)}, bf16[2,144,256]{2,1,0:T(8,128)(2,1)S(1)}, u32[]{:S(2)}, u32[]{:S(2)}) collective-permute-start(bf16[2,144,256]{2,1,0:T(8,128)(2,1)S(1)} %get-tuple-element.111), channel_id=1, source_target_pairs={{0,16},{8,72},{16,32},{24,88},{32,48},{40,104},{48,0},{56,120},{64... | collective-permute-start | bytes 442376 | tf_op jit(solution)/shard_map/ppermute | solution.py:39
  42.9 32.4 %copy-start.9 = (bf16[4,2,144,256]{3,2,1,0:T(8,128)(2,1)}, bf16[4,2,144,256]{3,2,1,0:T(8,128)(2,1)S(1)}, u32[]{:S(2)}) copy-start(bf16[4,2,144,256]{3,2,1,0:T(8,128)(2,1)S(1)} %pad_maximum_fusion.1.refs_0_) | copy-start | bytes 1769476
  42.9 13.5 %collective-permute-start.12 = (bf16[4,2,144,256]{3,2,1,0:T(8,128)(2,1)S(1)}, bf16[4,2,144,256]{3,2,1,0:T(8,128)(2,1)S(1)}, u32[]{:S(2)}, u32[]{:S(2)}) collective-permute-start(bf16[4,2,144,256]{3,2,1,0:T(8,128)(2,1)S(1)} %pad_maximum_fusion.1.refs_0_), channel_id=1, source_target_pairs={{0,192},{8,56},{16,208},{24,8},{32,224},{40,24},{48,240},{56,40},{... | collective-permute-start | bytes 1769480 | tf_op jit(solution)/shard_map/ppermute | solution.py:39
  45.3 12.3 %collective-permute-start.13 = (bf16[4,2,144,256]{3,2,1,0:T(8,128)(2,1)S(1)}, bf16[4,2,144,256]{3,2,1,0:T(8,128)(2,1)S(1)}, u32[]{:S(2)}, u32[]{:S(2)}) collective-permute-start(bf16[4,2,144,256]{3,2,1,0:T(8,128)(2,1)S(1)} %pad_maximum_fusion.1.refs_0_), channel_id=1, source_target_pairs={{0,128},{8,40},{16,144},{24,56},{32,160},{40,8},{48,176},{56,24},{... | collective-permute-start | bytes 1769480 | tf_op jit(solution)/shard_map/ppermute | solution.py:39
  45.8 23.9 %collective-permute-start.14 = (bf16[4,2,144,256]{3,2,1,0:T(8,128)(2,1)S(1)}, bf16[4,2,144,256]{3,2,1,0:T(8,128)(2,1)S(1)}, u32[]{:S(2)}, u32[]{:S(2)}) collective-permute-start(bf16[4,2,144,256]{3,2,1,0:T(8,128)(2,1)S(1)} %pad_maximum_fusion.1.refs_0_), channel_id=1, source_target_pairs={{0,64},{8,24},{16,80},{24,40},{32,96},{40,56},{48,112},{56,8},{64,... | collective-permute-start | bytes 1769480 | tf_op jit(solution)/shard_map/ppermute | solution.py:39
  46.4 28.8 %copy-start.4 = (bf16[512,512]{1,0:T(8,128)(2,1)}, bf16[512,512]{1,0:T(8,128)(2,1)S(1)}, u32[]{:S(2)}) copy-start(bf16[512,512]{1,0:T(8,128)(2,1)S(1)} %collective-permute-done.1.refs_2_) | copy-start | bytes 1572868
  46.4 23.4 %collective-permute-start.2 = (bf16[512,512]{1,0:T(8,128)(2,1)S(1)}, bf16[512,512]{1,0:T(8,128)(2,1)S(1)}, u32[]{:S(2)}, u32[]{:S(2)}) collective-permute-start(bf16[512,512]{1,0:T(8,128)(2,1)S(1)} %collective-permute-done.1.refs_2_), channel_id=1, source_target_pairs={{0,7},{1,0},{2,1},{3,2},{4,3},{5,4},{6,5},{7,6},{8,15},{9,8},{10,9... | collective-permute-start | bytes 1572872 | tf_op jit(solution)/shard_map/ppermute | solution.py:60
  49.1 26.2 %copy-start.5 = (bf16[512,512]{1,0:T(8,128)(2,1)}, bf16[512,512]{1,0:T(8,128)(2,1)S(1)}, u32[]{:S(2)}) copy-start(bf16[512,512]{1,0:T(8,128)(2,1)S(1)} %collective-permute-done.4.refs_5_) | copy-start | bytes 1572868
  49.1 20.7 %collective-permute-start.5 = (bf16[512,512]{1,0:T(8,128)(2,1)S(1)}, bf16[512,512]{1,0:T(8,128)(2,1)S(1)}, u32[]{:S(2)}, u32[]{:S(2)}) collective-permute-start(bf16[512,512]{1,0:T(8,128)(2,1)S(1)} %collective-permute-done.4.refs_5_), channel_id=1, source_target_pairs={{0,1},{1,2},{2,3},{3,4},{4,5},{5,6},{6,7},{7,0},{8,9},{9,10},{10,1... | collective-permute-start | bytes 1572872 | tf_op jit(solution)/shard_map/ppermute | solution.py:60
  56.4 18.9 %copy-start.6 = (bf16[4,2,144,256]{3,2,1,0:T(8,128)(2,1)}, bf16[4,2,144,256]{3,2,1,0:T(8,128)(2,1)S(1)}, u32[]{:S(2)}) copy-start(bf16[4,2,144,256]{3,2,1,0:T(8,128)(2,1)S(1)} %collective-permute-done.12.refs_1_) | copy-start | bytes 1769476
  57.6 17.7 %copy-start.7 = (bf16[4,2,144,256]{3,2,1,0:T(8,128)(2,1)}, bf16[4,2,144,256]{3,2,1,0:T(8,128)(2,1)S(1)}, u32[]{:S(2)}) copy-start(bf16[4,2,144,256]{3,2,1,0:T(8,128)(2,1)S(1)} %collective-permute-done.13.refs_2_) | copy-start | bytes 1769476
  69.8 5.5 %copy-start.8 = (bf16[4,2,144,256]{3,2,1,0:T(8,128)(2,1)}, bf16[4,2,144,256]{3,2,1,0:T(8,128)(2,1)S(1)}, u32[]{:S(2)}) copy-start(bf16[4,2,144,256]{3,2,1,0:T(8,128)(2,1)S(1)} %collective-permute-done.14.refs_3_) | copy-start | bytes 1769476
  69.8 5.5 %copy-start = (bf16[512,512]{1,0:T(8,128)(2,1)}, bf16[512,512]{1,0:T(8,128)(2,1)S(1)}, u32[]{:S(2)}) copy-start(bf16[512,512]{1,0:T(8,128)(2,1)S(1)} %collective-permute-done.2.refs_3_) | copy-start | bytes 1572868
  69.8 5.5 %copy-start.1 = (bf16[512,512]{1,0:T(8,128)(2,1)}, bf16[512,512]{1,0:T(8,128)(2,1)S(1)}, u32[]{:S(2)}) copy-start(bf16[512,512]{1,0:T(8,128)(2,1)S(1)} %collective-permute-done.5.refs_4_) | copy-start | bytes 1572868
  70.0 9.0 %collective-permute-start.16 = (bf16[3,4,2,144,256]{4,3,2,1,0:T(8,128)(2,1)S(1)}, bf16[3,4,2,144,256]{4,3,2,1,0:T(8,128)(2,1)S(1)}, u32[]{:S(2)}, u32[]{:S(2)}) collective-permute-start(bf16[3,4,2,144,256]{4,3,2,1,0:T(8,128)(2,1)S(1)} %pad_maximum_fusion), channel_id=1, source_target_pairs={{0,8},{8,0},{16,24},{24,16},{32,40},{40,32},{48,56},{56,48},{64,72... | collective-permute-start | bytes 5308424 | tf_op jit(solution)/shard_map/ppermute | solution.py:52
  74.8 4.2 %collective-permute-start.15 = (bf16[4,2,144,256]{3,2,1,0:T(8,128)(2,1)S(1)}, bf16[4,2,144,256]{3,2,1,0:T(8,128)(2,1)S(1)}, u32[]{:S(2)}, u32[]{:S(2)}) collective-permute-start(bf16[4,2,144,256]{3,2,1,0:T(8,128)(2,1)S(1)} %pad_maximum_fusion.1.refs_0_), channel_id=1, source_target_pairs={{0,8},{8,0},{16,24},{24,16},{32,40},{40,32},{48,56},{56,48},{64,72... | collective-permute-start | bytes 1769480 | tf_op jit(solution)/shard_map/ppermute | solution.py:52
  74.9 11.3 %collective-permute-start.6 = (bf16[256,512]{1,0:T(8,128)(2,1)S(1)}, bf16[256,512]{1,0:T(8,128)(2,1)S(1)}, u32[]{:S(2)}, u32[]{:S(2)}) collective-permute-start(bf16[256,512]{1,0:T(8,128)(2,1)S(1)} %slice.119), channel_id=1, source_target_pairs={{0,1},{1,2},{2,3},{3,4},{4,5},{5,6},{6,7},{7,0},{8,9},{9,10},{10,1... | collective-permute-start | bytes 786440 | tf_op jit(solution)/shard_map/ppermute | solution.py:60
  75.3 10.9 %collective-permute-start.7 = (bf16[256,512]{1,0:T(8,128)(2,1)S(1)}, bf16[256,512]{1,0:T(8,128)(2,1)S(1)}, u32[]{:S(2)}, u32[]{:S(2)}) collective-permute-start(bf16[256,512]{1,0:T(8,128)(2,1)S(1)} %slice.120), channel_id=1, source_target_pairs={{0,7},{1,0},{2,1},{3,2},{4,3},{5,4},{6,5},{7,6},{8,15},{9,8},{10,9... | collective-permute-start | bytes 786440 | tf_op jit(solution)/shard_map/ppermute | solution.py:60
  79.0 0.8 copy-start.15
  79.8 1.2 copy-start.14
  86.2 0.7 copy-start.10
  86.2 0.8 copy-start.11
  96.4 1.7 collective-permute-start.17
  100.4 9.0 %collective-permute-start.18 = (bf16[4,128,128]{2,1,0:T(8,128)(2,1)}, bf16[4,128,128]{2,1,0:T(8,128)(2,1)S(1)}, u32[]{:S(2)}, u32[]{:S(2)}) collective-permute-start(bf16[4,128,128]{2,1,0:T(8,128)(2,1)} %join_chip.1.q), channel_id=1, source_target_pairs={{0,16},{8,24},{16,32},{24,40},{32,48},{40,56},{48,0},{56,8},{64,80... | collective-permute-start | bytes 393224 | tf_op jit(solution)/shard_map/ppermute | solution.py:48
  100.4 9.0 %collective-permute-start.19 = (bf16[4,128,128]{2,1,0:T(8,128)(2,1)}, bf16[4,128,128]{2,1,0:T(8,128)(2,1)S(1)}, u32[]{:S(2)}, u32[]{:S(2)}) collective-permute-start(bf16[4,128,128]{2,1,0:T(8,128)(2,1)} %join_chip.1.q), channel_id=1, source_target_pairs={{0,32},{8,40},{16,48},{24,56},{32,0},{40,8},{48,16},{56,24},{64,96... | collective-permute-start | bytes 393224 | tf_op jit(solution)/shard_map/ppermute | solution.py:48
  101.9 7.8 %collective-permute-start.20 = (bf16[4,128,128]{2,1,0:T(8,128)(2,1)}, bf16[4,128,128]{2,1,0:T(8,128)(2,1)S(1)}, u32[]{:S(2)}, u32[]{:S(2)}) collective-permute-start(bf16[4,128,128]{2,1,0:T(8,128)(2,1)} %join_chip.1.q), channel_id=1, source_target_pairs={{0,48},{8,56},{16,0},{24,8},{32,16},{40,24},{48,32},{56,40},{64,11... | collective-permute-start | bytes 393224 | tf_op jit(solution)/shard_map/ppermute | solution.py:48
  109.4 0.7 copy-start.23
  109.4 0.7 copy-start.24
  112.8 8.8 %collective-permute-start.21 = (bf16[4,128,128]{2,1,0:T(8,128)(2,1)}, bf16[4,128,128]{2,1,0:T(8,128)(2,1)S(1)}, u32[]{:S(2)}, u32[]{:S(2)}) collective-permute-start(bf16[4,128,128]{2,1,0:T(8,128)(2,1)} %get-tuple-element.72), channel_id=1, source_target_pairs={{0,64},{8,72},{16,80},{24,88},{32,96},{40,104},{48,112},{56,120},{... | collective-permute-start | bytes 393224 | tf_op jit(solution)/shard_map/ppermute | solution.py:48
  112.8 8.8 %collective-permute-start.22 = (bf16[4,128,128]{2,1,0:T(8,128)(2,1)}, bf16[4,128,128]{2,1,0:T(8,128)(2,1)S(1)}, u32[]{:S(2)}, u32[]{:S(2)}) collective-permute-start(bf16[4,128,128]{2,1,0:T(8,128)(2,1)} %get-tuple-element.72), channel_id=1, source_target_pairs={{0,128},{8,136},{16,144},{24,152},{32,160},{40,168},{48,176},{56,1... | collective-permute-start | bytes 393224 | tf_op jit(solution)/shard_map/ppermute | solution.py:48
  114.2 7.3 %collective-permute-start.23 = (bf16[4,128,128]{2,1,0:T(8,128)(2,1)}, bf16[4,128,128]{2,1,0:T(8,128)(2,1)S(1)}, u32[]{:S(2)}, u32[]{:S(2)}) collective-permute-start(bf16[4,128,128]{2,1,0:T(8,128)(2,1)} %get-tuple-element.72), channel_id=1, source_target_pairs={{0,192},{8,200},{16,208},{24,216},{32,224},{40,232},{48,240},{56,2... | collective-permute-start | bytes 393224 | tf_op jit(solution)/shard_map/ppermute | solution.py:48
  121.5 0.7 copy-start.21
  121.6 0.7 copy-start.22
  124.4 3.1 %collective-permute-start.24 = (bf16[4,128,128]{2,1,0:T(8,128)(2,1)}, bf16[4,128,128]{2,1,0:T(8,128)(2,1)S(1)}, u32[]{:S(2)}, u32[]{:S(2)}) collective-permute-start(bf16[4,128,128]{2,1,0:T(8,128)(2,1)} %get-tuple-element.78), channel_id=1, source_target_pairs={{0,8},{8,0},{16,24},{24,16},{32,40},{40,32},{48,56},{56,48},{64,72... | collective-permute-start | bytes 393224 | tf_op jit(solution)/shard_map/ppermute | solution.py:52
  134.0 13.3 %collective-permute-start.26 = (bf16[4,4,256,256]{3,2,1,0:T(8,128)(2,1)}, bf16[4,4,256,256]{3,2,1,0:T(8,128)(2,1)S(1)}, u32[]{:S(2)}, u32[]{:S(2)}) collective-permute-start(bf16[4,4,256,256]{3,2,1,0:T(8,128)(2,1)} %get-tuple-element.87), channel_id=1, source_target_pairs={{0,8},{8,0},{16,24},{24,16},{32,40},{40,32},{48,56},{56,48},{64,72... | collective-permute-start | bytes 6291464 | tf_op jit(solution)/shard_map/ppermute | solution.py:52
  141.1 6.2 %collective-permute-start.25 = (bf16[4,4,256,256]{3,2,1,0:T(8,128)(2,1)}, bf16[4,4,256,256]{3,2,1,0:T(8,128)(2,1)S(1)}, u32[]{:S(2)}, u32[]{:S(2)}) collective-permute-start(bf16[4,4,256,256]{3,2,1,0:T(8,128)(2,1)} %get-tuple-element.85), channel_id=1, source_target_pairs={{0,8},{8,0},{16,24},{24,16},{32,40},{40,32},{48,56},{56,48},{64,72... | collective-permute-start | bytes 6291464 | tf_op jit(solution)/shard_map/ppermute | solution.py:52
  141.6 7.1 %copy-start.12 = (bf16[4,4,256,256]{3,2,1,0:T(8,128)(2,1)S(1)}, bf16[4,4,256,256]{3,2,1,0:T(8,128)(2,1)}, u32[]{:S(2)}) copy-start(bf16[4,4,256,256]{3,2,1,0:T(8,128)(2,1)} %get-tuple-element.82) | copy-start | bytes 6291460
  147.3 1.4 copy-start.13
  152.6 9.9 %collective-permute-start.27 = (bf16[2,2,256,256]{3,2,0,1:T(8,128)(2,1)}, bf16[2,2,256,256]{3,2,0,1:T(8,128)(2,1)}, u32[]{:S(2)}, u32[]{:S(2)}) collective-permute-start(bf16[2,2,256,256]{3,2,0,1:T(8,128)(2,1)} %get-tuple-element.104), channel_id=1, source_target_pairs={{0,16},{8,72},{16,32},{24,88},{32,48},{40,104},{48,0},{56,120},{64... | collective-permute-start | bytes 1572872 | tf_op jit(solution)/shard_map/ppermute | solution.py:39
  152.6 11.1 %collective-permute-start.29 = (bf16[2,2,256,256]{3,2,0,1:T(8,128)(2,1)}, bf16[2,2,256,256]{3,2,0,1:T(8,128)(2,1)}, u32[]{:S(2)}, u32[]{:S(2)}) collective-permute-start(bf16[2,2,256,256]{3,2,0,1:T(8,128)(2,1)} %get-tuple-element.105), channel_id=1, source_target_pairs={{0,48},{8,200},{16,0},{24,216},{32,16},{40,232},{48,32},{56,248},{... | collective-permute-start | bytes 1572872 | tf_op jit(solution)/shard_map/ppermute | solution.py:39
  163.6 15.3 %collective-permute-start.28 = (bf16[4,2,256,256]{3,2,0,1:T(8,128)(2,1)S(1)}, bf16[4,2,256,256]{3,2,0,1:T(8,128)(2,1)S(1)}, u32[]{:S(2)}, u32[]{:S(2)}) collective-permute-start(bf16[4,2,256,256]{3,2,0,1:T(8,128)(2,1)S(1)} %add_convert_fusion.1), channel_id=1, source_target_pairs={{0,16},{8,72},{16,32},{24,88},{32,48},{40,104},{48,0},{56,120},{64... | collective-permute-start | bytes 3145736 | tf_op jit(solution)/shard_map/ppermute | solution.py:39
  164.9 14.5 %collective-permute-start.30 = (bf16[4,2,256,256]{3,2,0,1:T(8,128)(2,1)S(1)}, bf16[4,2,256,256]{3,2,0,1:T(8,128)(2,1)S(1)}, u32[]{:S(2)}, u32[]{:S(2)}) collective-permute-start(bf16[4,2,256,256]{3,2,0,1:T(8,128)(2,1)S(1)} %add_convert_fusion), channel_id=1, source_target_pairs={{0,48},{8,200},{16,0},{24,216},{32,16},{40,232},{48,32},{56,248},{... | collective-permute-start | bytes 3145736 | tf_op jit(solution)/shard_map/ppermute | solution.py:39
  180.6 16.2 %copy-start.16 = (bf16[128,512]{1,0:T(8,128)(2,1)S(1)}, bf16[128,512]{1,0:T(8,128)(2,1)}, u32[]{:S(2)}) copy-start(bf16[128,512]{1,0:T(8,128)(2,1)} %iw.1) | copy-start | bytes 393220
  180.6 16.2 %copy-start.17 = (bf16[128,512]{1,0:T(8,128)(2,1)S(1)}, bf16[128,512]{1,0:T(8,128)(2,1)}, u32[]{:S(2)}) copy-start(bf16[128,512]{1,0:T(8,128)(2,1)} %ow.1) | copy-start | bytes 393220
  180.6 16.2 %copy-start.26 = (f32[512]{0:T(512)S(1)}, f32[512]{0:T(512)}, u32[]{:S(2)}) copy-start(f32[512]{0:T(512)} %param.12) | copy-start | bytes 6148
  180.6 7.0 %collective-permute-start.31 = (bf16[2,256,256]{2,1,0:T(8,128)(2,1)}, bf16[2,256,256]{2,1,0:T(8,128)(2,1)S(1)}, u32[]{:S(2)}, u32[]{:S(2)}) collective-permute-start(bf16[2,256,256]{2,1,0:T(8,128)(2,1)} %get-tuple-element.101), channel_id=1, source_target_pairs={{0,64},{8,24},{16,80},{24,40},{32,96},{40,56},{48,112},{56,8},{64,... | collective-permute-start | bytes 786440 | tf_op jit(solution)/shard_map/ppermute | solution.py:39
  180.6 10.6 %collective-permute-start.32 = (bf16[2,256,256]{2,1,0:T(8,128)(2,1)S(1)}, bf16[2,256,256]{2,1,0:T(8,128)(2,1)S(1)}, u32[]{:S(2)}, u32[]{:S(2)}) collective-permute-start(bf16[2,256,256]{2,1,0:T(8,128)(2,1)S(1)} %get-tuple-element.103), channel_id=1, source_target_pairs={{0,128},{8,40},{16,144},{24,56},{32,160},{40,8},{48,176},{56,24},{... | collective-permute-start | bytes 786440 | tf_op jit(solution)/shard_map/ppermute | solution.py:39
  184.2 7.1 %collective-permute-start.33 = (bf16[2,256,256]{2,1,0:T(8,128)(2,1)S(1)}, bf16[2,256,256]{2,1,0:T(8,128)(2,1)}, u32[]{:S(2)}, u32[]{:S(2)}) collective-permute-start(bf16[2,256,256]{2,1,0:T(8,128)(2,1)S(1)} %get-tuple-element.102), channel_id=1, source_target_pairs={{0,192},{8,56},{16,208},{24,8},{32,224},{40,24},{48,240},{56,40},{... | collective-permute-start | bytes 786440 | tf_op jit(solution)/shard_map/ppermute | solution.py:39
  192.3 4.5 %collective-permute-start.34 = (f32[2,128,256]{2,1,0:T(8,128)S(1)}, f32[2,128,256]{2,1,0:T(8,128)S(1)}, u32[]{:S(2)}, u32[]{:S(2)}) collective-permute-start(f32[2,128,256]{2,1,0:T(8,128)S(1)} %slice_select_fusion), channel_id=1, source_target_pairs={{0,8},{8,0},{16,24},{24,16},{32,40},{40,32},{48,56},{56,48},{64,72... | collective-permute-start | bytes 786440 | tf_op jit(solution)/shard_map/ppermute | solution.py:52
  198.7 20.7 %all-to-all-start = ((f32[32,8,512]{2,1,0:T(8,128)}), f32[32,8,512]{2,1,0:T(8,128)S(1)}, u32[]{:S(2)}, u32[]{:S(2)}) async-start(f32[32,8,512]{2,1,0:T(8,128)} %broadcast_in_dim.14), calls=%async_computation.1 | async-start | bytes 1048576 | tf_op jit(solution)/shard_map/all_to_all | solution.py:526
  206.3 2.8 %collective-permute-start.35 = (f32[1,128]{1,0:T(1,128)S(1)}, f32[1,128]{1,0:T(1,128)S(1)}, u32[]{:S(2)}, u32[]{:S(2)}) collective-permute-start(f32[1,128]{1,0:T(1,128)S(1)} %bitcast.86), channel_id=1, source_target_pairs={{0,1},{1,0},{2,3},{3,2},{4,5},{5,4},{6,7},{7,6},{8,9},{9,8},{10,11... | collective-permute-start | bytes 1544 | tf_op jit(solution)/shard_map/ppermute | solution.py:64
  209.1 3.6 %collective-permute-start.36 = (f32[1,128]{1,0:T(1,128)S(1)}, f32[1,128]{1,0:T(1,128)S(1)}, u32[]{:S(2)}, u32[]{:S(2)}) collective-permute-start(f32[1,128]{1,0:T(1,128)S(1)} %bitcast_add_fusion), channel_id=1, source_target_pairs={{0,2},{1,3},{2,0},{3,1},{4,6},{5,7},{6,4},{7,5},{8,10},{9,11},{10,... | collective-permute-start | bytes 1544 | tf_op jit(solution)/shard_map/ppermute | solution.py:64
  212.7 6.3 %collective-permute-start.37 = (f32[1,128]{1,0:T(1,128)S(1)}, f32[1,128]{1,0:T(1,128)S(1)}, u32[]{:S(2)}, u32[]{:S(2)}) collective-permute-start(f32[1,128]{1,0:T(1,128)S(1)} %add.187), channel_id=1, source_target_pairs={{0,4},{1,5},{2,6},{3,7},{4,0},{5,1},{6,2},{7,3},{8,12},{9,13},{10,... | collective-permute-start | bytes 1544 | tf_op jit(solution)/shard_map/ppermute | solution.py:64
  (4 other events, 2.6 us)
Sparse Core Ops, SparseCore 0:
  11.1 62.7 all-gather.1
  155.4 34.6 reduce-scatter.1

commit v4 on v2

--- a/solution.py
+++ b/solution.py
@@ -58,6 +58,10 @@
 
 def z_hop(v, d):
     return lax.ppermute(v, "tp", [(z, (z + d) % NZ) for z in range(NZ)])
+
+
+def z_xor(v, b):
+    return lax.ppermute(v, "tp", [(z, z ^ b) for z in range(NZ)])
 
 
 def after(v, other):
@@ -264,12 +268,11 @@
 
 
 def each_z(step):
-    def two(i, _):
-        step(2 * i)
-        step(2 * i + 1)
+    def one(k, _):
+        step(k)
         return 0
 
-    lax.fori_loop(0, NZ // 2, two, 0)
+    lax.fori_loop(0, NZ, one, 0)
 
 
 def project_body(pos, *refs):
@@ -639,7 +642,9 @@
     in_sum = jnp.sum(in_total * in_slopes, axis=0)[None]
     out_sum = jnp.sum(out_total * out_slopes, axis=1)[None]
     in_sum = everyones(in_sum, "seq", NY * NX * NC, 8)
-    out_sum = everyones(out_sum, "tp", NZ, 1)
+    for bits in (1, 2, 4):
+        out_sum = out_sum + z_xor(out_sum, bits)
+    out_sum = out_sum[0]
     return (
         grad_tokens,
         in_total * in_inside,

time: 228 us -> 218 us (0.956)
  blocking collectives: 11.9 us -> 0 us
  starting transfers between devices: 65.5 us -> 71.9 us
  waiting for transfers between devices: 69.3 us -> 63.1 us
    all_to_all x1 -> x0, blocking collectives: 11.9 us -> none  [everyones(): return jnp.sum(lax.all_to_all(parts, axis, 0, 0, tiled=True)[:, 0], axis=0)]
    all_to_all x1, waiting for transfers between devices: 11 us -> 0.01 us  [everyones(): return jnp.sum(lax.all_to_all(parts, axis, 0, 0, tiled=True)[:, 0], axis=0)]
    ppermute x0 -> x3, starting transfers between devices: none -> 7.89 us  [z_xor(): return lax.ppermute(v, 'tp', [(z, z ^ b) for z in range(NZ)])]
    ppermute x0 -> x3, waiting for transfers between devices: none -> 4.77 us  [z_xor(): return lax.ppermute(v, 'tp', [(z, z ^ b) for z in range(NZ)])]
  transfers between devices with their start and end apart: 40 -> 43, of which waited for: 19 -> 22; matrix products, arithmetic and copies ran while one was open for 4% -> 4% of each run, Pallas kernels for 10% -> 11%
where the time goes in v4:
time: 218 us; the launch traced here: 216 us
  starting transfers between devices  71.9 us (33%)
  waiting for transfers between devices  63.1 us (29%)
  Pallas kernels  46.4 us (21%)
  between operations  14.5 us (7%)
  other arithmetic  11.5 us (5%)
  local copies, waits for them, and re-layouts  8.09 us (4%)
    pallas_call x11, Pallas kernels, call(): pl.pallas_call(body, out_shape=outs, in_specs=[smem] + [anyw] * away + [v...  46.4 us
    ppermute x13, waiting for transfers between devices, hop(): return lax.ppermute(v, 'seq', pairs)  30 us
    ppermute x8, waiting for transfers between devices, z_hop(): return lax.ppermute(v, 'tp', [(z, (z + d) % NZ) for z in range(NZ)])  17.8 us
    ppermute x13, starting transfers between devices, hop(): return lax.ppermute(v, 'seq', pairs)  16.7 us
    ppermute x10, starting transfers between devices, seq_xor(): return lax.ppermute(v, 'seq', [(s, s ^ bits) for s in range(NY * NX * NC)])  15.6 us
    ppermute x8, starting transfers between devices, z_hop(): return lax.ppermute(v, 'tp', [(z, (z + d) % NZ) for z in range(NZ)])  15.6 us
    ppermute x6, starting transfers between devices, axis_hop(): return lax.ppermute(v, 'seq', pairs)  8.51 us
    ppermute x3, starting transfers between devices, z_xor(): return lax.ppermute(v, 'tp', [(z, z ^ b) for z in range(NZ)])  7.89 us
  transfers between devices with their start and end apart: 43, of which 22 were waited for; matrix products, arithmetic and copies ran while one was open for 4% of the time, Pallas kernels for 11%

profile of v4, /device:TPU:1, one launch (start us, length us, event | category | flops | bytes accessed | tf_op | source)
XLA Modules:
  0.0 215.5 jit_solution(8530361251782726753)
XLA Ops:
  7.8 2.6 %prep.1 = (bf16[512,512]{1,0:T(8,128)(2,1)}, bf16[144,256]{1,0:T(8,128)(2,1)}, bf16[144,256]{1,0:T(8,128)(2,1)}, bf16[128,512]{1,0:T(8,128)(2,1)}, f32[256,8]{1,...) custom-call(s32[4]{0:T(128)} %pad_add_fusion.pos, ...), custom_call_target="tpu_custom_call" | custom-call | flops 1000000 | bytes 2058256 | tf_op jit(solution)/shard_map/prep/pallas_call | solution.py:96
  10.6 2.5 %collective-permute-start.3 = (bf16[512,512]{1,0:T(8,128)(2,1)}, bf16[512,512]{1,0:T(8,128)(2,1)S(1)}, u32[]{:S(2)}, u32[]{:S(2)}) collective-permute-start(bf16[512,512]{1,0:T(8,128)(2,1)} %get-tuple-element.44.refs_0_), channel_id=1, source_target_pairs={{0,1},{1,2},{2,3},{3,4},{4,5},{5,6},{6,7},{7,0},{8,9},{9,10},{10,1... | collective-permute-start | bytes 1572872 | tf_op jit(solution)/shard_map/ppermute | solution.py:60
  13.1 1.0 collective-permute-start.8
  14.0 3.8 %collective-permute-start = (bf16[512,512]{1,0:T(8,128)(2,1)}, bf16[512,512]{1,0:T(8,128)(2,1)S(1)}, u32[]{:S(2)}, u32[]{:S(2)}) collective-permute-start(bf16[512,512]{1,0:T(8,128)(2,1)} %get-tuple-element.44.refs_0_), channel_id=1, source_target_pairs={{0,7},{1,0},{2,1},{3,2},{4,3},{5,4},{6,5},{7,6},{8,15},{9,8},{10,9... | collective-permute-start | bytes 1572872 | tf_op jit(solution)/shard_map/ppermute | solution.py:60
  17.8 0.9 fusion.22
  18.7 2.8 %collective-permute-start.9 = (bf16[2,144,256]{2,1,0:T(8,128)(2,1)S(1)}, bf16[2,144,256]{2,1,0:T(8,128)(2,1)S(1)}, u32[]{:S(2)}, u32[]{:S(2)}) collective-permute-start(bf16[2,144,256]{2,1,0:T(8,128)(2,1)S(1)} %get-tuple-element.103), channel_id=1, source_target_pairs={{0,48},{8,200},{16,0},{24,216},{32,16},{40,232},{48,32},{56,248},{... | collective-permute-start | bytes 442376 | tf_op jit(solution)/shard_map/ppermute | solution.py:39
  22.6 6.3 %collective-permute-done.3.refs_6_ = bf16[512,512]{1,0:T(8,128)(2,1)S(1)} collective-permute-done((bf16[512,512]{1,0:T(8,128)(2,1)}, bf16[512,512]{1,0:T(8,128)(2,1)S(1)}, u32[]{:S(2)}, u32[]{:S(2)}) %collective-permute-start.3) | collective-permute-done | bytes 524320 | tf_op jit(solution)/shard_map/ppermute | solution.py:60
  29.0 2.6 %collective-permute-start.12 = (bf16[4,2,144,256]{3,2,1,0:T(8,128)(2,1)S(1)}, bf16[4,2,144,256]{3,2,1,0:T(8,128)(2,1)S(1)}, u32[]{:S(2)}, u32[]{:S(2)}) collective-permute-start(bf16[4,2,144,256]{3,2,1,0:T(8,128)(2,1)S(1)} %pad_maximum_fusion.refs_0_), channel_id=1, source_target_pairs={{0,192},{8,56},{16,208},{24,8},{32,224},{40,24},{48,240},{56,40},{... | collective-permute-start | bytes 1769480 | tf_op jit(solution)/shard_map/ppermute | solution.py:39
  31.6 2.7 %collective-permute-start.1 = (bf16[512,512]{1,0:T(8,128)(2,1)S(1)}, bf16[512,512]{1,0:T(8,128)(2,1)S(1)}, u32[]{:S(2)}, u32[]{:S(2)}) collective-permute-start(bf16[512,512]{1,0:T(8,128)(2,1)S(1)} %collective-permute-done.refs_1_), channel_id=1, source_target_pairs={{0,7},{1,0},{2,1},{3,2},{4,3},{5,4},{6,5},{7,6},{8,15},{9,8},{10,9... | collective-permute-start | bytes 1572872 | tf_op jit(solution)/shard_map/ppermute | solution.py:60
  34.2 1.2 collective-permute-start.13
  35.8 6.6 %collective-permute-done.4.refs_5_ = bf16[512,512]{1,0:T(8,128)(2,1)S(1)} collective-permute-done((bf16[512,512]{1,0:T(8,128)(2,1)S(1)}, bf16[512,512]{1,0:T(8,128)(2,1)S(1)}, u32[]{:S(2)}, u32[]{:S(2)}) %collective-permute-start.4) | collective-permute-done | bytes 524320 | tf_op jit(solution)/shard_map/ppermute | solution.py:60
  42.4 3.7 %collective-permute-done.12.refs_1_ = bf16[4,2,144,256]{3,2,1,0:T(8,128)(2,1)S(1)} collective-permute-done((bf16[4,2,144,256]{3,2,1,0:T(8,128)(2,1)S(1)}, bf16[4,2,144,256]{3,2,1,0:T(8,128)(2,1)S(1)}, u32[]{:S(2)}, u32[]{:S(2)}) %collective-permute-start.12) | collective-permute-done | bytes 589856 | tf_op jit(solution)/shard_map/ppermute | solution.py:39
  46.1 1.7 collective-permute-start.15
  47.8 3.0 %collective-permute-start.2 = (bf16[512,512]{1,0:T(8,128)(2,1)S(1)}, bf16[512,512]{1,0:T(8,128)(2,1)S(1)}, u32[]{:S(2)}, u32[]{:S(2)}) collective-permute-start(bf16[512,512]{1,0:T(8,128)(2,1)S(1)} %collective-permute-done.1.refs_2_), channel_id=1, source_target_pairs={{0,7},{1,0},{2,1},{3,2},{4,3},{5,4},{6,5},{7,6},{8,15},{9,8},{10,9... | collective-permute-start | bytes 1572872 | tf_op jit(solution)/shard_map/ppermute | solution.py:60
  51.5 2.7 %collective-permute-start.17 = (bf16[4,2,144,256]{3,2,1,0:T(8,128)(2,1)S(1)}, bf16[4,2,144,256]{3,2,1,0:T(8,128)(2,1)S(1)}, u32[]{:S(2)}, u32[]{:S(2)}) collective-permute-start(bf16[4,2,144,256]{3,2,1,0:T(8,128)(2,1)S(1)} %collective-permute-done.13.refs_2_), channel_id=1, source_target_pairs={{0,8},{8,0},{16,24},{24,16},{32,40},{40,32},{48,56},{56,48},{64,72... | collective-permute-start | bytes 1769480 | tf_op jit(solution)/shard_map/ppermute | solution.py:52
  55.0 3.0 %collective-permute-start.18 = (bf16[4,2,144,256]{3,2,1,0:T(8,128)(2,1)S(1)}, bf16[4,2,144,256]{3,2,1,0:T(8,128)(2,1)}, u32[]{:S(2)}, u32[]{:S(2)}) collective-permute-start(bf16[4,2,144,256]{3,2,1,0:T(8,128)(2,1)S(1)} %collective-permute-done.14.refs_3_), channel_id=1, source_target_pairs={{0,8},{8,0},{16,24},{24,16},{32,40},{40,32},{48,56},{56,48},{64,72... | collective-permute-start | bytes 1769480 | tf_op jit(solution)/shard_map/ppermute | solution.py:52
  58.0 4.1 %collective-permute-done.2.refs_3_ = bf16[512,512]{1,0:T(8,128)(2,1)S(1)} collective-permute-done((bf16[512,512]{1,0:T(8,128)(2,1)S(1)}, bf16[512,512]{1,0:T(8,128)(2,1)S(1)}, u32[]{:S(2)}, u32[]{:S(2)}) %collective-permute-start.2) | collective-permute-done | bytes 524320 | tf_op jit(solution)/shard_map/ppermute | solution.py:60
  62.3 3.4 %collective-permute-start.7 = (bf16[256,512]{1,0:T(8,128)(2,1)S(1)}, bf16[256,512]{1,0:T(8,128)(2,1)}, u32[]{:S(2)}, u32[]{:S(2)}) collective-permute-start(bf16[256,512]{1,0:T(8,128)(2,1)S(1)} %slice.120), channel_id=1, source_target_pairs={{0,7},{1,0},{2,1},{3,2},{4,3},{5,4},{6,5},{7,6},{8,15},{9,8},{10,9... | collective-permute-start | bytes 786440 | tf_op jit(solution)/shard_map/ppermute | solution.py:60
  65.8 0.8 copy-done.14
  66.7 5.3 %assemble.1 = (bf16[4096,512]{1,0:T(8,128)(2,1)}, f32[24,256]{1,0:T(8,128)}) custom-call(s32[4]{0:T(128)} %pad_add_fusion.pos, bf16[4,2,144,256]{3,2,1,0:T(8,128)(2,1)} %copy-done.6, bf16[4,2,144,256]{3,2,1,0:T(8,128)(2,1)} %copy-done.10, bf16[4,2,144,256]{3,2,1,0:T(8,128)(2,1)} %copy-done.11, bf16[4,2,144,256]{3,2,1,0:T(8,128)(2,1)} %copy-done.12, ...), custom_call_target="tpu_custom_call" | custom-call | flops 1000000 | bytes 8937488 | tf_op jit(solution)/shard_map/assemble/pallas_call | solution.py:96
  72.1 1.9 all-gather.2.cloned.1.call-done.refs_10_.w_in
  74.0 9.4 %project.1 = (bf16[256,512]{1,0:T(8,128)(2,1)}, bf16[256,512]{1,0:T(8,128)(2,1)}, bf16[4,128,128]{2,1,0:T(8,128)(2,1)}, bf16[4,128,128]{2,1,0:T(8,128)(2,1)}) custom-call(s32[4]{0:T(128)} %pad_add_fusion.pos, bf16[512,512]{1,0:T(8,128)(2,1)} %get-tuple-element.44.refs_0_, bf16[512,512]{1,0:T(8,128)(2,1)} %copy-done.3, bf16[512,512]{1,0:T(8,128)(2,1)} %copy-done.5, ...), custom_call_target="tpu_custom_call" | custom-call | flops 2147483648 | bytes 13649936 | tf_op jit(solution)/shard_map/project/pallas_call | solution.py:96
  83.8 1.3 collective-permute-done.19.other
  85.7 1.7 join_chip.1.q
  87.4 0.9 collective-permute-start.20
  88.3 2.4 %collective-permute-start.21 = (bf16[4,128,128]{2,1,0:T(8,128)(2,1)}, bf16[4,128,128]{2,1,0:T(8,128)(2,1)S(1)}, u32[]{:S(2)}, u32[]{:S(2)}) collective-permute-start(bf16[4,128,128]{2,1,0:T(8,128)(2,1)} %join_chip.1.q), channel_id=1, source_target_pairs={{0,32},{8,40},{16,48},{24,56},{32,0},{40,8},{48,16},{56,24},{64,96... | collective-permute-start | bytes 393224 | tf_op jit(solution)/shard_map/ppermute | solution.py:48
  90.6 1.0 collective-permute-start.22
  91.6 2.5 %grad_local.1.refs_9_ = f32[256,512]{1,0:T(8,128)} custom-call(s32[4]{0:T(128)} %pad_add_fusion.pos, bf16[256,512]{1,0:T(8,128)(2,1)} %get-tuple-element.55.vals, bf16[256,128]{1,0:T(8,128)(2,1)} %refs_10_.2, bf16[256,128]{1,0:T(8,128)(2,1)} %refs_10_.3, f32[256,8]{1,0:T(8,128)} %get-tuple-element.56.a_ref, f32[8,256]{1,0:T(8,128)} %get-tuple-element.57.at_ref), custom_call_target="tpu_custom_call" | custom-call | flops 1000000000 | bytes 933904 | tf_op jit(solution)/shard_map/grad_local/pallas_call | solution.py:96
  94.2 2.9 %collective-permute-done.21.g2 = bf16[4,128,128]{2,1,0:T(8,128)(2,1)S(1)} collective-permute-done((bf16[4,128,128]{2,1,0:T(8,128)(2,1)}, bf16[4,128,128]{2,1,0:T(8,128)(2,1)S(1)}, u32[]{:S(2)}, u32[]{:S(2)}) %collective-permute-start.21) | collective-permute-done | bytes 131104 | tf_op jit(solution)/shard_map/ppermute | solution.py:48
  98.3 2.0 join_row.1
  100.4 4.2 %collective-permute-start.24 = (bf16[4,128,128]{2,1,0:T(8,128)(2,1)}, bf16[4,128,128]{2,1,0:T(8,128)(2,1)S(1)}, u32[]{:S(2)}, u32[]{:S(2)}) collective-permute-start(bf16[4,128,128]{2,1,0:T(8,128)(2,1)} %get-tuple-element.64), channel_id=1, source_target_pairs={{0,128},{8,136},{16,144},{24,152},{32,160},{40,168},{48,176},{56,1... | collective-permute-start | bytes 393224 | tf_op jit(solution)/shard_map/ppermute | solution.py:48
  104.6 2.5 %mixed_local.1.refs_9_ = f32[256,512]{1,0:T(8,128)} custom-call(s32[4]{0:T(128)} %pad_add_fusion.pos, bf16[256,512]{1,0:T(8,128)(2,1)} %get-tuple-element.65.vals, bf16[256,128]{1,0:T(8,128)(2,1)} %refs_10_.2, bf16[256,128]{1,0:T(8,128)(2,1)} %refs_10_.3, f32[256,8]{1,0:T(8,128)} %get-tuple-element.56.a_ref, f32[8,256]{1,0:T(8,128)} %get-tuple-element.57.at_ref), custom_call_target="tpu_custom_call" | custom-call | flops 1000000000 | bytes 933904 | tf_op jit(solution)/shard_map/mixed_local/pallas_call | solution.py:96
  107.1 2.5 %collective-permute-done.24.g2 = bf16[4,128,128]{2,1,0:T(8,128)(2,1)S(1)} collective-permute-done((bf16[4,128,128]{2,1,0:T(8,128)(2,1)}, bf16[4,128,128]{2,1,0:T(8,128)(2,1)S(1)}, u32[]{:S(2)}, u32[]{:S(2)}) %collective-permute-start.24) | collective-permute-done | bytes 131104 | tf_op jit(solution)/shard_map/ppermute | solution.py:48
  110.7 2.1 join_rows.1
  112.8 2.1 collective-permute-start.26
  114.9 1.2 collective-permute-done.26.refs_13_
  116.7 5.9 %out_parts.1 = (bf16[4,4,256,256]{3,2,1,0:T(8,128)(2,1)}, bf16[4,4,256,256]{3,2,1,0:T(8,128)(2,1)}) custom-call(s32[4]{0:T(128)} %pad_add_fusion.pos, bf16[512,512]{1,0:T(8,128)(2,1)} %get-tuple-element.44.refs_0_, bf16[512,512]{1,0:T(8,128)(2,1)} %copy-done.3, bf16[512,512]{1,0:T(8,128)(2,1)} %copy-done.5, bf16[512,512]{1,0:T(8,128)(2,1)} %copy-done.1, ...), custom_call_target="tpu_custom_call" | custom-call | flops 1073741824 | bytes 9248784 | tf_op jit(solution)/shard_map/out_parts/pallas_call | solution.py:96
  123.3 6.6 %in_parts.1 = (bf16[4,4,256,256]{3,2,1,0:T(8,128)(2,1)}, bf16[4,4,256,256]{3,2,1,0:T(8,128)(2,1)}, bf16[256,512]{1,0:T(8,128)(2,1)}) custom-call(s32[4]{0:T(128)} %pad_add_fusion.pos, bf16[512,512]{1,0:T(8,128)(2,1)} %get-tuple-element.44.refs_0_, bf16[512,512]{1,0:T(8,128)(2,1)} %copy-done.3, bf16[512,512]{1,0:T(8,128)(2,1)} %copy-done.5, ...), custom_call_target="tpu_custom_call" | custom-call | flops 1073741824 | bytes 9512976 | tf_op jit(solution)/shard_map/in_parts/pallas_call | solution.py:96
  130.2 5.7 %token_parts.1 = bf16[8,256,512]{2,1,0:T(8,128)(2,1)} custom-call(s32[4]{0:T(128)} %pad_add_fusion.pos, bf16[4096,512]{1,0:T(8,128)(2,1)} %all-gather.2.cloned.1.call-done.refs_10_.w_in, bf16[256,512]{1,0:T(8,128)(2,1)} %get-tuple-element.75.gs_ref), custom_call_target="tpu_custom_call" | custom-call | flops 1073741824 | bytes 6553616 | tf_op jit(solution)/shard_map/token_parts/pallas_call | solution.py:96
  135.9 1.4 copy-done.9
  137.3 2.8 %fusion = (bf16[4,1,256,256]{3,2,0,1:T(8,128)(2,1)S(1)}, bf16[4,1,256,256]{3,2,0,1:T(8,128)(2,1)S(1)}, bf16[4,1,256,256]{3,2,0,1:T(8,128)(2,1)S(1)}, bf16[4,1,25...) fusion(bf16[4,4,256,256]{3,2,1,0:T(8,128)(2,1)} %copy-done.9, ...), kind=kLoop, calls=%fused_computation.14 | loop fusion | flops 8388608 | bytes 12582912 | tf_op jit(solution)/shard_map/add | solution.py:496
  140.1 1.1 fusion.8
  141.2 2.7 %collective-permute-start.31 = (bf16[2,2,256,256]{3,2,0,1:T(8,128)(2,1)}, bf16[2,2,256,256]{3,2,0,1:T(8,128)(2,1)}, u32[]{:S(2)}, u32[]{:S(2)}) collective-permute-start(bf16[2,2,256,256]{3,2,0,1:T(8,128)(2,1)} %get-tuple-element.97), channel_id=1, source_target_pairs={{0,48},{8,200},{16,0},{24,216},{32,16},{40,232},{48,32},{56,248},{... | collective-permute-start | bytes 1572872 | tf_op jit(solution)/shard_map/ppermute | solution.py:39
  143.9 7.2 %collective-permute-done.29 = bf16[2,2,256,256]{3,2,0,1:T(8,128)(2,1)} collective-permute-done((bf16[2,2,256,256]{3,2,0,1:T(8,128)(2,1)}, bf16[2,2,256,256]{3,2,0,1:T(8,128)(2,1)}, u32[]{:S(2)}, u32[]{:S(2)}) %collective-permute-start.29) | collective-permute-done | bytes 524320 | tf_op jit(solution)/shard_map/ppermute | solution.py:39
  151.0 1.2 add_convert_fusion.1
  152.3 1.2 add_convert_fusion
  153.5 2.7 %collective-permute-start.32 = (bf16[4,2,256,256]{3,2,0,1:T(8,128)(2,1)S(1)}, bf16[4,2,256,256]{3,2,0,1:T(8,128)(2,1)S(1)}, u32[]{:S(2)}, u32[]{:S(2)}) collective-permute-start(bf16[4,2,256,256]{3,2,0,1:T(8,128)(2,1)S(1)} %add_convert_fusion), channel_id=1, source_target_pairs={{0,48},{8,200},{16,0},{24,216},{32,16},{40,232},{48,32},{56,248},{... | collective-permute-start | bytes 3145736 | tf_op jit(solution)/shard_map/ppermute | solution.py:39
  156.2 11.2 %collective-permute-done.30 = bf16[4,2,256,256]{3,2,0,1:T(8,128)(2,1)S(1)} collective-permute-done((bf16[4,2,256,256]{3,2,0,1:T(8,128)(2,1)S(1)}, bf16[4,2,256,256]{3,2,0,1:T(8,128)(2,1)S(1)}, u32[]{:S(2)}, u32[]{:S(2)}) %collective-permute-start.30) | collective-permute-done | bytes 1048608 | tf_op jit(solution)/shard_map/ppermute | solution.py:39
  169.2 2.6 %collective-permute-start.34 = (bf16[2,256,256]{2,1,0:T(8,128)(2,1)S(1)}, bf16[2,256,256]{2,1,0:T(8,128)(2,1)S(1)}, u32[]{:S(2)}, u32[]{:S(2)}) collective-permute-start(bf16[2,256,256]{2,1,0:T(8,128)(2,1)S(1)} %get-tuple-element.95), channel_id=1, source_target_pairs={{0,128},{8,40},{16,144},{24,56},{32,160},{40,8},{48,176},{56,24},{... | collective-permute-start | bytes 786440 | tf_op jit(solution)/shard_map/ppermute | solution.py:39
  172.5 3.8 %collective-permute-done.33 = bf16[2,256,256]{2,1,0:T(8,128)(2,1)S(1)} collective-permute-done((bf16[2,256,256]{2,1,0:T(8,128)(2,1)}, bf16[2,256,256]{2,1,0:T(8,128)(2,1)S(1)}, u32[]{:S(2)}, u32[]{:S(2)}) %collective-permute-start.33) | collective-permute-done | bytes 262176 | tf_op jit(solution)/shard_map/ppermute | solution.py:39
  176.2 2.4 %collective-permute-done.34 = bf16[2,256,256]{2,1,0:T(8,128)(2,1)S(1)} collective-permute-done((bf16[2,256,256]{2,1,0:T(8,128)(2,1)S(1)}, bf16[2,256,256]{2,1,0:T(8,128)(2,1)S(1)}, u32[]{:S(2)}, u32[]{:S(2)}) %collective-permute-start.34) | collective-permute-done | bytes 262176 | tf_op jit(solution)/shard_map/ppermute | solution.py:39
  178.6 0.8 collective-permute-done.35
  179.5 1.1 fusion.11
  180.6 3.6 %collective-permute-start.36 = (f32[2,128,256]{2,1,0:T(8,128)S(1)}, f32[2,128,256]{2,1,0:T(8,128)S(1)}, u32[]{:S(2)}, u32[]{:S(2)}) collective-permute-start(f32[2,128,256]{2,1,0:T(8,128)S(1)} %slice_select_fusion), channel_id=1, source_target_pairs={{0,8},{8,0},{16,24},{24,16},{32,40},{40,32},{48,56},{56,48},{64,72... | collective-permute-start | bytes 786440 | tf_op jit(solution)/shard_map/ppermute | solution.py:52
  184.2 0.8 dynamic_slice.3
  185.4 1.0 fusion.15
  186.4 0.9 broadcast_in_dim.14
  187.3 7.6 %all-to-all-start = ((f32[32,8,512]{2,1,0:T(8,128)}), f32[32,8,512]{2,1,0:T(8,128)S(1)}, u32[]{:S(2)}, u32[]{:S(2)}) async-start(f32[32,8,512]{2,1,0:T(8,128)} %broadcast_in_dim.14), calls=%async_computation.1 | async-start | bytes 1048576 | tf_op jit(solution)/shard_map/all_to_all | solution.py:525
  194.9 1.2 collective-permute-start.37
  196.1 1.5 collective-permute-done.37
  197.7 2.2 %collective-permute-start.38 = (f32[1,128]{1,0:T(1,128)S(1)}, f32[1,128]{1,0:T(1,128)S(1)}, u32[]{:S(2)}, u32[]{:S(2)}) collective-permute-start(f32[1,128]{1,0:T(1,128)S(1)} %bitcast_add_fusion), channel_id=1, source_target_pairs={{0,2},{1,3},{2,0},{3,1},{4,6},{5,7},{6,4},{7,5},{8,10},{9,11},{10,... | collective-permute-start | bytes 1544 | tf_op jit(solution)/shard_map/ppermute | solution.py:64
  199.9 1.4 collective-permute-done.38
  201.2 4.4 %collective-permute-start.39 = (f32[1,128]{1,0:T(1,128)S(1)}, f32[1,128]{1,0:T(1,128)S(1)}, u32[]{:S(2)}, u32[]{:S(2)}) collective-permute-start(f32[1,128]{1,0:T(1,128)S(1)} %add.187), channel_id=1, source_target_pairs={{0,4},{1,5},{2,6},{3,7},{4,0},{5,1},{6,2},{7,3},{8,12},{9,13},{10,... | collective-permute-start | bytes 1544 | tf_op jit(solution)/shard_map/ppermute | solution.py:64
  205.7 1.9 collective-permute-done.39
  (111 shorter events, 13.2 us)
Async XLA Ops:
  7.2 66.8 %all-gather.2.cloned.1.call-start = ((), (), s32[]{:S(2)}) async-start(), calls=%async_computation.2 | async-start | bytes 4325376 | tf_op jit(solution)/shard_map/all_gather | solution.py:556
  10.5 198.2 %reduce-scatter.2.cloned.1.call-start = ((), (), s32[]{:S(2)}) async-start(), calls=%async_computation.3 | async-start | bytes 2359296 | tf_op jit(solution)/shard_map/reduce_scatter | solution.py:633
  10.6 18.3 %collective-permute-start.3 = (bf16[512,512]{1,0:T(8,128)(2,1)}, bf16[512,512]{1,0:T(8,128)(2,1)S(1)}, u32[]{:S(2)}, u32[]{:S(2)}) collective-permute-start(bf16[512,512]{1,0:T(8,128)(2,1)} %get-tuple-element.44.refs_0_), channel_id=1, source_target_pairs={{0,1},{1,2},{2,3},{3,4},{4,5},{5,6},{6,7},{7,0},{8,9},{9,10},{10,1... | collective-permute-start | bytes 1572872 | tf_op jit(solution)/shard_map/ppermute | solution.py:60
  13.1 4.7 %collective-permute-start.8 = (bf16[144,256]{1,0:T(8,128)(2,1)}, bf16[144,256]{1,0:T(8,128)(2,1)S(1)}, u32[]{:S(2)}, u32[]{:S(2)}) collective-permute-start(bf16[144,256]{1,0:T(8,128)(2,1)} %get-tuple-element.46), channel_id=1, source_target_pairs={{0,8},{8,0},{16,24},{24,16},{32,40},{40,32},{48,56},{56,48},{64,72... | collective-permute-start | bytes 221192 | tf_op jit(solution)/shard_map/ppermute | solution.py:52
  14.0 17.5 %collective-permute-start = (bf16[512,512]{1,0:T(8,128)(2,1)}, bf16[512,512]{1,0:T(8,128)(2,1)S(1)}, u32[]{:S(2)}, u32[]{:S(2)}) collective-permute-start(bf16[512,512]{1,0:T(8,128)(2,1)} %get-tuple-element.44.refs_0_), channel_id=1, source_target_pairs={{0,7},{1,0},{2,1},{3,2},{4,3},{5,4},{6,5},{7,6},{8,15},{9,8},{10,9... | collective-permute-start | bytes 1572872 | tf_op jit(solution)/shard_map/ppermute | solution.py:60
  18.7 10.2 %collective-permute-start.9 = (bf16[2,144,256]{2,1,0:T(8,128)(2,1)S(1)}, bf16[2,144,256]{2,1,0:T(8,128)(2,1)S(1)}, u32[]{:S(2)}, u32[]{:S(2)}) collective-permute-start(bf16[2,144,256]{2,1,0:T(8,128)(2,1)S(1)} %get-tuple-element.103), channel_id=1, source_target_pairs={{0,48},{8,200},{16,0},{24,216},{32,16},{40,232},{48,32},{56,248},{... | collective-permute-start | bytes 442376 | tf_op jit(solution)/shard_map/ppermute | solution.py:39
  21.5 7.4 %collective-permute-start.10 = (bf16[2,144,256]{2,1,0:T(8,128)(2,1)S(1)}, bf16[2,144,256]{2,1,0:T(8,128)(2,1)S(1)}, u32[]{:S(2)}, u32[]{:S(2)}) collective-permute-start(bf16[2,144,256]{2,1,0:T(8,128)(2,1)S(1)} %get-tuple-element.103), channel_id=1, source_target_pairs={{0,32},{8,136},{16,48},{24,152},{32,0},{40,168},{48,16},{56,184},{... | collective-permute-start | bytes 442376 | tf_op jit(solution)/shard_map/ppermute | solution.py:39
  21.9 7.0 %collective-permute-start.11 = (bf16[2,144,256]{2,1,0:T(8,128)(2,1)S(1)}, bf16[2,144,256]{2,1,0:T(8,128)(2,1)S(1)}, u32[]{:S(2)}, u32[]{:S(2)}) collective-permute-start(bf16[2,144,256]{2,1,0:T(8,128)(2,1)S(1)} %get-tuple-element.103), channel_id=1, source_target_pairs={{0,16},{8,72},{16,32},{24,88},{32,48},{40,104},{48,0},{56,120},{64... | collective-permute-start | bytes 442376 | tf_op jit(solution)/shard_map/ppermute | solution.py:39
  28.9 43.1 %copy-start.2 = (bf16[512,512]{1,0:T(8,128)(2,1)}, bf16[512,512]{1,0:T(8,128)(2,1)S(1)}, u32[]{:S(2)}) copy-start(bf16[512,512]{1,0:T(8,128)(2,1)S(1)} %collective-permute-done.3.refs_6_) | copy-start | bytes 1572868
  28.9 13.5 %collective-permute-start.4 = (bf16[512,512]{1,0:T(8,128)(2,1)S(1)}, bf16[512,512]{1,0:T(8,128)(2,1)S(1)}, u32[]{:S(2)}, u32[]{:S(2)}) collective-permute-start(bf16[512,512]{1,0:T(8,128)(2,1)S(1)} %collective-permute-done.3.refs_6_), channel_id=1, source_target_pairs={{0,1},{1,2},{2,3},{3,4},{4,5},{5,6},{6,7},{7,0},{8,9},{9,10},{10,1... | collective-permute-start | bytes 1572872 | tf_op jit(solution)/shard_map/ppermute | solution.py:60
  29.0 36.7 %copy-start.6 = (bf16[4,2,144,256]{3,2,1,0:T(8,128)(2,1)}, bf16[4,2,144,256]{3,2,1,0:T(8,128)(2,1)S(1)}, u32[]{:S(2)}) copy-start(bf16[4,2,144,256]{3,2,1,0:T(8,128)(2,1)S(1)} %pad_maximum_fusion.refs_0_) | copy-start | bytes 1769476
  29.0 17.1 %collective-permute-start.12 = (bf16[4,2,144,256]{3,2,1,0:T(8,128)(2,1)S(1)}, bf16[4,2,144,256]{3,2,1,0:T(8,128)(2,1)S(1)}, u32[]{:S(2)}, u32[]{:S(2)}) collective-permute-start(bf16[4,2,144,256]{3,2,1,0:T(8,128)(2,1)S(1)} %pad_maximum_fusion.refs_0_), channel_id=1, source_target_pairs={{0,192},{8,56},{16,208},{24,8},{32,224},{40,24},{48,240},{56,40},{... | collective-permute-start | bytes 1769480 | tf_op jit(solution)/shard_map/ppermute | solution.py:39
  31.6 40.5 %copy-start.3 = (bf16[512,512]{1,0:T(8,128)(2,1)}, bf16[512,512]{1,0:T(8,128)(2,1)S(1)}, u32[]{:S(2)}) copy-start(bf16[512,512]{1,0:T(8,128)(2,1)S(1)} %collective-permute-done.refs_1_) | copy-start | bytes 1572868
  31.6 16.2 %collective-permute-start.1 = (bf16[512,512]{1,0:T(8,128)(2,1)S(1)}, bf16[512,512]{1,0:T(8,128)(2,1)S(1)}, u32[]{:S(2)}, u32[]{:S(2)}) collective-permute-start(bf16[512,512]{1,0:T(8,128)(2,1)S(1)} %collective-permute-done.refs_1_), channel_id=1, source_target_pairs={{0,7},{1,0},{2,1},{3,2},{4,3},{5,4},{6,5},{7,6},{8,15},{9,8},{10,9... | collective-permute-start | bytes 1572872 | tf_op jit(solution)/shard_map/ppermute | solution.py:60
  34.2 16.6 %collective-permute-start.13 = (bf16[4,2,144,256]{3,2,1,0:T(8,128)(2,1)S(1)}, bf16[4,2,144,256]{3,2,1,0:T(8,128)(2,1)S(1)}, u32[]{:S(2)}, u32[]{:S(2)}) collective-permute-start(bf16[4,2,144,256]{3,2,1,0:T(8,128)(2,1)S(1)} %pad_maximum_fusion.refs_0_), channel_id=1, source_target_pairs={{0,128},{8,40},{16,144},{24,56},{32,160},{40,8},{48,176},{56,24},{... | collective-permute-start | bytes 1769480 | tf_op jit(solution)/shard_map/ppermute | solution.py:39
  35.5 16.1 %collective-permute-start.14 = (bf16[4,2,144,256]{3,2,1,0:T(8,128)(2,1)S(1)}, bf16[4,2,144,256]{3,2,1,0:T(8,128)(2,1)S(1)}, u32[]{:S(2)}, u32[]{:S(2)}) collective-permute-start(bf16[4,2,144,256]{3,2,1,0:T(8,128)(2,1)S(1)} %pad_maximum_fusion.refs_0_), channel_id=1, source_target_pairs={{0,64},{8,24},{16,80},{24,40},{32,96},{40,56},{48,112},{56,8},{64,... | collective-permute-start | bytes 1769480 | tf_op jit(solution)/shard_map/ppermute | solution.py:39
  42.4 29.6 %copy-start.4 = (bf16[512,512]{1,0:T(8,128)(2,1)}, bf16[512,512]{1,0:T(8,128)(2,1)S(1)}, u32[]{:S(2)}) copy-start(bf16[512,512]{1,0:T(8,128)(2,1)S(1)} %collective-permute-done.4.refs_5_) | copy-start | bytes 1572868
  42.4 12.6 %collective-permute-start.5 = (bf16[512,512]{1,0:T(8,128)(2,1)S(1)}, bf16[512,512]{1,0:T(8,128)(2,1)S(1)}, u32[]{:S(2)}, u32[]{:S(2)}) collective-permute-start(bf16[512,512]{1,0:T(8,128)(2,1)S(1)} %collective-permute-done.4.refs_5_), channel_id=1, source_target_pairs={{0,1},{1,2},{2,3},{3,4},{4,5},{5,6},{6,7},{7,0},{8,9},{9,10},{10,1... | collective-permute-start | bytes 1572872 | tf_op jit(solution)/shard_map/ppermute | solution.py:60
  46.1 19.6 %copy-start.10 = (bf16[4,2,144,256]{3,2,1,0:T(8,128)(2,1)}, bf16[4,2,144,256]{3,2,1,0:T(8,128)(2,1)S(1)}, u32[]{:S(2)}) copy-start(bf16[4,2,144,256]{3,2,1,0:T(8,128)(2,1)S(1)} %collective-permute-done.12.refs_1_) | copy-start | bytes 1769476
  46.1 16.2 %collective-permute-start.15 = (bf16[4,2,144,256]{3,2,1,0:T(8,128)(2,1)S(1)}, bf16[4,2,144,256]{3,2,1,0:T(8,128)(2,1)S(1)}, u32[]{:S(2)}, u32[]{:S(2)}) collective-permute-start(bf16[4,2,144,256]{3,2,1,0:T(8,128)(2,1)S(1)} %pad_maximum_fusion.refs_0_), channel_id=1, source_target_pairs={{0,8},{8,0},{16,24},{24,16},{32,40},{40,32},{48,56},{56,48},{64,72... | collective-permute-start | bytes 1769480 | tf_op jit(solution)/shard_map/ppermute | solution.py:52
  47.8 24.2 %copy-start.5 = (bf16[512,512]{1,0:T(8,128)(2,1)}, bf16[512,512]{1,0:T(8,128)(2,1)S(1)}, u32[]{:S(2)}) copy-start(bf16[512,512]{1,0:T(8,128)(2,1)S(1)} %collective-permute-done.1.refs_2_) | copy-start | bytes 1572868
  47.8 14.3 %collective-permute-start.2 = (bf16[512,512]{1,0:T(8,128)(2,1)S(1)}, bf16[512,512]{1,0:T(8,128)(2,1)S(1)}, u32[]{:S(2)}, u32[]{:S(2)}) collective-permute-start(bf16[512,512]{1,0:T(8,128)(2,1)S(1)} %collective-permute-done.1.refs_2_), channel_id=1, source_target_pairs={{0,7},{1,0},{2,1},{3,2},{4,3},{5,4},{6,5},{7,6},{8,15},{9,8},{10,9... | collective-permute-start | bytes 1572872 | tf_op jit(solution)/shard_map/ppermute | solution.py:60
  50.8 15.0 %copy-start.11 = (bf16[4,2,144,256]{3,2,1,0:T(8,128)(2,1)}, bf16[4,2,144,256]{3,2,1,0:T(8,128)(2,1)S(1)}, u32[]{:S(2)}) copy-start(bf16[4,2,144,256]{3,2,1,0:T(8,128)(2,1)S(1)} %collective-permute-done.13.refs_2_) | copy-start | bytes 1769476
  50.8 14.9 %collective-permute-start.16 = (bf16[4,2,144,256]{3,2,1,0:T(8,128)(2,1)S(1)}, bf16[4,2,144,256]{3,2,1,0:T(8,128)(2,1)S(1)}, u32[]{:S(2)}, u32[]{:S(2)}) collective-permute-start(bf16[4,2,144,256]{3,2,1,0:T(8,128)(2,1)S(1)} %collective-permute-done.12.refs_1_), channel_id=1, source_target_pairs={{0,8},{8,0},{16,24},{24,16},{32,40},{40,32},{48,56},{56,48},{64,72... | collective-permute-start | bytes 1769480 | tf_op jit(solution)/shard_map/ppermute | solution.py:52
  51.5 14.2 %copy-start.12 = (bf16[4,2,144,256]{3,2,1,0:T(8,128)(2,1)}, bf16[4,2,144,256]{3,2,1,0:T(8,128)(2,1)S(1)}, u32[]{:S(2)}) copy-start(bf16[4,2,144,256]{3,2,1,0:T(8,128)(2,1)S(1)} %collective-permute-done.14.refs_3_) | copy-start | bytes 1769476
  51.5 14.2 %collective-permute-start.17 = (bf16[4,2,144,256]{3,2,1,0:T(8,128)(2,1)S(1)}, bf16[4,2,144,256]{3,2,1,0:T(8,128)(2,1)S(1)}, u32[]{:S(2)}, u32[]{:S(2)}) collective-permute-start(bf16[4,2,144,256]{3,2,1,0:T(8,128)(2,1)S(1)} %collective-permute-done.13.refs_2_), channel_id=1, source_target_pairs={{0,8},{8,0},{16,24},{24,16},{32,40},{40,32},{48,56},{56,48},{64,72... | collective-permute-start | bytes 1769480 | tf_op jit(solution)/shard_map/ppermute | solution.py:52
  55.0 17.1 %copy-start = (bf16[512,512]{1,0:T(8,128)(2,1)}, bf16[512,512]{1,0:T(8,128)(2,1)S(1)}, u32[]{:S(2)}) copy-start(bf16[512,512]{1,0:T(8,128)(2,1)S(1)} %collective-permute-done.5.refs_4_) | copy-start | bytes 1572868
  55.0 10.8 %collective-permute-start.18 = (bf16[4,2,144,256]{3,2,1,0:T(8,128)(2,1)S(1)}, bf16[4,2,144,256]{3,2,1,0:T(8,128)(2,1)}, u32[]{:S(2)}, u32[]{:S(2)}) collective-permute-start(bf16[4,2,144,256]{3,2,1,0:T(8,128)(2,1)S(1)} %collective-permute-done.14.refs_3_), channel_id=1, source_target_pairs={{0,8},{8,0},{16,24},{24,16},{32,40},{40,32},{48,56},{56,48},{64,72... | collective-permute-start | bytes 1769480 | tf_op jit(solution)/shard_map/ppermute | solution.py:52
  62.1 10.0 %copy-start.1 = (bf16[512,512]{1,0:T(8,128)(2,1)}, bf16[512,512]{1,0:T(8,128)(2,1)S(1)}, u32[]{:S(2)}) copy-start(bf16[512,512]{1,0:T(8,128)(2,1)S(1)} %collective-permute-done.2.refs_3_) | copy-start | bytes 1572868
  62.1 10.0 %collective-permute-start.6 = (bf16[256,512]{1,0:T(8,128)(2,1)S(1)}, bf16[256,512]{1,0:T(8,128)(2,1)S(1)}, u32[]{:S(2)}, u32[]{:S(2)}) collective-permute-start(bf16[256,512]{1,0:T(8,128)(2,1)S(1)} %slice.119), channel_id=1, source_target_pairs={{0,1},{1,2},{2,3},{3,4},{4,5},{5,6},{6,7},{7,0},{8,9},{9,10},{10,1... | collective-permute-start | bytes 786440 | tf_op jit(solution)/shard_map/ppermute | solution.py:60
  62.3 3.5 %copy-start.13 = (bf16[4,2,144,256]{3,2,1,0:T(8,128)(2,1)}, bf16[4,2,144,256]{3,2,1,0:T(8,128)(2,1)S(1)}, u32[]{:S(2)}) copy-start(bf16[4,2,144,256]{3,2,1,0:T(8,128)(2,1)S(1)} %collective-permute-done.15.refs_4_) | copy-start | bytes 1769476
  62.3 9.8 %collective-permute-start.7 = (bf16[256,512]{1,0:T(8,128)(2,1)S(1)}, bf16[256,512]{1,0:T(8,128)(2,1)}, u32[]{:S(2)}, u32[]{:S(2)}) collective-permute-start(bf16[256,512]{1,0:T(8,128)(2,1)S(1)} %slice.120), channel_id=1, source_target_pairs={{0,7},{1,0},{2,1},{3,2},{4,3},{5,4},{6,5},{7,6},{8,15},{9,8},{10,9... | collective-permute-start | bytes 786440 | tf_op jit(solution)/shard_map/ppermute | solution.py:60
  65.7 0.8 copy-start.14
  65.7 1.0 copy-start.15
  72.1 1.9 copy-start.7
  83.4 1.6 collective-permute-start.19
  87.4 6.7 %collective-permute-start.20 = (bf16[4,128,128]{2,1,0:T(8,128)(2,1)}, bf16[4,128,128]{2,1,0:T(8,128)(2,1)S(1)}, u32[]{:S(2)}, u32[]{:S(2)}) collective-permute-start(bf16[4,128,128]{2,1,0:T(8,128)(2,1)} %join_chip.1.q), channel_id=1, source_target_pairs={{0,16},{8,24},{16,32},{24,40},{32,48},{40,56},{48,0},{56,8},{64,80... | collective-permute-start | bytes 393224 | tf_op jit(solution)/shard_map/ppermute | solution.py:48
  88.3 8.7 %collective-permute-start.21 = (bf16[4,128,128]{2,1,0:T(8,128)(2,1)}, bf16[4,128,128]{2,1,0:T(8,128)(2,1)S(1)}, u32[]{:S(2)}, u32[]{:S(2)}) collective-permute-start(bf16[4,128,128]{2,1,0:T(8,128)(2,1)} %join_chip.1.q), channel_id=1, source_target_pairs={{0,32},{8,40},{16,48},{24,56},{32,0},{40,8},{48,16},{56,24},{64,96... | collective-permute-start | bytes 393224 | tf_op jit(solution)/shard_map/ppermute | solution.py:48
  90.6 6.4 %collective-permute-start.22 = (bf16[4,128,128]{2,1,0:T(8,128)(2,1)}, bf16[4,128,128]{2,1,0:T(8,128)(2,1)S(1)}, u32[]{:S(2)}, u32[]{:S(2)}) collective-permute-start(bf16[4,128,128]{2,1,0:T(8,128)(2,1)} %join_chip.1.q), channel_id=1, source_target_pairs={{0,48},{8,56},{16,0},{24,8},{32,16},{40,24},{48,32},{56,40},{64,11... | collective-permute-start | bytes 393224 | tf_op jit(solution)/shard_map/ppermute | solution.py:48
  94.2 2.9 %copy-start.23 = (bf16[4,128,128]{2,1,0:T(8,128)(2,1)}, bf16[4,128,128]{2,1,0:T(8,128)(2,1)S(1)}, u32[]{:S(2)}) copy-start(bf16[4,128,128]{2,1,0:T(8,128)(2,1)S(1)} %collective-permute-done.20.g1) | copy-start | bytes 393220
  100.3 6.8 %collective-permute-start.23 = (bf16[4,128,128]{2,1,0:T(8,128)(2,1)}, bf16[4,128,128]{2,1,0:T(8,128)(2,1)S(1)}, u32[]{:S(2)}, u32[]{:S(2)}) collective-permute-start(bf16[4,128,128]{2,1,0:T(8,128)(2,1)} %get-tuple-element.64), channel_id=1, source_target_pairs={{0,64},{8,72},{16,80},{24,88},{32,96},{40,104},{48,112},{56,120},{... | collective-permute-start | bytes 393224 | tf_op jit(solution)/shard_map/ppermute | solution.py:48
  100.4 9.3 %collective-permute-start.24 = (bf16[4,128,128]{2,1,0:T(8,128)(2,1)}, bf16[4,128,128]{2,1,0:T(8,128)(2,1)S(1)}, u32[]{:S(2)}, u32[]{:S(2)}) collective-permute-start(bf16[4,128,128]{2,1,0:T(8,128)(2,1)} %get-tuple-element.64), channel_id=1, source_target_pairs={{0,128},{8,136},{16,144},{24,152},{32,160},{40,168},{48,176},{56,1... | collective-permute-start | bytes 393224 | tf_op jit(solution)/shard_map/ppermute | solution.py:48
  104.6 5.4 %collective-permute-start.25 = (bf16[4,128,128]{2,1,0:T(8,128)(2,1)}, bf16[4,128,128]{2,1,0:T(8,128)(2,1)S(1)}, u32[]{:S(2)}, u32[]{:S(2)}) collective-permute-start(bf16[4,128,128]{2,1,0:T(8,128)(2,1)} %get-tuple-element.64), channel_id=1, source_target_pairs={{0,192},{8,200},{16,208},{24,216},{32,224},{40,232},{48,240},{56,2... | collective-permute-start | bytes 393224 | tf_op jit(solution)/shard_map/ppermute | solution.py:48
  107.1 2.9 %copy-start.20 = (bf16[4,128,128]{2,1,0:T(8,128)(2,1)}, bf16[4,128,128]{2,1,0:T(8,128)(2,1)S(1)}, u32[]{:S(2)}) copy-start(bf16[4,128,128]{2,1,0:T(8,128)(2,1)S(1)} %collective-permute-done.23.g1) | copy-start | bytes 393220
  112.8 3.3 %collective-permute-start.26 = (bf16[4,128,128]{2,1,0:T(8,128)(2,1)}, bf16[4,128,128]{2,1,0:T(8,128)(2,1)S(1)}, u32[]{:S(2)}, u32[]{:S(2)}) collective-permute-start(bf16[4,128,128]{2,1,0:T(8,128)(2,1)} %get-tuple-element.70), channel_id=1, source_target_pairs={{0,8},{8,0},{16,24},{24,16},{32,40},{40,32},{48,56},{56,48},{64,72... | collective-permute-start | bytes 393224 | tf_op jit(solution)/shard_map/ppermute | solution.py:52
  122.6 13.3 %collective-permute-start.28 = (bf16[4,4,256,256]{3,2,1,0:T(8,128)(2,1)}, bf16[4,4,256,256]{3,2,1,0:T(8,128)(2,1)S(1)}, u32[]{:S(2)}, u32[]{:S(2)}) collective-permute-start(bf16[4,4,256,256]{3,2,1,0:T(8,128)(2,1)} %get-tuple-element.79), channel_id=1, source_target_pairs={{0,8},{8,0},{16,24},{24,16},{32,40},{40,32},{48,56},{56,48},{64,72... | collective-permute-start | bytes 6291464 | tf_op jit(solution)/shard_map/ppermute | solution.py:52
  129.9 6.0 %collective-permute-start.27 = (bf16[4,4,256,256]{3,2,1,0:T(8,128)(2,1)}, bf16[4,4,256,256]{3,2,1,0:T(8,128)(2,1)S(1)}, u32[]{:S(2)}, u32[]{:S(2)}) collective-permute-start(bf16[4,4,256,256]{3,2,1,0:T(8,128)(2,1)} %get-tuple-element.77), channel_id=1, source_target_pairs={{0,8},{8,0},{16,24},{24,16},{32,40},{40,32},{48,56},{56,48},{64,72... | collective-permute-start | bytes 6291464 | tf_op jit(solution)/shard_map/ppermute | solution.py:52
  130.2 7.1 %copy-start.8 = (bf16[4,4,256,256]{3,2,1,0:T(8,128)(2,1)S(1)}, bf16[4,4,256,256]{3,2,1,0:T(8,128)(2,1)}, u32[]{:S(2)}) copy-start(bf16[4,4,256,256]{3,2,1,0:T(8,128)(2,1)} %get-tuple-element.74) | copy-start | bytes 6291460
  135.9 1.4 copy-start.9
  141.2 9.9 %collective-permute-start.29 = (bf16[2,2,256,256]{3,2,0,1:T(8,128)(2,1)}, bf16[2,2,256,256]{3,2,0,1:T(8,128)(2,1)}, u32[]{:S(2)}, u32[]{:S(2)}) collective-permute-start(bf16[2,2,256,256]{3,2,0,1:T(8,128)(2,1)} %get-tuple-element.96), channel_id=1, source_target_pairs={{0,16},{8,72},{16,32},{24,88},{32,48},{40,104},{48,0},{56,120},{64... | collective-permute-start | bytes 1572872 | tf_op jit(solution)/shard_map/ppermute | solution.py:39
  141.2 11.1 %collective-permute-start.31 = (bf16[2,2,256,256]{3,2,0,1:T(8,128)(2,1)}, bf16[2,2,256,256]{3,2,0,1:T(8,128)(2,1)}, u32[]{:S(2)}, u32[]{:S(2)}) collective-permute-start(bf16[2,2,256,256]{3,2,0,1:T(8,128)(2,1)} %get-tuple-element.97), channel_id=1, source_target_pairs={{0,48},{8,200},{16,0},{24,216},{32,16},{40,232},{48,32},{56,248},{... | collective-permute-start | bytes 1572872 | tf_op jit(solution)/shard_map/ppermute | solution.py:39
  152.2 15.2 %collective-permute-start.30 = (bf16[4,2,256,256]{3,2,0,1:T(8,128)(2,1)S(1)}, bf16[4,2,256,256]{3,2,0,1:T(8,128)(2,1)S(1)}, u32[]{:S(2)}, u32[]{:S(2)}) collective-permute-start(bf16[4,2,256,256]{3,2,0,1:T(8,128)(2,1)S(1)} %add_convert_fusion.1), channel_id=1, source_target_pairs={{0,16},{8,72},{16,32},{24,88},{32,48},{40,104},{48,0},{56,120},{64... | collective-permute-start | bytes 3145736 | tf_op jit(solution)/shard_map/ppermute | solution.py:39
  153.5 14.5 %collective-permute-start.32 = (bf16[4,2,256,256]{3,2,0,1:T(8,128)(2,1)S(1)}, bf16[4,2,256,256]{3,2,0,1:T(8,128)(2,1)S(1)}, u32[]{:S(2)}, u32[]{:S(2)}) collective-permute-start(bf16[4,2,256,256]{3,2,0,1:T(8,128)(2,1)S(1)} %add_convert_fusion), channel_id=1, source_target_pairs={{0,48},{8,200},{16,0},{24,216},{32,16},{40,232},{48,32},{56,248},{... | collective-permute-start | bytes 3145736 | tf_op jit(solution)/shard_map/ppermute | solution.py:39
  169.2 16.2 %copy-start.16 = (bf16[128,512]{1,0:T(8,128)(2,1)S(1)}, bf16[128,512]{1,0:T(8,128)(2,1)}, u32[]{:S(2)}) copy-start(bf16[128,512]{1,0:T(8,128)(2,1)} %iw.1) | copy-start | bytes 393220
  169.2 16.2 %copy-start.17 = (bf16[128,512]{1,0:T(8,128)(2,1)S(1)}, bf16[128,512]{1,0:T(8,128)(2,1)}, u32[]{:S(2)}) copy-start(bf16[128,512]{1,0:T(8,128)(2,1)} %ow.1) | copy-start | bytes 393220
  169.2 16.2 %copy-start.26 = (f32[512]{0:T(512)S(1)}, f32[512]{0:T(512)}, u32[]{:S(2)}) copy-start(f32[512]{0:T(512)} %param.12) | copy-start | bytes 6148
  169.2 7.1 %collective-permute-start.33 = (bf16[2,256,256]{2,1,0:T(8,128)(2,1)}, bf16[2,256,256]{2,1,0:T(8,128)(2,1)S(1)}, u32[]{:S(2)}, u32[]{:S(2)}) collective-permute-start(bf16[2,256,256]{2,1,0:T(8,128)(2,1)} %get-tuple-element.93), channel_id=1, source_target_pairs={{0,64},{8,24},{16,80},{24,40},{32,96},{40,56},{48,112},{56,8},{64,... | collective-permute-start | bytes 786440 | tf_op jit(solution)/shard_map/ppermute | solution.py:39
  169.2 9.4 %collective-permute-start.34 = (bf16[2,256,256]{2,1,0:T(8,128)(2,1)S(1)}, bf16[2,256,256]{2,1,0:T(8,128)(2,1)S(1)}, u32[]{:S(2)}, u32[]{:S(2)}) collective-permute-start(bf16[2,256,256]{2,1,0:T(8,128)(2,1)S(1)} %get-tuple-element.95), channel_id=1, source_target_pairs={{0,128},{8,40},{16,144},{24,56},{32,160},{40,8},{48,176},{56,24},{... | collective-permute-start | bytes 786440 | tf_op jit(solution)/shard_map/ppermute | solution.py:39
  171.8 7.7 %collective-permute-start.35 = (bf16[2,256,256]{2,1,0:T(8,128)(2,1)S(1)}, bf16[2,256,256]{2,1,0:T(8,128)(2,1)}, u32[]{:S(2)}, u32[]{:S(2)}) collective-permute-start(bf16[2,256,256]{2,1,0:T(8,128)(2,1)S(1)} %get-tuple-element.94), channel_id=1, source_target_pairs={{0,192},{8,56},{16,208},{24,8},{32,224},{40,24},{48,240},{56,40},{... | collective-permute-start | bytes 786440 | tf_op jit(solution)/shard_map/ppermute | solution.py:39
  180.6 4.8 %collective-permute-start.36 = (f32[2,128,256]{2,1,0:T(8,128)S(1)}, f32[2,128,256]{2,1,0:T(8,128)S(1)}, u32[]{:S(2)}, u32[]{:S(2)}) collective-permute-start(f32[2,128,256]{2,1,0:T(8,128)S(1)} %slice_select_fusion), channel_id=1, source_target_pairs={{0,8},{8,0},{16,24},{24,16},{32,40},{40,32},{48,56},{56,48},{64,72... | collective-permute-start | bytes 786440 | tf_op jit(solution)/shard_map/ppermute | solution.py:52
  187.3 20.8 %all-to-all-start = ((f32[32,8,512]{2,1,0:T(8,128)}), f32[32,8,512]{2,1,0:T(8,128)S(1)}, u32[]{:S(2)}, u32[]{:S(2)}) async-start(f32[32,8,512]{2,1,0:T(8,128)} %broadcast_in_dim.14), calls=%async_computation.1 | async-start | bytes 1048576 | tf_op jit(solution)/shard_map/all_to_all | solution.py:525
  194.9 2.8 %collective-permute-start.37 = (f32[1,128]{1,0:T(1,128)S(1)}, f32[1,128]{1,0:T(1,128)S(1)}, u32[]{:S(2)}, u32[]{:S(2)}) collective-permute-start(f32[1,128]{1,0:T(1,128)S(1)} %bitcast.80), channel_id=1, source_target_pairs={{0,1},{1,0},{2,3},{3,2},{4,5},{5,4},{6,7},{7,6},{8,9},{9,8},{10,11... | collective-permute-start | bytes 1544 | tf_op jit(solution)/shard_map/ppermute | solution.py:64
  197.7 3.6 %collective-permute-start.38 = (f32[1,128]{1,0:T(1,128)S(1)}, f32[1,128]{1,0:T(1,128)S(1)}, u32[]{:S(2)}, u32[]{:S(2)}) collective-permute-start(f32[1,128]{1,0:T(1,128)S(1)} %bitcast_add_fusion), channel_id=1, source_target_pairs={{0,2},{1,3},{2,0},{3,1},{4,6},{5,7},{6,4},{7,5},{8,10},{9,11},{10,... | collective-permute-start | bytes 1544 | tf_op jit(solution)/shard_map/ppermute | solution.py:64
  201.2 6.3 %collective-permute-start.39 = (f32[1,128]{1,0:T(1,128)S(1)}, f32[1,128]{1,0:T(1,128)S(1)}, u32[]{:S(2)}, u32[]{:S(2)}) collective-permute-start(f32[1,128]{1,0:T(1,128)S(1)} %add.187), channel_id=1, source_target_pairs={{0,4},{1,5},{2,6},{3,7},{4,0},{5,1},{6,2},{7,3},{8,12},{9,13},{10,... | collective-permute-start | bytes 1544 | tf_op jit(solution)/shard_map/ppermute | solution.py:64
  (6 other events, 3.9 us)
Sparse Core Ops, SparseCore 0:
  11.1 62.8 all-gather.1
  144.0 36.4 reduce-scatter.1
